TPU v7x, 32 devices: a whole 2x2x4 slice. The times are simulated.
32 devices in a mesh: seq: 2 (over x), fsdp: 4 (over z), dp: 4 (over y, core).
Axes of the slice: x: 2, y: 2, z: 4, core: 2. Of those that a mesh axis runs over, the one named last changes fastest.
Arguments:
- image_in: bfloat16 [32, 1024, 1536], P(('fsdp', 'dp'), 'seq'), may hold values from -6 to 6
- text_in: bfloat16 [32, 154, 1536], P(('fsdp', 'dp'), 'seq'), may hold values from -6 to 6
- modulation: float32 [32, 2, 6, 1536], P(('fsdp', 'dp')), may hold values from -3 to 3
- text_len: int32 [32], P(('fsdp', 'dp')), may hold values from 1 to 154, as said below
- w_qkv: bfloat16 [2, 1536, 4608], P(None, 'fsdp'), may hold values from -0.15625 to 0.15625
- b_qkv: bfloat16 [2, 4608], P(None, 'fsdp'), may hold values from -0.59765625 to 0.59765625
- w_out: bfloat16 [2, 1536, 1536], P(None, 'fsdp'), may hold values from -0.875 to 0.875
- b_out: bfloat16 [2, 1536], P(None, 'fsdp'), may hold values from -3 to 3
- w_up: bfloat16 [2, 1536, 6144], P(None, 'fsdp'), may hold values from -0.15625 to 0.15625
- b_up: bfloat16 [2, 6144], P(None, 'fsdp'), may hold values from -3 to 3
- w_down: bfloat16 [2, 6144, 1536], P(None, 'fsdp'), may hold values from -0.078125 to 0.078125
- b_down: bfloat16 [2, 1536], P(None, 'fsdp'), may hold values from -3 to 3
- d_image: bfloat16 [32, 1024, 1536], P(('fsdp', 'dp'), 'seq'), may hold values from -6 to 6
- d_text: bfloat16 [32, 154, 1536], P(('fsdp', 'dp'), 'seq'), may hold values from -6 to 6
Outputs:
- out_image: bfloat16 [32, 1024, 1536], P(('fsdp', 'dp'), 'seq')
- out_text: bfloat16 [32, 154, 1536], P(('fsdp', 'dp'), 'seq')
- grad_image: float32 [32, 1024, 1536], P(('fsdp', 'dp'), 'seq')
- grad_text: float32 [32, 154, 1536], P(('fsdp', 'dp'), 'seq')
- grad_modulation: float32 [32, 2, 6, 1536], P(('fsdp', 'dp'))
- grad_w_qkv: float32 [2, 1536, 4608], P(None, ('seq', 'fsdp', 'dp'))
- grad_b_qkv: float32 [2, 4608], P(None, ('seq', 'fsdp', 'dp'))
- grad_w_out: float32 [2, 1536, 1536], P(None, ('seq', 'fsdp', 'dp'))
- grad_b_out: float32 [2, 1536], P(None, ('seq', 'fsdp', 'dp'))
- grad_w_up: float32 [2, 1536, 6144], P(None, ('seq', 'fsdp', 'dp'))
- grad_b_up: float32 [2, 6144], P(None, ('seq', 'fsdp', 'dp'))
- grad_w_down: float32 [2, 6144, 1536], P(None, ('seq', 'fsdp', 'dp'))
- grad_b_down: float32 [2, 1536], P(None, ('seq', 'fsdp', 'dp'))
Inputs may be any that keep to these rules, and one draw needn't show every extreme that they name: Each sequence has text_len real text tokens among its 154 text slots.
All inputs are finite; a program needn't handle non-finite values.
Results may differ from a plain program's by a relative error of at most 0.0085.
Values may be sent and summed in bfloat16 or wider, within the bound.
A program may use at most 768 MiB of HBM per device.

v0:
```python
import math

import jax
import jax.numpy as jnp
from jax import lax
from jax.sharding import PartitionSpec as P

HEADS = 24
HEAD_DIM = 64
MICRO = 2


EPSILON = 1e-06
MASKED = -1000000000.0


def normalize(values):
    row_mean = jnp.mean(values, axis=-1, keepdims=True)
    centred = values - row_mean
    variance = jnp.mean(centred * centred, axis=-1, keepdims=True)
    inverse = lax.rsqrt(variance + EPSILON)
    return (centred * inverse, inverse)


def normalize_back(normed, inverse, upstream):
    mean_one = jnp.mean(upstream, axis=-1, keepdims=True)
    mean_two = jnp.mean(upstream * normed, axis=-1, keepdims=True)
    return inverse * (upstream - mean_one - normed * mean_two)


def linear(values, weight, offset):
    return jnp.einsum(
        "mnd,dc->mnc", values, weight, preferred_element_type=jnp.float32
    ) + offset.astype(jnp.float32)


def linear_back(upstream, weight):
    return jnp.einsum("mnc,dc->mnd", upstream, weight, preferred_element_type=jnp.float32)


def gelu_tanh(values):
    return jax.nn.gelu(values, approximate=True)


def stream_rows(values, stream, image_len):
    if stream == 0:
        return values[:, :image_len]
    return values[:, image_len:]


def reduce_grads(weight_terms, bias_terms):
    return (
        lax.psum_scatter(weight_terms[0], ("seq", "fsdp", "dp"), scatter_dimension=1, tiled=True),
        lax.psum_scatter(weight_terms[1], ("seq", "fsdp", "dp"), scatter_dimension=1, tiled=True),
        lax.psum_scatter(weight_terms[2], ("seq", "fsdp", "dp"), scatter_dimension=1, tiled=True),
        lax.psum_scatter(weight_terms[3], ("seq", "fsdp", "dp"), scatter_dimension=1, tiled=True),
        lax.psum_scatter(bias_terms[0], ("seq", "fsdp", "dp"), scatter_dimension=1, tiled=True),
        lax.psum_scatter(bias_terms[1], ("seq", "fsdp", "dp"), scatter_dimension=1, tiled=True),
        lax.psum_scatter(bias_terms[2], ("seq", "fsdp", "dp"), scatter_dimension=1, tiled=True),
        lax.psum_scatter(bias_terms[3], ("seq", "fsdp", "dp"), scatter_dimension=1, tiled=True),
    )


def attend_sequence(queries, key_vals, key_valid, head_dim, head_group):
    length = queries.shape[0]
    key_len = key_vals.shape[0]
    model_width = queries.shape[1]
    group_cols = head_group * head_dim
    factor = head_dim ** (-0.5)

    def per_group(group_index):
        col_start = group_index * group_cols
        query_part = lax.dynamic_slice_in_dim(queries, col_start, group_cols, 1).reshape(
            length, head_group, head_dim
        )
        key_part = lax.dynamic_slice_in_dim(key_vals, col_start, group_cols, 1).reshape(
            key_len, head_group, head_dim
        )
        value_part = lax.dynamic_slice_in_dim(
            key_vals, model_width + col_start, group_cols, 1
        ).reshape(key_len, head_group, head_dim)
        scores = (
            jnp.einsum("qhd,khd->hqk", query_part, key_part, preferred_element_type=jnp.float32)
            * factor
        )
        scores = jnp.where(key_valid[None, None, :], scores, MASKED)
        row_max = jnp.max(scores, axis=-1, keepdims=True)
        exponent = jnp.exp(scores - row_max)
        totals = jnp.sum(exponent, axis=-1, keepdims=True)
        attn_probs = (exponent / totals).astype(jnp.bfloat16)
        output = jnp.einsum(
            "hqk,khd->qhd", attn_probs, value_part, preferred_element_type=jnp.float32
        )
        return (
            output.reshape(length, group_cols).astype(jnp.bfloat16),
            (row_max + jnp.log(totals))[..., 0],
        )

    outputs, log_sums = lax.map(per_group, jnp.arange(model_width // group_cols))
    return (outputs.transpose(1, 0, 2).reshape(length, model_width), log_sums)


def attend_back(queries, key_vals, key_valid, log_sums, d_output, head_dim, head_group):
    length = queries.shape[0]
    key_len = key_vals.shape[0]
    model_width = queries.shape[1]
    group_cols = head_group * head_dim
    factor = head_dim ** (-0.5)

    def per_group(tensors):
        group_index, log_sum = tensors
        col_start = group_index * group_cols
        query_part = lax.dynamic_slice_in_dim(queries, col_start, group_cols, 1).reshape(
            length, head_group, head_dim
        )
        key_part = lax.dynamic_slice_in_dim(key_vals, col_start, group_cols, 1).reshape(
            key_len, head_group, head_dim
        )
        value_part = lax.dynamic_slice_in_dim(
            key_vals, model_width + col_start, group_cols, 1
        ).reshape(key_len, head_group, head_dim)
        grad_part = lax.dynamic_slice_in_dim(d_output, col_start, group_cols, 1).reshape(
            length, head_group, head_dim
        )
        scores = (
            jnp.einsum("qhd,khd->hqk", query_part, key_part, preferred_element_type=jnp.float32)
            * factor
        )
        scores = jnp.where(key_valid[None, None, :], scores, MASKED)
        attn_probs = jnp.exp(scores - log_sum[..., None])
        d_probs = jnp.einsum(
            "qhd,khd->hqk", grad_part, value_part, preferred_element_type=jnp.float32
        )
        inner_sum = jnp.sum(attn_probs * d_probs, axis=-1, keepdims=True)
        d_scores = (attn_probs * (d_probs - inner_sum)).astype(jnp.bfloat16)
        d_query = (
            jnp.einsum("hqk,khd->qhd", d_scores, key_part, preferred_element_type=jnp.float32)
            * factor
        )
        d_key = (
            jnp.einsum("hqk,qhd->khd", d_scores, query_part, preferred_element_type=jnp.float32)
            * factor
        )
        d_value = jnp.einsum(
            "hqk,qhd->khd",
            attn_probs.astype(jnp.bfloat16),
            grad_part,
            preferred_element_type=jnp.float32,
        )
        return (
            d_query.reshape(length, group_cols),
            d_key.reshape(key_len, group_cols),
            d_value.reshape(key_len, group_cols),
        )

    d_queries, d_keys, d_values = lax.map(
        per_group, (jnp.arange(model_width // group_cols), log_sums)
    )
    d_queries = d_queries.transpose(1, 0, 2).reshape(length, model_width)
    d_keys = d_keys.transpose(1, 0, 2).reshape(key_len, model_width)
    d_values = d_values.transpose(1, 0, 2).reshape(key_len, model_width)
    return (d_queries, jnp.concatenate([d_keys, d_values], axis=-1))


def local(
    image_in,
    text_in,
    modulation,
    text_len,
    w_qkv,
    b_qkv,
    w_out,
    b_out,
    w_up,
    b_up,
    w_down,
    b_down,
    d_image,
    d_text,
):
    seq_local = image_in.shape[0]
    per_micro = seq_local // MICRO
    image_len = image_in.shape[1]
    text_local = text_in.shape[1]
    local_len = image_len + text_local
    model_width = image_in.shape[2]
    head_group = math.gcd(HEADS, 8)
    positions = jnp.arange(local_len * lax.axis_size("seq"), dtype=jnp.int32)
    within = positions % local_len
    text_slot = positions // local_len * text_local + within - image_len
    forward_set = (
        lax.all_gather(w_qkv, "fsdp", axis=1, tiled=True),
        lax.all_gather(b_qkv, "fsdp", axis=1, tiled=True),
        lax.all_gather(w_out, "fsdp", axis=1, tiled=True),
        lax.all_gather(b_out, "fsdp", axis=1, tiled=True),
        lax.all_gather(w_up, "fsdp", axis=1, tiled=True),
        lax.all_gather(b_up, "fsdp", axis=1, tiled=True),
        lax.all_gather(w_down, "fsdp", axis=1, tiled=True),
        lax.all_gather(b_down, "fsdp", axis=1, tiled=True),
    )
    backward_set = (
        lax.all_gather(w_qkv, "fsdp", axis=1, tiled=True),
        lax.all_gather(w_out, "fsdp", axis=1, tiled=True),
        lax.all_gather(w_up, "fsdp", axis=1, tiled=True),
        lax.all_gather(w_down, "fsdp", axis=1, tiled=True),
    )
    weight_qkv, bias_qkv, weight_out, bias_out, weight_up, bias_up, weight_down, bias_down = (
        forward_set
    )
    back_qkv, back_out, back_up, back_down = backward_set
    results = [[], []]
    input_grads = [[], []]
    modulation_parts = []
    grad_pairs = [[[] for layer_slot in range(4)] for stream in range(2)]
    for micro_index in range(MICRO):
        row_start = micro_index * per_micro
        row_stop = row_start + per_micro
        stream_inputs = (
            image_in[row_start:row_stop].astype(jnp.float32),
            text_in[row_start:row_stop].astype(jnp.float32),
        )
        cotangents = (
            d_image[row_start:row_stop].astype(jnp.float32),
            d_text[row_start:row_stop].astype(jnp.float32),
        )
        gains_micro = modulation[row_start:row_stop]
        fronts = []
        for stream in range(2):
            conditioning = gains_micro[:, stream]
            normed, inverse = normalize(stream_inputs[stream])
            modded = (
                normed * (1.0 + conditioning[:, 1, None, :]) + conditioning[:, 0, None, :]
            ).astype(jnp.bfloat16)
            projected = linear(modded, weight_qkv[stream], bias_qkv[stream]).astype(jnp.bfloat16)
            fronts.append((normed, inverse, modded, projected))
        joint_rows = jnp.concatenate([fronts[0][3], fronts[1][3]], axis=1)
        queries = joint_rows[..., :model_width]
        key_vals = lax.all_gather(joint_rows[..., model_width:], "seq", axis=1, tiled=True)
        text_counts = text_len[row_start:row_stop]
        key_valid = (within[None, :] < image_len) | (text_slot[None, :] < text_counts[:, None])
        attended, log_sums = lax.map(
            lambda tensors: attend_sequence(
                tensors[0], tensors[1], tensors[2], HEAD_DIM, head_group
            ),
            (queries, key_vals, key_valid),
        )
        middles = []
        for stream in range(2):
            conditioning = gains_micro[:, stream]
            attn_rows = stream_rows(attended, stream, image_len)
            branch = linear(attn_rows, weight_out[stream], bias_out[stream])
            middle = stream_inputs[stream] + conditioning[:, 2, None, :] * branch
            normed_two, inverse_two = normalize(middle)
            modded_two = (
                normed_two * (1.0 + conditioning[:, 4, None, :]) + conditioning[:, 3, None, :]
            ).astype(jnp.bfloat16)
            middles.append((attn_rows, branch, middle, normed_two, inverse_two, modded_two))
        hiddens = []
        for stream in range(2):
            hidden = linear(middles[stream][5], weight_up[stream], bias_up[stream])
            hiddens.append((hidden, gelu_tanh(hidden).astype(jnp.bfloat16)))
        kept_rest = []
        for stream in range(2):
            conditioning = gains_micro[:, stream]
            attn_rows, branch, middle, normed_two, inverse_two, modded_two = middles[stream]
            hidden, active = hiddens[stream]
            mlp_out = linear(active, weight_down[stream], bias_down[stream])
            results[stream].append(
                (middle + conditioning[:, 5, None, :] * mlp_out).astype(jnp.bfloat16)
            )
            kept_rest.append(
                (attn_rows, branch, normed_two, inverse_two, modded_two, hidden, active, mlp_out)
            )
        partial_state = []
        for stream in range(2):
            conditioning = gains_micro[:, stream]
            hidden = kept_rest[stream][5]
            mlp_out = kept_rest[stream][7]
            upstream = cotangents[stream]
            d_gate_two = jnp.sum(upstream * mlp_out, axis=1)
            d_mlp = (conditioning[:, 5, None, :] * upstream).astype(jnp.bfloat16)
            d_active = linear_back(d_mlp, back_down[stream])
            d_hidden = jax.vjp(gelu_tanh, hidden)[1](d_active)[0].astype(jnp.bfloat16)
            partial_state.append((d_gate_two, d_mlp, d_hidden))
        stream_state = []
        d_branches = []
        for stream in range(2):
            conditioning = gains_micro[:, stream]
            attn_rows, branch, normed_two, inverse_two, modded_two, hidden, active, mlp_out = (
                kept_rest[stream]
            )
            d_gate_two, d_mlp, d_hidden = partial_state[stream]
            upstream = cotangents[stream]
            d_modded_two = linear_back(d_hidden, back_up[stream])
            d_shift_two = jnp.sum(d_modded_two, axis=1)
            d_scale_two = jnp.sum(d_modded_two * normed_two, axis=1)
            d_middle = upstream + normalize_back(
                normed_two, inverse_two, d_modded_two * (1.0 + conditioning[:, 4, None, :])
            )
            d_gate_one = jnp.sum(d_middle * branch, axis=1)
            d_branch = (conditioning[:, 2, None, :] * d_middle).astype(jnp.bfloat16)
            d_branches.append(d_branch)
            grad_pairs[stream][1].append((attn_rows, d_branch))
            grad_pairs[stream][2].append((modded_two, d_hidden))
            grad_pairs[stream][3].append((active, d_mlp))
            stream_state.append((d_middle, d_gate_one, d_shift_two, d_scale_two, d_gate_two))
        d_attended = [linear_back(d_branches[stream], back_out[stream]) for stream in range(2)]
        d_joint = jnp.concatenate(d_attended, axis=1).astype(jnp.bfloat16)
        d_queries, d_key_vals = lax.map(
            lambda tensors: attend_back(
                tensors[0], tensors[1], tensors[2], tensors[3], tensors[4], HEAD_DIM, head_group
            ),
            (queries, key_vals, key_valid, log_sums, d_joint),
        )
        d_local = lax.psum_scatter(
            d_key_vals.astype(jnp.bfloat16), "seq", scatter_dimension=1, tiled=True
        ).astype(jnp.float32)
        d_fronts = jnp.concatenate([d_queries, d_local], axis=-1).astype(jnp.bfloat16)
        gain_grads = []
        for stream in range(2):
            conditioning = gains_micro[:, stream]
            normed, inverse, modded, projected = fronts[stream]
            d_middle, d_gate_one, d_shift_two, d_scale_two, d_gate_two = stream_state[stream]
            grad_part = stream_rows(d_fronts, stream, image_len)
            d_modded = linear_back(grad_part, back_qkv[stream])
            d_shift_one = jnp.sum(d_modded, axis=1)
            d_scale_one = jnp.sum(d_modded * normed, axis=1)
            input_grads[stream].append(
                d_middle
                + normalize_back(normed, inverse, d_modded * (1.0 + conditioning[:, 1, None, :]))
            )
            grad_pairs[stream][0].append((modded, grad_part))
            gain_grads.append(
                jnp.stack(
                    [d_shift_one, d_scale_one, d_gate_one, d_shift_two, d_scale_two, d_gate_two],
                    axis=1,
                )
            )
        modulation_parts.append(jnp.stack(gain_grads, axis=1))
    grad_modulation = lax.psum(
        jnp.concatenate(modulation_parts, axis=0).astype(jnp.bfloat16), "seq"
    ).astype(jnp.float32)
    weight_terms = []
    bias_terms = []
    for layer_slot in range(4):
        weight_streams = []
        bias_streams = []
        for stream in range(2):
            left_side = jnp.concatenate(
                [pair_item[0] for pair_item in grad_pairs[stream][layer_slot]], axis=0
            )
            right_side = jnp.concatenate(
                [pair_item[1] for pair_item in grad_pairs[stream][layer_slot]], axis=0
            )
            weight_streams.append(
                jnp.einsum("mnd,mnc->dc", left_side, right_side, preferred_element_type=jnp.float32)
            )
            bias_streams.append(jnp.sum(right_side, axis=(0, 1), dtype=jnp.float32))
        weight_terms.append(jnp.stack(weight_streams))
        bias_terms.append(jnp.stack(bias_streams))
    reduced = reduce_grads(weight_terms, bias_terms)
    out_image = jnp.concatenate(results[0], axis=0)
    out_text = jnp.concatenate(results[1], axis=0)
    grad_image = jnp.concatenate(input_grads[0], axis=0)
    grad_text = jnp.concatenate(input_grads[1], axis=0)
    return (
        out_image,
        out_text,
        grad_image,
        grad_text,
        grad_modulation,
        reduced[0],
        reduced[4],
        reduced[1],
        reduced[5],
        reduced[2],
        reduced[6],
        reduced[3],
        reduced[7],
    )


def solution(mesh):
    in_specs = (
        P(("fsdp", "dp"), "seq", None),
        P(("fsdp", "dp"), "seq", None),
        P(("fsdp", "dp"), None, None, None),
        P(("fsdp", "dp")),
        P(None, "fsdp", None),
        P(None, "fsdp"),
        P(None, "fsdp", None),
        P(None, "fsdp"),
        P(None, "fsdp", None),
        P(None, "fsdp"),
        P(None, "fsdp", None),
        P(None, "fsdp"),
        P(("fsdp", "dp"), "seq", None),
        P(("fsdp", "dp"), "seq", None),
    )
    out_specs = (
        P(("fsdp", "dp"), "seq", None),
        P(("fsdp", "dp"), "seq", None),
        P(("fsdp", "dp"), "seq", None),
        P(("fsdp", "dp"), "seq", None),
        P(("fsdp", "dp"), None, None, None),
        P(None, ("seq", "fsdp", "dp"), None),
        P(None, ("seq", "fsdp", "dp")),
        P(None, ("seq", "fsdp", "dp"), None),
        P(None, ("seq", "fsdp", "dp")),
        P(None, ("seq", "fsdp", "dp"), None),
        P(None, ("seq", "fsdp", "dp")),
        P(None, ("seq", "fsdp", "dp"), None),
        P(None, ("seq", "fsdp", "dp")),
    )
    return jax.shard_map(local, mesh=mesh, in_specs=in_specs, out_specs=out_specs, check_vma=False)
```

profile of v0, /device:TPU:9, one launch (start us, length us, event | category | flops | bytes accessed | tf_op | source)
XLA Modules:
  0.0 5900.2 jit_solution(17730630045603115181)
XLA Ops:
  27.2 456.4 %all-gather.7.cloned.1.call-done = bf16[2,1536,4608]{2,1,0:T(8,128)(2,1)} async-done(((bf16[2,384,4608]{2,1,0:T(8,128)(2,1)}), bf16[2,1536,4608]{2,1,0:T(8,128)(2,1)}) %all-gather.7.cloned.1.call-update) | async-done | bytes 28311568 | tf_op jit(solution)/shard_map/all_gather | solution.py:192
  504.9 31.5 copy.118
  585.7 125.3 %all-gather.9.cloned.1.call-done = bf16[1,1178,3072]{2,0,1:T(2,128)(2,1)} async-done(((bf16[1,589,3072]{2,0,1:T(2,128)(2,1)}), bf16[1,1178,3072]{2,0,1:T(2,128)(2,1)}) %all-gather.9.cloned.1.call-update) | async-done | bytes 7237648 | tf_op jit(solution)/shard_map/all_gather | solution.py:238
  710.9 31.1 copy.162
  743.4 113.7 %while.102 = (s32[]{:T(128)}, bf16[3,589,512]{1,2,0:T(8,128)(2,1)}, f32[3,8,589]{2,1,0:T(8,128)S(1)}, s32[3]{0:T(128)S(1)}, bf16[1178,3072]{0,1:T(8,128)(2,1)}, ...) while((s32[]{:T(128)}, bf16[3,589,512]{1,2,0:T(8,128)(2,1)}, ...), condition=%wide.region_7.8_spmd.clone, body=%wide.region_4.7_spmd.clone.sunk | while | flops 1487915264 | bytes 171315088 | solution.py:99
  891.0 617.6 %all-gather.13.cloned.1.call-done = bf16[2,1536,6144]{2,1,0:T(8,128)(2,1)} async-done(((bf16[2,384,6144]{2,1,0:T(8,128)(2,1)}), bf16[2,1536,6144]{2,1,0:T(8,128)(2,1)}) %all-gather.13.cloned.1.call-update) | async-done | bytes 37748752 | tf_op jit(solution)/shard_map/all_gather | solution.py:196
  1527.3 613.5 %all-gather.15.cloned.1.call-done = bf16[2,6144,1536]{2,1,0:T(8,128)(2,1)} async-done(((bf16[2,1536,1536]{2,1,0:T(8,128)(2,1)}), bf16[2,6144,1536]{2,1,0:T(8,128)(2,1)}) %all-gather.15.cloned.1.call-update) | async-done | bytes 37748752 | tf_op jit(solution)/shard_map/all_gather | solution.py:198
  2253.2 227.4 %while.104 = (s32[]{:T(128)}, bf16[3,589,512]{1,2,0:T(8,128)(2,1)}, bf16[3,1178,512]{1,2,0:T(8,128)(2,1)}, bf16[3,1178,512]{1,2,0:T(8,128)(2,1)}, s32[3]{0:T(128...) while((s32[]{:T(128)}, bf16[3,589,512]{1,2,0:T(8,128)(2,1)}, ...), condition=%wide.region_30.31_spmd.clone, body=%wide.region_28.30_spmd.clone.sunk | while | flops 3604253184 | bytes 204930000 | solution.py:156
  2498.2 87.1 %fusion.8 = bf16[592,3072]{1,0:T(8,128)(2,1)} fusion(bf16[1,1178,3072]{2,1,0:T(8,128)(2,1)} %copy.131), kind=kCustom, calls=%all-reduce-scatter | all-reduce-scatter fusion | flops 3637249 | bytes 10875392
  2652.4 31.5 copy.124
  2720.5 138.4 %all-gather.17.cloned.1.call-done = bf16[1,1178,3072]{2,0,1:T(2,128)(2,1)} async-done(((bf16[1,589,3072]{2,0,1:T(2,128)(2,1)}), bf16[1,1178,3072]{2,0,1:T(2,128)(2,1)}) %all-gather.17.cloned.1.call-update) | async-done | bytes 7237648 | tf_op jit(solution)/shard_map/all_gather | solution.py:238
  2858.9 30.8 copy.163
  2891.1 113.7 %while.103 = (s32[]{:T(128)}, bf16[3,589,512]{1,2,0:T(8,128)(2,1)}, f32[3,8,589]{2,1,0:T(8,128)S(1)}, s32[3]{0:T(128)S(1)}, bf16[1178,3072]{0,1:T(8,128)(2,1)}, ...) while((s32[]{:T(128)}, bf16[3,589,512]{1,2,0:T(8,128)(2,1)}, ...), condition=%wide.region_17.18_spmd.clone, body=%wide.region_14.17_spmd.clone.sunk | while | flops 1487915264 | bytes 171315088 | solution.py:99
  3201.6 227.2 %while.105 = (s32[]{:T(128)}, bf16[3,589,512]{1,2,0:T(8,128)(2,1)}, bf16[3,1178,512]{1,2,0:T(8,128)(2,1)}, bf16[3,1178,512]{1,2,0:T(8,128)(2,1)}, s32[3]{0:T(128...) while((s32[]{:T(128)}, bf16[3,589,512]{1,2,0:T(8,128)(2,1)}, ...), condition=%wide.region_40.41_spmd.clone, body=%wide.region_38.40_spmd.clone.sunk | while | flops 3604253184 | bytes 204930000 | solution.py:156
  3446.3 86.3 %fusion.9 = bf16[592,3072]{1,0:T(8,128)(2,1)} fusion(bf16[1,1178,3072]{2,1,0:T(8,128)(2,1)} %copy.137), kind=kCustom, calls=%all-reduce-scatter.1 | all-reduce-scatter fusion | flops 3637249 | bytes 10875392
  3668.2 38.1 pad_maximum_fusion.2
  3724.3 27.1 convolution_bitcast_fusion.2
  3751.4 50.0 pad_maximum_fusion
  3835.4 27.6 convolution_bitcast_fusion.3
  3863.0 53.2 pad_maximum_fusion.1
  3941.7 146.3 %reduce-scatter.25.cloned.1.call-done = f32[2,48,1536]{2,1,0:T(8,128)} async-done(((f32[2,1536,1536]{2,1,0:T(8,128)}), f32[2,48,1536]{2,1,0:T(8,128)}) %reduce-scatter.25.cloned.1.call-update) | async-done | bytes 589840 | tf_op jit(solution)/shard_map/reduce_scatter | solution.py:54
  4088.0 478.9 %reduce-scatter.23.cloned.1.call-done = f32[2,48,4608]{2,1,0:T(8,128)} async-done(((f32[2,1536,4608]{2,1,0:T(8,128)}), f32[2,48,4608]{2,1,0:T(8,128)}) %reduce-scatter.23.cloned.1.call-update) | async-done | bytes 1769488 | tf_op jit(solution)/shard_map/reduce_scatter | solution.py:53
  4566.9 662.8 %reduce-scatter.27.cloned.1.call-done = f32[2,48,6144]{2,1,0:T(8,128)} async-done(((f32[2,1536,6144]{2,1,0:T(8,128)}), f32[2,48,6144]{2,1,0:T(8,128)}) %reduce-scatter.27.cloned.1.call-update) | async-done | bytes 2359312 | tf_op jit(solution)/shard_map/reduce_scatter | solution.py:55
  5229.7 663.7 %reduce-scatter.29.cloned.1.call-done = f32[2,192,1536]{2,1,0:T(8,128)} async-done(((f32[2,6144,1536]{2,1,0:T(8,128)}), f32[2,192,1536]{2,1,0:T(8,128)}) %reduce-scatter.29.cloned.1.call-update) | async-done | bytes 2359312 | tf_op jit(solution)/shard_map/reduce_scatter | solution.py:56
  (910 shorter events, 1474.8 us)
Async XLA Ops:
  7.2 476.4 %all-gather.7.cloned.1.call-start = ((), (), s32[]{:S(2)}) async-start(), calls=%async_computation.8 | async-start | bytes 35389440 | tf_op jit(solution)/shard_map/all_gather | solution.py:192
  7.9 703.0 %all-gather.9.cloned.1.call-start = ((), (), s32[]{:S(2)}) async-start(), calls=%async_computation.9 | async-start | bytes 21712896 | tf_op jit(solution)/shard_map/all_gather | solution.py:238
  19.4 560.4 %copy-start.125 = (f32[1536]{0:T(1024)}, f32[1536]{0:T(1024)S(1)}, u32[]{:S(2)}) copy-start(f32[1536]{0:T(1024)S(1)} %get-tuple-element.858) | copy-start | bytes 18436
  20.1 557.9 %copy-start.135 = (f32[1536]{0:T(1024)}, f32[1536]{0:T(1024)S(1)}, u32[]{:S(2)}) copy-start(f32[1536]{0:T(1024)S(1)} %get-tuple-element.846) | copy-start | bytes 18436
  20.2 474.5 %copy-start.153 = (f32[4608]{0:T(1024)}, f32[4608]{0:T(1024)S(1)}, u32[]{:S(2)}) copy-start(f32[4608]{0:T(1024)S(1)} %get-tuple-element.870) | copy-start | bytes 55300
  25.1 469.7 %copy-start.87 = (bf16[1,77,1536]{2,1,0:T(8,128)(2,1)}, bf16[1,77,1536]{2,1,0:T(8,128)(2,1)S(1)}, u32[]{:S(2)}) copy-start(bf16[1,77,1536]{2,1,0:T(8,128)(2,1)S(1)} %fusion.249) | copy-start | bytes 709636
  536.5 340.0 %all-gather.11.cloned.1.call-start = ((), (), s32[]{:S(2)}) async-start(), calls=%async_computation.10 | async-start | bytes 11796480 | tf_op jit(solution)/shard_map/all_gather | solution.py:194
  537.2 971.5 %all-gather.13.cloned.1.call-start = ((), (), s32[]{:S(2)}) async-start(), calls=%async_computation.11 | async-start | bytes 47185920 | tf_op jit(solution)/shard_map/all_gather | solution.py:196
  537.8 1603.0 %all-gather.15.cloned.1.call-start = ((), (), s32[]{:S(2)}) async-start(), calls=%async_computation.12 | async-start | bytes 47185920 | tf_op jit(solution)/shard_map/all_gather | solution.py:198
  538.4 2320.4 %all-gather.17.cloned.1.call-start = ((), (), s32[]{:S(2)}) async-start(), calls=%async_computation.13 | async-start | bytes 21712896 | tf_op jit(solution)/shard_map/all_gather | solution.py:238
  888.3 1345.3 %copy-start.14 = (f32[1,512,1536]{2,1,0:T(8,128)}, f32[1,512,1536]{2,1,0:T(8,128)S(1)}, u32[]{:S(2)}) copy-start(f32[1,512,1536]{2,1,0:T(8,128)S(1)} %get-tuple-element.959) | copy-start | bytes 9437188
  889.3 1294.6 %copy-start.91 = (bf16[1,77,1536]{2,1,0:T(8,128)(2,1)}, bf16[1,77,1536]{2,1,0:T(8,128)(2,1)S(1)}, u32[]{:S(2)}) copy-start(bf16[1,77,1536]{2,1,0:T(8,128)(2,1)S(1)} %add_convert_fusion.5) | copy-start | bytes 709636
  891.0 1249.8 %copy-start.108 = (f32[1,6144]{1,0:T(1,128)S(1)}, f32[1,6144]{1,0:T(1,128)}, u32[]{:S(2)}) copy-start(f32[1,6144]{1,0:T(1,128)} %get-tuple-element.1008) | copy-start | bytes 73732
  2586.1 13.0 collective-permute-start
  2684.0 1232.3 %reduce-scatter.37.cloned.1.call-start = ((), (), s32[]{:S(2)}) async-start(), calls=%async_computation.22 | async-start | bytes 811008
  2698.1 1225.3 %reduce-scatter.33.cloned.1.call-start = ((), (), s32[]{:S(2)}) async-start(), calls=%async_computation.20 | async-start | bytes 811008
  3533.5 33.1 collective-permute-start.1
  3547.4 389.6 %reduce-scatter.35.cloned.1.call-start = ((), (), s32[]{:S(2)}) async-start(), calls=%async_computation.21 | async-start | bytes 3244032
  3566.3 372.3 %reduce-scatter.31.cloned.1.call-start = ((), (), s32[]{:S(2)}) async-start(), calls=%async_computation.19 | async-start | bytes 2433024
  3618.7 321.4 %all-reduce.6.cloned.1.call-start = ((), (), s32[]{:S(2)}) async-start(), calls=%async_computation.14 | async-start | bytes 196608 | tf_op jit(solution)/shard_map/psum | solution.py:340
  3619.5 468.5 %reduce-scatter.25.cloned.1.call-start = ((), (), s32[]{:S(2)}) async-start(), calls=%async_computation.16 | async-start | bytes 19464192 | tf_op jit(solution)/shard_map/reduce_scatter | solution.py:54
  3634.2 932.7 %reduce-scatter.23.cloned.1.call-start = ((), (), s32[]{:S(2)}) async-start(), calls=%async_computation.15 | async-start | bytes 58392576 | tf_op jit(solution)/shard_map/reduce_scatter | solution.py:53
  3706.4 1523.2 %reduce-scatter.27.cloned.1.call-start = ((), (), s32[]{:S(2)}) async-start(), calls=%async_computation.17 | async-start | bytes 77856768 | tf_op jit(solution)/shard_map/reduce_scatter | solution.py:55
  3801.4 2091.9 %reduce-scatter.29.cloned.1.call-start = ((), (), s32[]{:S(2)}) async-start(), calls=%async_computation.18 | async-start | bytes 77856768 | tf_op jit(solution)/shard_map/reduce_scatter | solution.py:56
  (240 other events, 3100.1 us)
Sparse Core Ops, SparseCore 0:
  9.6 473.9 all-gather.6
  536.6 174.2 all-gather.8
  712.5 163.9 all-gather.10
  877.9 630.7 all-gather.12
  1510.1 630.6 all-gather.14
  2684.1 174.7 all-gather.16
  2864.0 93.7 reduce-scatter.36
  3547.5 95.2 reduce-scatter.32
  3648.2 100.5 reduce-scatter.34
  3753.9 98.1 reduce-scatter.30
  3855.0 21.3 all-reduce.5
  3884.4 203.6 reduce-scatter.24
  4096.2 470.6 reduce-scatter.22
  4573.7 655.8 reduce-scatter.26
  5237.6 655.6 reduce-scatter.28
where the time goes:
time: 5920 us; the launch traced here: 5900 us
  waiting for transfers between devices  3920 us (66%)
  matrix products  889 us (15%)
  local copies, waits for them, and re-layouts  435 us (7%)
  other arithmetic  403 us (7%)
  blocking collectives  214 us (4%)
    reduce_scatter x1, waiting for transfers between devices, reduce_grads(): lax.psum_scatter(weight_terms[3], ('seq', 'fsdp', 'dp'), scatter_dimensio...  664 us
    reduce_scatter x1, waiting for transfers between devices, reduce_grads(): lax.psum_scatter(weight_terms[2], ('seq', 'fsdp', 'dp'), scatter_dimensio...  663 us
    all_gather x1, waiting for transfers between devices, local(): lax.all_gather(w_up, 'fsdp', axis=1, tiled=True)  618 us
    all_gather x1, waiting for transfers between devices, local(): lax.all_gather(w_down, 'fsdp', axis=1, tiled=True)  614 us
    reduce_scatter x1, waiting for transfers between devices, reduce_grads(): lax.psum_scatter(weight_terms[0], ('seq', 'fsdp', 'dp'), scatter_dimensio...  479 us
    all_gather x1, waiting for transfers between devices, local(): lax.all_gather(w_qkv, 'fsdp', axis=1, tiled=True)  456 us
    all_gather x2, waiting for transfers between devices, local(): lax.all_gather(joint_rows[..., model_width:], 'seq', axis=1, tiled=True)  264 us
    dot_general x16, matrix products, linear(): jnp.einsum('mnd,dc->mnc', values, weight, preferred_element_type=jnp.floa...  191 us
  transfers between devices with their start and end apart: 17, of which 10 were waited for; matrix products, arithmetic and copies ran while one was open for 21% of the time, Pallas kernels for 0%

commit v1 on v0

v1 whole, which is shorter than its diff:
```python
import functools

import jax
import jax.numpy as jnp
from jax import lax
from jax.experimental import pallas as pl
from jax.experimental.pallas import tpu as pltpu
from jax.sharding import PartitionSpec as P

EPSILON = 1e-06
HEAD_DIM=64
MASKED=-1000000000.0
def dot(a,b,ca,cb):
    return lax.dot_general(a,b,(((ca,),(cb,)),((),())),preferred_element_type=jnp.float32)

def attn_fwd_kernel(ti,tt,tq,len_ref,qi,ki,vi,qt,kt,vt,oi,ot,lse,ktp,vtp):
    tp=ktp.shape[0]
    ktp[...]=jnp.zeros_like(ktp); vtp[...]=jnp.zeros_like(vtp)
    ktp[:tt,:]=kt[...]; vtp[:tt,:]=vt[...]
    n_len=len_ref[0]; half=len_ref[1]; mine=len_ref[2]
    r=lax.broadcasted_iota(jnp.int32,(1,tp),1)
    pos=jnp.where(r<half,mine*half+r,(1-mine)*half+r-half)
    valid=(r<2*half)&(pos<n_len)
    lane=lax.broadcasted_iota(jnp.int32,(1,2*HEAD_DIM),1)
    k_img=ki[...]; v_img=vi[...]; k_txt=ktp[...]; v_txt=vtp[...]
    def one(q,rows):
        outs=[];lses=[]
        for h in range(2):
            qh=jnp.where((lane<HEAD_DIM)==(h==0),q.astype(jnp.float32)*(HEAD_DIM**-0.5),0.0).astype(jnp.bfloat16)
            s1=dot(qh,k_img,1,1); s2=dot(qh,k_txt,1,1)
            s2=jnp.where(valid,s2,MASKED)
            m=jnp.maximum(jnp.max(s1,axis=1,keepdims=True),jnp.max(s2,axis=1,keepdims=True))
            e1=jnp.exp(s1-m); e2=jnp.exp(s2-m)
            l=jnp.sum(e1,axis=1,keepdims=True)+jnp.sum(e2,axis=1,keepdims=True)
            inv=1.0/l
            o=dot((e1*inv).astype(jnp.bfloat16),v_img,1,0)+dot((e2*inv).astype(jnp.bfloat16),v_txt,1,0)
            outs.append(o); lses.append(m+jnp.log(l))
        o=jnp.where(lane<HEAD_DIM,outs[0],outs[1]).astype(jnp.bfloat16)
        both=jnp.where(lane<HEAD_DIM,jnp.broadcast_to(lses[0],(rows,128)),jnp.broadcast_to(lses[1],(rows,128)))
        return o,both.T
    def step(i,_):
        start=pl.multiple_of(i*tq,tq)
        o,b=one(qi[pl.ds(start,tq),:],tq)
        oi[pl.ds(start,tq),:]=o
        lse[0,0:1,pl.ds(start,tq)]=b[0:1]; lse[0,1:2,pl.ds(start,tq)]=b[64:65]
        return 0
    lax.fori_loop(0,ti//tq,step,0)
    qpad=jnp.concatenate([qt[...],jnp.zeros((tp-tt,128),jnp.bfloat16)],axis=0)
    o,b=one(qpad,tp)
    ot[...]=o[:tt]
    lse[0,0:1,ti:ti+tp]=b[0:1]; lse[0,1:2,ti:ti+tp]=b[64:65]

def attn_fwd(qkv_i,qkv_t,info,tq=256):
    ti,w3=qkv_i.shape; tt=qkv_t.shape[0]; w=w3//3; n=w//128; tp=256
    bi=lambda off: pl.BlockSpec((ti,128),lambda p,s,off=off:(0,p+off*n))
    bt=lambda off: pl.BlockSpec((tt,128),lambda p,s,off=off:(0,p+off*n))
    return pl.pallas_call(functools.partial(attn_fwd_kernel,ti,tt,tq),
        grid_spec=pltpu.PrefetchScalarGridSpec(num_scalar_prefetch=1,grid=(n,),
            in_specs=[bi(0),bi(1),bi(2),bt(0),bt(1),bt(2)],
            out_specs=[bi(0),bt(0),pl.BlockSpec((1,8,ti+tp),lambda p,s:(p,0,0))],
            scratch_shapes=[pltpu.VMEM((tp,128),jnp.bfloat16)]*2),
        out_shape=[jax.ShapeDtypeStruct((ti,w),jnp.bfloat16),jax.ShapeDtypeStruct((tt,w),jnp.bfloat16),
                   jax.ShapeDtypeStruct((n,8,ti+tp),jnp.float32)],
        compiler_params=pltpu.CompilerParams(vmem_limit_bytes=48<<20),
        cost_estimate=pl.CostEstimate(flops=8*(ti+tt)*(ti+tt)*w,bytes_accessed=8*(ti+tt)*w,transcendentals=2*n*(ti+tt)*(ti+tt)),
        name="attn_fwd")(info,qkv_i,qkv_i,qkv_i,qkv_t,qkv_t,qkv_t)

def attn_bwd_kernel(ti,tt,tq,len_ref,qi,ki,vi,qt,kt,vt,oi,ot,di,dt,lse,outi,outt,ktp,vtp,dk1,dk2,dv1,dv2,dqi,dqt):
    j=pl.program_id(1)
    tp=ktp.shape[0]
    @pl.when(j==0)
    def _():
        ktp[...]=jnp.zeros_like(ktp); vtp[...]=jnp.zeros_like(vtp)
        ktp[:tt,:]=kt[...]; vtp[:tt,:]=vt[...]
        n_len=len_ref[0]; half=len_ref[1]; mine=len_ref[2]
        r=lax.broadcasted_iota(jnp.int32,(tp,1),0)
        pos=jnp.where(r<half,mine*half+r,(1-mine)*half+r-half)
        valid=(r<2*half)&(pos<n_len)
        lane=lax.broadcasted_iota(jnp.int32,(1,128),1)
        sub=lax.broadcasted_iota(jnp.int32,(8,128),0); lane8=lax.broadcasted_iota(jnp.int32,(8,128),1)
        sel=jnp.where((lane8//HEAD_DIM)==sub,1.0,0.0).astype(jnp.bfloat16)
        k_img=ki[...]; v_img=vi[...]; k_txt=ktp[...]; v_txt=vtp[...]
        for ref in (dk1,dk2,dv1,dv2): ref[...]=jnp.zeros_like(ref)
        def one(q,do,o,ls):
            prod=do.astype(jnp.float32)*o.astype(jnp.float32)
            hi=prod.astype(jnp.bfloat16); lo=(prod-hi.astype(jnp.float32)).astype(jnp.bfloat16)
            dsum=dot(sel,hi,1,1)+dot(sel,lo,1,1)
            qs=(q.astype(jnp.float32)*(HEAD_DIM**-0.5))
            dof=do.astype(jnp.float32)
            dqs=[]
            for h in range(2):
                mk=(lane<HEAD_DIM)==(h==0)
                qh=jnp.where(mk,qs,0.0).astype(jnp.bfloat16)
                dh=jnp.where(mk,dof,0.0).astype(jnp.bfloat16)
                L=ls[h:h+1]; D=dsum[h:h+1]
                s1=dot(k_img,qh,1,1); s2=dot(k_txt,qh,1,1)
                p1=jnp.exp(s1-L); p2=jnp.where(valid,jnp.exp(s2-L),0.0)
                dp1=dot(v_img,dh,1,1); dp2=dot(v_txt,dh,1,1)
                ds1=(p1*(dp1-D)).astype(jnp.bfloat16); ds2=(p2*(dp2-D)).astype(jnp.bfloat16)
                dv1[...]+=dot(p1.astype(jnp.bfloat16),dh,1,0)
                dv2[...]+=dot(p2.astype(jnp.bfloat16),dh,1,0)
                dk1[...]+=dot(ds1,qh,1,0)
                dk2[...]+=dot(ds2,qh,1,0)
                dqs.append(dot(ds1,k_img,0,0)+dot(ds2,k_txt,0,0))
            return (jnp.where(lane<HEAD_DIM,dqs[0],dqs[1])*(HEAD_DIM**-0.5)).astype(jnp.bfloat16)
        def step(i,_):
            start=pl.multiple_of(i*tq,tq)
            sl=pl.ds(start,tq)
            dqi[sl,:]=one(qi[sl,:],di[sl,:],oi[sl,:],lse[0,:,sl])
            return 0
        lax.fori_loop(0,ti//tq,step,0)
        pad=lambda a: jnp.concatenate([a,jnp.zeros((tp-tt,128),jnp.bfloat16)],axis=0)
        dqt[...]=one(pad(qt[...]),pad(dt[...]),pad(ot[...]),lse[0,:,ti:ti+tp])[:tt]
        outi[...]=dqi[...]; outt[...]=dqt[...]
    @pl.when(j==1)
    def _():
        outi[...]=dk1[...].astype(jnp.bfloat16); outt[...]=dk2[:tt,:].astype(jnp.bfloat16)
    @pl.when(j==2)
    def _():
        outi[...]=dv1[...].astype(jnp.bfloat16); outt[...]=dv2[:tt,:].astype(jnp.bfloat16)

def attn_bwd(qkv_i,qkv_t,o_i,o_t,d_i,d_t,lse,info,tq=256):
    ti,w3=qkv_i.shape; tt=qkv_t.shape[0]; w=w3//3; n=w//128; tp=256
    bi=lambda off: pl.BlockSpec((ti,128),lambda p,j,s,off=off:(0,p+off*n))
    bt=lambda off: pl.BlockSpec((tt,128),lambda p,j,s,off=off:(0,p+off*n))
    return pl.pallas_call(functools.partial(attn_bwd_kernel,ti,tt,tq),
        grid_spec=pltpu.PrefetchScalarGridSpec(num_scalar_prefetch=1,grid=(n,3),
            in_specs=[bi(0),bi(1),bi(2),bt(0),bt(1),bt(2),bi(0),bt(0),bi(0),bt(0),pl.BlockSpec((1,8,ti+tp),lambda p,j,s:(p,0,0))],
            out_specs=[pl.BlockSpec((ti,128),lambda p,j,s:(0,p+j*n)),pl.BlockSpec((tt,128),lambda p,j,s:(0,p+j*n))],
            scratch_shapes=[pltpu.VMEM((tp,128),jnp.bfloat16)]*2+[pltpu.VMEM((ti,128),jnp.float32),pltpu.VMEM((tp,128),jnp.float32)]*2
              +[pltpu.VMEM((ti,128),jnp.bfloat16),pltpu.VMEM((tt,128),jnp.bfloat16)]),
        out_shape=[jax.ShapeDtypeStruct((ti,w3),jnp.bfloat16),jax.ShapeDtypeStruct((tt,w3),jnp.bfloat16)],
        compiler_params=pltpu.CompilerParams(vmem_limit_bytes=56<<20),
        cost_estimate=pl.CostEstimate(flops=20*(ti+tt)*(ti+tt)*w,bytes_accessed=16*(ti+tt)*w,transcendentals=2*n*(ti+tt)*(ti+tt)),
        name="attn_bwd")(info,qkv_i,qkv_i,qkv_i,qkv_t,qkv_t,qkv_t,o_i,o_t,d_i,d_t,lse)


def normalize(values):
    row_mean = jnp.mean(values, axis=-1, keepdims=True)
    centred = values - row_mean
    variance = jnp.mean(centred * centred, axis=-1, keepdims=True)
    inverse = lax.rsqrt(variance + EPSILON)
    return (centred * inverse, inverse)


def normalize_back(normed, inverse, upstream):
    mean_one = jnp.mean(upstream, axis=-1, keepdims=True)
    mean_two = jnp.mean(upstream * normed, axis=-1, keepdims=True)
    return inverse * (upstream - mean_one - normed * mean_two)


def linear(values, weight, offset):
    return jnp.dot(values, weight, preferred_element_type=jnp.float32) + offset.astype(jnp.float32)


def linear_back(upstream, weight):
    return dot(upstream, weight, 1, 1)


def gelu_tanh(values):
    return jax.nn.gelu(values, approximate=True)


def coords():
    dp = lax.axis_index("dp")
    return lax.axis_index("seq"), lax.axis_index("fsdp"), dp // 4, (dp // 2) % 2, dp % 2


def flip_x(a):
    return lax.ppermute(a, "seq", [(0, 1), (1, 0)])


def flip_y(a):
    return lax.ppermute(a, "dp", [(i, i ^ 2) for i in range(lax.axis_size("dp"))])


def flip_core(a):
    return lax.ppermute(a, "dp", [(i, i ^ 1) for i in range(lax.axis_size("dp"))])


def shift_z(a, k):
    n = lax.axis_size("fsdp")
    return lax.ppermute(a, "fsdp", [(i, (i + k) % n) for i in range(n)])


def shift_group(a, k):
    n = lax.axis_size("dp")
    return lax.ppermute(a, "dp", [(i, (i + 4 * k) % n) for i in range(n)])


def assemble(shard, parts):
    s, r, cols = shard.shape
    fs = parts[0][1].shape[0] + 1
    q, h = r // 4, cols // 2
    width = next(t for t in (768, 384, 256, 128) if h % t == 0 and fs * r * t * 2 <= (5 << 20))
    steps = [(i, j) for i in range(s) for j in range(cols // width)]

    def kernel(*refs):
        own, ins = refs[0], refs[1 : 1 + len(parts)]
        outs = refs[1 + len(parts) : 1 + len(parts) + s]
        buf, in_sem, out_sem = refs[1 + len(parts) + s :]
        x, z, _, y, c = coords()

        def loads(step):
            i, j = steps[step]
            slot = step % 2
            jobs = [(own.at[i, :, pl.ds(j * width, width)], z * r, r)]
            return i, j, slot, jobs

        def run(c_val):
            def copies(step):
                i, j, slot, jobs = loads(step)
                half = j * width // h
                dc_need = half ^ c_val
                for ref, ((dx, dy, dc), _) in zip(ins, parts):
                    if dc != dc_need:
                        continue
                    for k in range(1, fs):
                        src_z = lax.rem(z - k + fs, fs)
                        xx = x + dx - 2 * x * dx
                        yy = y + dy - 2 * y * dy
                        jobs.append(
                            (ref.at[k - 1, i, :, pl.ds(j * width - half * h, width)], src_z * r + (xx * 2 + yy) * q, q)
                        )
                return [
                    pltpu.make_async_copy(src, buf.at[slot, pl.ds(pl.multiple_of(row, 16), n), :], in_sem.at[slot, m])
                    for m, (src, row, n) in enumerate(jobs)
                ]

            def store(step):
                i, j = steps[step]
                return pltpu.make_async_copy(buf.at[step % 2], outs[i].at[:, pl.ds(j * width, width)], out_sem.at[step % 2])

            for cp in copies(0):
                cp.start()
            for step in range(len(steps)):
                if step + 1 < len(steps):
                    if step >= 1:
                        store(step - 1).wait()
                    for cp in copies(step + 1):
                        cp.start()
                for cp in copies(step):
                    cp.wait()
                store(step).start()
            if len(steps) > 1:
                store(len(steps) - 2).wait()
            store(len(steps) - 1).wait()

        for c_val in range(2):
            @pl.when(c == c_val)
            def _():
                run(c_val)

    n_in = 1 + 4 * (fs - 1)
    return pl.pallas_call(
        kernel,
        out_shape=[jax.ShapeDtypeStruct((r * fs, cols), shard.dtype)] * s,
        in_specs=[pl.BlockSpec(memory_space=pl.ANY)] * (1 + len(parts)),
        out_specs=[pl.BlockSpec(memory_space=pl.ANY)] * s,
        scratch_shapes=[
            pltpu.VMEM((2, fs * r, width), shard.dtype),
            pltpu.SemaphoreType.DMA((2, n_in)),
            pltpu.SemaphoreType.DMA((2,)),
        ],
        compiler_params=pltpu.CompilerParams(vmem_limit_bytes=32 << 20),
        cost_estimate=pl.CostEstimate(flops=0, bytes_accessed=4 * s * r * fs * cols, transcendentals=0),
        name="assemble",
    )(shard, *[a for _, a in parts])


def gather_weight(shard, x_first):
    fs = lax.axis_size("fsdp")
    x, z, _, y, c = coords()
    s, r, cols = shard.shape
    q, h = r // 4, cols // 2
    piece = lax.dynamic_slice(shard, (0, (x * 2 + y) * q, c * h), (s, q, h))
    slots, current = [], piece
    for _ in range(1, fs):
        current = shift_z(current, 1)
        slots.append(current)
    own = jnp.stack(slots)
    if x_first:
        first = flip_x(own)
        parts = [((0, 0, 0), own), ((1, 0, 0), first), ((0, 1, 0), flip_y(own)), ((1, 1, 0), flip_y(first))]
    else:
        first = flip_y(own)
        parts = [((0, 0, 0), own), ((0, 1, 0), first), ((1, 0, 0), flip_x(own)), ((1, 1, 0), flip_x(first))]
    parts = parts + [((dx, dy, 1), flip_core(a)) for (dx, dy, _), a in parts]
    return assemble(shard, parts)


def wgrad_kernel(sel_ref, a0, b0, a1, b1, out):
    out[...] = (dot(a0[...], b0[...], 0, 0) + dot(a1[...], b1[...], 0, 0)).astype(out.dtype)


def wgrad(a0, b0, a1, b1, row_half, col_half):
    tokens, rows = a0.shape
    cols = b0.shape[1]
    tr = tc = 768
    nr, nc = rows // 2 // tr, cols // 2 // tc
    a_spec = pl.BlockSpec((tokens, tr), lambda i, j, s: (0, s[0] * nr + i))
    b_spec = pl.BlockSpec((tokens, tc), lambda i, j, s: (0, s[1] * nc + j))
    return pl.pallas_call(
        wgrad_kernel,
        grid_spec=pltpu.PrefetchScalarGridSpec(
            num_scalar_prefetch=1,
            grid=(nr, nc),
            in_specs=[a_spec, b_spec, a_spec, b_spec],
            out_specs=pl.BlockSpec((tr, tc), lambda i, j, s: (i, j)),
        ),
        out_shape=jax.ShapeDtypeStruct((rows // 2, cols // 2), jnp.bfloat16),
        compiler_params=pltpu.CompilerParams(vmem_limit_bytes=48 << 20),
        cost_estimate=pl.CostEstimate(
            flops=2 * 2 * tokens * rows * cols // 4,
            bytes_accessed=2 * (tokens * rows + tokens * cols) + rows * cols // 2,
            transcendentals=0,
        ),
        name="wgrad",
    )(jnp.stack([row_half, col_half]).astype(jnp.int32), a0, b0, a1, b1)


def reduce_weight(pairs):
    fs, groups = lax.axis_size("fsdp"), lax.axis_size("dp") // 4
    x, z, g, y, c = coords()
    finals = []
    for left, right in pairs:
        far_left, far_right = flip_core(left), flip_core(right)
        send = wgrad(left, right, far_left, far_right, 1 - x, c)
        recv = flip_x(send)
        keep = wgrad(left, right, far_left, far_right, x, c)
        half_rows, half_cols = keep.shape
        q = half_rows // (fs * groups * 2)
        view = lambda a: a.reshape(fs, groups, 2, q, half_cols)
        at = lambda a, i, axis: lax.dynamic_index_in_dim(a, i, axis, keepdims=False)
        send_y = (
            at(view(keep), 1 - y, 2).astype(jnp.float32) + at(view(recv), 1 - y, 2).astype(jnp.float32)
        ).astype(jnp.bfloat16)
        recv_y = flip_y(send_y)

        def block(index):
            return (
                at(at(view(keep), y, 2), index, 0).astype(jnp.float32)
                + at(at(view(recv), y, 2), index, 0).astype(jnp.float32)
                + at(recv_y, index, 0).astype(jnp.float32)
            )

        total = block(z)
        for k in range(1, fs):
            total = total + shift_z(block((z + k) % fs).astype(jnp.bfloat16), k).astype(jnp.float32)
        mine = at(total, g, 0)
        for k in range(1, groups):
            mine = mine + shift_group(at(total, (g + k) % groups, 0), k)
        rows = q // 2
        near = lax.dynamic_slice_in_dim(mine, c * rows, rows, 0)
        far = flip_core(lax.dynamic_slice_in_dim(mine, (1 - c) * rows, rows, 0))
        finals.append(
            jnp.concatenate([jnp.where(c == 0, near, far), jnp.where(c == 0, far, near)], axis=1)
        )
    return jnp.stack(finals)


def local(
    image_in,
    text_in,
    modulation,
    text_len,
    w_qkv,
    b_qkv,
    w_out,
    b_out,
    w_up,
    b_up,
    w_down,
    b_down,
    d_image,
    d_text,
):
    x, z, g, y, c = coords()
    image_half, text_half = image_in.shape[1], text_in.shape[1]
    width = image_in.shape[2]
    text_rows = -(-2 * text_half // 16) * 16

    def take(arr):
        return lax.dynamic_index_in_dim(arr, x, 0, keepdims=False)

    def give(arr):
        return flip_x(lax.dynamic_index_in_dim(arr, 1 - x, 0, keepdims=False))

    def join(arr, rows):
        near, far = take(arr), give(arr)
        pad = jnp.zeros((rows - 2 * near.shape[0], width), near.dtype)
        return jnp.concatenate([near, far, pad], axis=0)

    def unjoin(arr, half, kind):
        near = arr[:half].astype(kind)
        far = flip_x(arr[half : 2 * half].astype(jnp.bfloat16)).astype(kind)
        return jnp.where(x == 0, jnp.stack([near, far]), jnp.stack([far, near]))

    streams = (join(image_in, 2 * image_half), join(text_in, text_rows))
    weight_qkv = gather_weight(w_qkv, True)
    small = lax.all_gather(
        jnp.concatenate([b_qkv, b_out, b_up, b_down], axis=1), "fsdp", axis=0, tiled=False
    )
    edges = [0]
    for b in (b_qkv, b_out, b_up, b_down):
        edges.append(edges[-1] + b.shape[1])
    biases = [
        small[:, :, edges[i] : edges[i + 1]].transpose(1, 0, 2).reshape(2, -1) for i in range(4)
    ]
    bias_qkv, bias_out, bias_up, bias_down = biases
    weight_out = gather_weight(w_out, False)
    weight_up = gather_weight(w_up, True)
    weight_down = gather_weight(w_down, False)
    cotangents = (join(d_image, 2 * image_half), join(d_text, text_rows))
    gains = take(modulation)
    info = jnp.stack([take(text_len), jnp.int32(text_half), x.astype(jnp.int32)])

    fronts = []
    for s in range(2):
        mod = gains[s]
        normed, inverse = normalize(streams[s].astype(jnp.float32))
        modded = (normed * (1.0 + mod[1]) + mod[0]).astype(jnp.bfloat16)
        projected = linear(modded, weight_qkv[s], bias_qkv[s]).astype(jnp.bfloat16)
        fronts.append((normed, inverse, modded, projected))
    att_i, att_t, lse = attn_fwd(fronts[0][3], fronts[1][3], info, tq=2 * image_half)
    attended = (att_i, att_t)
    outs, state = [], []
    for s in range(2):
        mod = gains[s]
        branch = linear(attended[s], weight_out[s], bias_out[s])
        middle = streams[s].astype(jnp.float32) + mod[2] * branch
        normed_two, inverse_two = normalize(middle)
        modded_two = (normed_two * (1.0 + mod[4]) + mod[3]).astype(jnp.bfloat16)
        hidden = linear(modded_two, weight_up[s], bias_up[s])
        active = gelu_tanh(hidden).astype(jnp.bfloat16)
        mlp_out = linear(active, weight_down[s], bias_down[s])
        outs.append((middle + mod[5] * mlp_out).astype(jnp.bfloat16))
        upstream = cotangents[s].astype(jnp.float32)
        d_gate_two = jnp.sum(upstream * mlp_out, axis=0)
        d_mlp = (mod[5] * upstream).astype(jnp.bfloat16)
        state.append((branch, normed_two, inverse_two, modded_two, hidden, active, upstream, d_gate_two, d_mlp))
    grads_down = reduce_weight([(state[s][5], state[s][8]) for s in range(2)])
    backs = []
    for s in range(2):
        mod = gains[s]
        branch, normed_two, inverse_two, modded_two, hidden, active, upstream, d_gate_two, d_mlp = state[s]
        d_active = linear_back(d_mlp, weight_down[s])
        d_hidden = jax.vjp(gelu_tanh, hidden)[1](d_active)[0].astype(jnp.bfloat16)
        d_modded_two = linear_back(d_hidden, weight_up[s])
        d_shift_two = jnp.sum(d_modded_two, axis=0)
        d_scale_two = jnp.sum(d_modded_two * normed_two, axis=0)
        d_middle = upstream + normalize_back(normed_two, inverse_two, d_modded_two * (1.0 + mod[4]))
        d_gate_one = jnp.sum(d_middle * branch, axis=0)
        d_branch = (mod[2] * d_middle).astype(jnp.bfloat16)
        d_attended = linear_back(d_branch, weight_out[s]).astype(jnp.bfloat16)
        backs.append((d_hidden, d_shift_two, d_scale_two, d_middle, d_gate_one, d_branch, d_attended))
    grads_up = reduce_weight([(state[s][3], backs[s][0]) for s in range(2)])
    grads_out = reduce_weight([(attended[s], backs[s][5]) for s in range(2)])
    d_front = attn_bwd(
        fronts[0][3], fronts[1][3], att_i, att_t, backs[0][6], backs[1][6], lse, info, tq=image_half
    )
    grads_qkv = reduce_weight([(fronts[s][2], d_front[s]) for s in range(2)])
    input_grads, gain_grads = [], []
    for s in range(2):
        mod = gains[s]
        normed, inverse, modded, _ = fronts[s]
        d_hidden, d_shift_two, d_scale_two, d_middle, d_gate_one, d_branch, _ = backs[s]
        d_modded = linear_back(d_front[s], weight_qkv[s])
        d_shift_one = jnp.sum(d_modded, axis=0)
        d_scale_one = jnp.sum(d_modded * normed, axis=0)
        input_grads.append(d_middle + normalize_back(normed, inverse, d_modded * (1.0 + mod[1])))
        gain_grads.append(
            jnp.stack([d_shift_one, d_scale_one, d_gate_one, d_shift_two, d_scale_two, state[s][7]])
        )
    mine = jnp.stack(gain_grads)
    theirs = flip_x(mine)
    grad_modulation = jnp.where(x == 0, jnp.stack([mine, theirs]), jnp.stack([theirs, mine]))

    axes = ("seq", "fsdp", "dp")
    count = lax.axis_size(axes)

    def bias_rows(right):
        total = jnp.stack([jnp.sum(r.astype(jnp.float32), axis=0) for r in right])
        return total.reshape(2, count, -1).transpose(1, 0, 2).reshape(count, -1)

    def reduce_bias(rights):
        rows = [bias_rows(r) for r in rights]
        cut = lax.psum_scatter(jnp.concatenate(rows, axis=1), axes, scatter_dimension=0, tiled=True)[0]
        result, start = [], 0
        for r in rows:
            result.append(cut[start : start + r.shape[1]].reshape(2, -1))
            start += r.shape[1]
        return result

    gb_out, gb_up, gb_down = reduce_bias(
        [[backs[s][5] for s in range(2)], [backs[s][0] for s in range(2)], [state[s][8] for s in range(2)]]
    )
    (gb_qkv,) = reduce_bias([d_front])
    return (
        unjoin(outs[0], image_half, jnp.bfloat16),
        unjoin(outs[1], text_half, jnp.bfloat16),
        unjoin(input_grads[0], image_half, jnp.float32),
        unjoin(input_grads[1], text_half, jnp.float32),
        grad_modulation,
        grads_qkv,
        gb_qkv,
        grads_out,
        gb_out,
        grads_up,
        gb_up,
        grads_down,
        gb_down,
    )


def solution(mesh):
    tokens = P(("fsdp", "dp"), "seq", None)
    weight, bias = P(None, "fsdp", None), P(None, "fsdp")
    in_specs = (tokens, tokens, P(("fsdp", "dp"), None, None, None), P(("fsdp", "dp")))
    in_specs += (weight, bias) * 4 + (tokens, tokens)
    grad_w, grad_b = P(None, ("seq", "fsdp", "dp"), None), P(None, ("seq", "fsdp", "dp"))
    out_specs = (tokens,) * 4 + (P(("fsdp", "dp"), None, None, None),) + (grad_w, grad_b) * 4
    return jax.shard_map(local, mesh=mesh, in_specs=in_specs, out_specs=out_specs, check_vma=False)
```

time: 5920 us -> 2190 us (0.37)
  waiting for transfers between devices: 3920 us -> 785 us
  matrix products: 889 us -> 274 us
  Pallas kernels: 0 us -> 438 us
  local copies, waits for them, and re-layouts: 435 us -> 80.4 us
  other arithmetic: 403 us -> 135 us
  starting transfers between devices: 6.24 us -> 253 us
    all_gather x6 -> x0, waiting for transfers between devices: 1970 us -> none  [the longest x1 618 us: local(): lax.all_gather(w_up, 'fsdp', axis=1, tiled=True)]
    reduce_scatter x4 -> x0, waiting for transfers between devices: 1950 us -> none  [the longest x1 664 us: reduce_grads(): lax.psum_scatter(weight_terms[3], ('seq', 'fsdp', 'dp'), scatter_dimensio...]
    ppermute x0 -> x113, waiting for transfers between devices: none -> 785 us  [the longest x23 374 us: flip_x(): return lax.ppermute(a, 'seq', [(0, 1), (1, 0)])]
    dot_general x82 -> x16, matrix products: 889 us -> 274 us  [the longest x8 150 us: dot(): lax.dot_general(a, b, (((ca,), (cb,)), ((), ())), preferred_element_type=...]
    pallas_call x0 -> x22, Pallas kernels: none -> 438 us  [the longest x1 145 us: attn_bwd(): pl.pallas_call(functools.partial(attn_bwd_kernel, ti, tt, tq), grid_spec=...]
    ppermute x0 -> x113, starting transfers between devices: none -> 253 us  [the longest x40 151 us: flip_core(): lax.ppermute(a, 'dp', [(i, i ^ 1) for i in range(lax.axis_size('dp'))])]
    another operation x8 -> x21, other arithmetic: 156 us -> 20 us  [the longest x4 9.79 us: gather_weight(): own = jnp.stack(slots)]
    unnamed x444 -> x333, local copies, waits for them, and re-layouts: 151 us -> 21 us
  transfers between devices with their start and end apart: 17 -> 114, of which waited for: 10 -> 38; matrix products, arithmetic and copies ran while one was open for 21% -> 22% of each run, Pallas kernels for 0% -> 20%
where the time goes in v1:
time: 2190 us; the launch traced here: 2180 us
  waiting for transfers between devices  785 us (36%)
  Pallas kernels  438 us (20%)
  matrix products  274 us (13%)
  starting transfers between devices  253 us (12%)
  blocking collectives  202 us (9%)
  other arithmetic  135 us (6%)
  local copies, waits for them, and re-layouts  80.4 us (4%)
    ppermute x23, waiting for transfers between devices, flip_x(): return lax.ppermute(a, 'seq', [(0, 1), (1, 0)])  374 us
    ppermute x36, waiting for transfers between devices, shift_z(): return lax.ppermute(a, 'fsdp', [(i, (i + k) % n) for i in range(n)])  241 us
    unnamed x1, blocking collectives  189 us
    ppermute x14, waiting for transfers between devices, flip_y(): lax.ppermute(a, 'dp', [(i, i ^ 2) for i in range(lax.axis_size('dp'))])  162 us
    ppermute x40, starting transfers between devices, flip_core(): lax.ppermute(a, 'dp', [(i, i ^ 1) for i in range(lax.axis_size('dp'))])  151 us
    dot_general x8, matrix products, dot(): lax.dot_general(a, b, (((ca,), (cb,)), ((), ())), preferred_element_type=...  150 us
    pallas_call x1, Pallas kernels, attn_bwd(): pl.pallas_call(functools.partial(attn_bwd_kernel, ti, tt, tq), grid_spec=...  145 us
    pallas_call x16, Pallas kernels, wgrad(): pl.pallas_call(wgrad_kernel, grid_spec=pltpu.PrefetchScalarGridSpec(num_s...  141 us
  transfers between devices with their start and end apart: 114, of which 38 were waited for; matrix products, arithmetic and copies ran while one was open for 22% of the time, Pallas kernels for 20%

profile of v1, /device:TPU:9, one launch (start us, length us, event | category | flops | bytes accessed | tf_op | source)
XLA Modules:
  0.0 2184.2 jit_solution(16808830953654389052)
XLA Ops:
  62.7 38.5 %collective-permute-done.3 = bf16[2,96,2304]{2,1,0:T(8,128)(2,1)} collective-permute-done((bf16[2,96,2304]{2,1,0:T(8,128)(2,1)}, bf16[2,96,2304]{2,1,0:T(8,128)(2,1)}, u32[]{:S(2)}, u32[]{:S(2)}) %collective-permute-start.3) | collective-permute-done | bytes 884768 | tf_op jit(solution)/shard_map/ppermute | solution.py:183
  158.3 55.8 %collective-permute-done.16.refs_3_ = bf16[3,2,96,768]{3,2,1,0:T(8,128)(2,1)} collective-permute-done((bf16[3,2,96,768]{3,2,1,0:T(8,128)(2,1)S(1)}, bf16[3,2,96,768]{3,2,1,0:T(8,128)(2,1)}, u32[]{:S(2)}, u32[]{:S(2)}) %collective-permute-start.16) | collective-permute-done | bytes 884768 | tf_op jit(solution)/shard_map/ppermute | solution.py:170
  298.4 25.4 %collective-permute-done.6.refs_4_ = bf16[3,2,96,2304]{3,2,1,0:T(8,128)(2,1)} collective-permute-done((bf16[3,2,96,2304]{3,2,1,0:T(8,128)(2,1)}, bf16[3,2,96,2304]{3,2,1,0:T(8,128)(2,1)}, u32[]{:S(2)}, u32[]{:S(2)}) %collective-permute-start.6) | collective-permute-done | bytes 2654240 | tf_op jit(solution)/shard_map/ppermute | solution.py:174
  361.6 38.0 %collective-permute-done.35.refs_2_ = bf16[3,2,384,768]{3,2,1,0:T(8,128)(2,1)} collective-permute-done((bf16[3,2,384,768]{3,2,1,0:T(8,128)(2,1)S(1)}, bf16[3,2,384,768]{3,2,1,0:T(8,128)(2,1)}, u32[]{:S(2)}, u32[]{:S(2)}) %collective-permute-start.35) | collective-permute-done | bytes 3538976 | tf_op jit(solution)/shard_map/ppermute | solution.py:174
  428.8 23.9 %assemble.4 = (bf16[1536,4608]{1,0:T(8,128)(2,1)}, bf16[1536,4608]{1,0:T(8,128)(2,1)}) custom-call(bf16[2,384,4608]{2,1,0:T(8,128)(2,1)} %refs_0_.4, bf16[3,2,96,2304]{3,2,1,0:T(8,128)(2,1)} %pad_maximum_fusion.4.refs_1_, bf16[3,2,96,2304]{3,2,1,0:T(8,128)(2,1)} %collective-permute-done.4.refs_2_, bf16[3,2,96,2304]{3,2,1,0:T(8,128)(2,1)} %collective-permute-done.5.refs_3_, ...), custom_call_target="tpu_custom_call" | custom-call | bytes 56623104 | tf_op jit(solution)/shard_map/assemble/pallas_call | solution.py:255
  483.8 55.5 %collective-permute-done.36.refs_3_ = bf16[3,2,384,768]{3,2,1,0:T(8,128)(2,1)} collective-permute-done((bf16[3,2,384,768]{3,2,1,0:T(8,128)(2,1)S(1)}, bf16[3,2,384,768]{3,2,1,0:T(8,128)(2,1)}, u32[]{:S(2)}, u32[]{:S(2)}) %collective-permute-start.36) | collective-permute-done | bytes 3538976 | tf_op jit(solution)/shard_map/ppermute | solution.py:170
  539.3 30.5 %collective-permute-start.40 = (bf16[3,2,384,768]{3,2,1,0:T(8,128)(2,1)}, bf16[3,2,384,768]{3,2,1,0:T(8,128)(2,1)}, u32[]{:S(2)}, u32[]{:S(2)}) collective-permute-start(bf16[3,2,384,768]{3,2,1,0:T(8,128)(2,1)} %collective-permute-done.36.refs_3_), channel_id=1, source_target_pairs={{0,1},{1,0},{2,3},{3,2},{4,5},{5,4},{6,7},{7,6},{8,9},{9,8},{10,11... | collective-permute-start | bytes 10616840 | tf_op jit(solution)/shard_map/ppermute | solution.py:178
  569.8 65.4 %attn_fwd.1 = (bf16[1024,1536]{1,0:T(8,128)(2,1)}, bf16[160,1536]{1,0:T(8,128)(2,1)}, f32[12,8,1280]{2,1,0:T(8,128)S(1)}) custom-call(s32[3]{0:T(128)S(1)} %pad_add_fusion.len_ref, bf16[1024,4608]{1,0:T(8,128)(2,1)} %add_convert_fusion.qi.ki.vi, bf16[1024,4608]{1,0:T(8,128)(2,1)} %add_convert_fusion.qi.ki.vi, bf16[1024,4608]{1,0:T(8,128)(2,1)} %add_convert_fusion.qi.ki.vi, ...), custom_call_target="tpu_custom_call" | custom-call | flops 17226006528 | bytes 14548992 | tf_op jit(solution)/shard_map/attn_fwd/pallas_call | solution.py:57
  656.9 25.0 %assemble.7 = (bf16[6144,1536]{1,0:T(8,128)(2,1)}, bf16[6144,1536]{1,0:T(8,128)(2,1)}) custom-call(bf16[2,1536,1536]{2,1,0:T(8,128)(2,1)} %refs_0_.7, bf16[3,2,384,768]{3,2,1,0:T(8,128)(2,1)S(1)} %pad_maximum_fusion.1.refs_1_, bf16[3,2,384,768]{3,2,1,0:T(8,128)(2,1)} %collective-permute-done.35.refs_2_, ...), custom_call_target="tpu_custom_call" | custom-call | bytes 75497472 | tf_op jit(solution)/shard_map/assemble/pallas_call | solution.py:255
  698.3 31.5 %assemble.6 = (bf16[1536,6144]{1,0:T(8,128)(2,1)}, bf16[1536,6144]{1,0:T(8,128)(2,1)}) custom-call(bf16[2,384,6144]{2,1,0:T(8,128)(2,1)} %refs_0_.6, bf16[3,2,96,3072]{3,2,1,0:T(8,128)(2,1)} %pad_maximum_fusion.refs_1_, bf16[3,2,96,3072]{3,2,1,0:T(8,128)(2,1)} %collective-permute-done.25.refs_2_, bf16[3,2,96,3072]{3,2,1,0:T(8,128)(2,1)} %collective-permute-done.26.refs_3_, ...), custom_call_target="tpu_custom_call" | custom-call | bytes 75497472 | tf_op jit(solution)/shard_map/assemble/pallas_call | solution.py:255
  763.4 25.4 %fusion.132 = f32[1024,6144]{1,0:T(8,128)} fusion(bf16[1024,1536]{1,0:T(8,128)(2,1)S(1)} %copy-done.2, bf16[1536,6144]{1,0:T(8,128)(2,1)} %get-tuple-element.30), kind=kOutput, calls=%fused_computation.348 | convolution fusion | flops 19327352832 | bytes 47185920 | tf_op jit(solution)/shard_map/dot_general | solution.py:153
  788.8 43.2 %convert_reduce_fusion = (f32[6144]{0:T(1024)}, bf16[1024,6144]{1,0:T(8,128)(2,1)}, bf16[1024,6144]{1,0:T(8,128)(2,1)}) fusion(f32[1024,6144]{1,0:T(8,128)} %fusion.132, f32[6144]{0:T(1024)S(1)} %bitcast.509, bf16[1024,1536]{1,0:T(8,128)(2,1)S(1)} %copy-done, bf16[6144,1536]{1,0:T(8,128)(2,1)} %get-tuple-element.31), kind=kOutput, calls=%fused_computation.9 | convolution fusion | flops 19484633088 | bytes 72400896 | tf_op jit(solution)/shard_map/dot_general | solution.py:14
  832.1 31.0 %multiply_reduce_fusion = (f32[1536]{0:T(1024)}, f32[1024]{0:T(1024)S(1)}, f32[1024]{0:T(1024)S(1)}, f32[1536]{0:T(1024)}, f32[1024,1536]{1,0:T(8,128)}) fusion(f32[1024,1536]{1,0:T(8,128)} %copy-done.33, f32[1024]{0:T(1024)S(1)} %copy-done.134, f32[1024]{0:T(1024)S(1)} %copy-done.113, f32[1536]{0:T(1024)S(1)} %copy-done.123, ...), kind=kOutput, calls=%fused_computation.39 | convolution fusion | flops 19341502464 | bytes 44075008 | tf_op jit(solution)/shard_map/dot_general | solution.py:14
  863.1 32.4 %fusion.22 = (f32[1536]{0:T(1024)S(1)}, bf16[1024,1536]{1,0:T(8,128)(2,1)}, f32[1536]{0:T(1024)}, bf16[1024,1536]{1,0:T(8,128)(2,1)S(1)}, f32[1024,1536]{1,0:T(8,128)}) fusion(f32[1536]{0:T(1024)S(1)} %copy-done.146, bf16[512,1536]{1,0:T(8,128)(2,1)} %copy-done.67, bf16[512,1536]{1,0:T(8,128)(2,1)S(1)} %copy-done.47, f32[1024,1536]{1,0:T(8,128)} %copy-done.33, ...), kind=kOutput, calls=%fused_computation.35 | convolution fusion | flops 19361951744 | bytes 59822080 | tf_op jit(solution)/shard_map/dot_general | solution.py:153
  905.6 145.5 %attn_bwd.1 = (bf16[1024,4608]{1,0:T(8,128)(2,1)}, bf16[160,4608]{1,0:T(8,128)(2,1)}) custom-call(s32[3]{0:T(128)} %copy-done.22, bf16[1024,4608]{1,0:T(8,128)(2,1)} %add_convert_fusion.qi.ki.vi, bf16[1024,4608]{1,0:T(8,128)(2,1)} %add_convert_fusion.qi.ki.vi, bf16[1024,4608]{1,0:T(8,128)(2,1)} %add_convert_fusion.qi.ki.vi, bf16[160,4608]{1,0:T(8,128)(2,1)} %copy-done.24, ...), custom_call_target="tpu_custom_call" | custom-call | flops 43065016320 | bytes 29097984 | tf_op jit(solution)/shard_map/attn_bwd/pallas_call | solution.py:126
  1051.1 23.2 %fusion.19 = (f32[1536]{0:T(1024)S(1)}, f32[1024]{0:T(1024)S(1)}, f32[1024]{0:T(1024)S(1)}, f32[1536]{0:T(1024)S(1)}, f32[1024,1536]{1,0:T(8,128)}) fusion(f32[1024]{0:T(1024)S(1)} %copy-done.111, f32[1024]{0:T(1024)S(1)} %copy-done.109, bf16[512,1536]{1,0:T(8,128)(2,1)S(1)} %copy-done.32, bf16[512,1536]{1,0:T(8,128)(2,1)S(1)} %copy-done.28, ...), kind=kOutput, calls=%fused_computation.32 | convolution fusion | flops 14515955712 | bytes 33064960 | tf_op jit(solution)/shard_map/dot_general | solution.py:14
  1171.3 57.5 %collective-permute-done.67 = bf16[768,768]{1,0:T(8,128)(2,1)} collective-permute-done((bf16[768,768]{1,0:T(8,128)(2,1)}, bf16[768,768]{1,0:T(8,128)(2,1)}, u32[]{:S(2)}, u32[]{:S(2)}) %collective-permute-start.67) | collective-permute-done | bytes 1179680 | tf_op jit(solution)/shard_map/ppermute | solution.py:170
  1259.0 38.8 %collective-permute-done.48 = f32[2,6,1536]{2,0,1:T(2,128)S(1)} collective-permute-done((f32[2,6,1536]{2,0,1:T(2,128)S(1)}, f32[2,6,1536]{2,0,1:T(2,128)S(1)}, u32[]{:S(2)}, u32[]{:S(2)}) %collective-permute-start.48) | collective-permute-done | bytes 73760 | tf_op jit(solution)/shard_map/ppermute | solution.py:170
  1370.7 188.8 %all-reduce = f32[32,288]{1,0:T(8,128)S(1)} all-reduce(f32[32,288]{1,0:T(8,128)S(1)} %reshape.2497), channel_id=3, replica_groups=mesh['seq'=2,'fsdp'=4,'dp'=4] {'seq','fsdp','dp'}, use_global_device_ids=true, to_apply=%region_30.31.clone | all-reduce | flops 9216 | bytes 73728
  1692.6 32.4 %collective-permute-done.94 = bf16[1,96,3072]{2,1,0:T(8,128)(2,1)S(1)} collective-permute-done((bf16[1,96,3072]{2,1,0:T(8,128)(2,1)S(1)}, bf16[1,96,3072]{2,1,0:T(8,128)(2,1)S(1)}, u32[]{:S(2)}, u32[]{:S(2)}) %collective-permute-start.94) | collective-permute-done | bytes 589856 | tf_op jit(solution)/shard_map/ppermute | solution.py:183
  1913.0 39.2 %collective-permute-done.83 = bf16[768,3072]{1,0:T(8,128)(2,1)} collective-permute-done((bf16[768,3072]{1,0:T(8,128)(2,1)}, bf16[768,3072]{1,0:T(8,128)(2,1)}, u32[]{:S(2)}, u32[]{:S(2)}) %collective-permute-start.83) | collective-permute-done | bytes 4718624 | tf_op jit(solution)/shard_map/ppermute | solution.py:170
  1963.6 89.7 %collective-permute-done.99 = bf16[3072,768]{1,0:T(8,128)(2,1)} collective-permute-done((bf16[3072,768]{1,0:T(8,128)(2,1)}, bf16[3072,768]{1,0:T(8,128)(2,1)}, u32[]{:S(2)}, u32[]{:S(2)}) %collective-permute-start.99) | collective-permute-done | bytes 4718624 | tf_op jit(solution)/shard_map/ppermute | solution.py:170
  2070.5 34.7 %collective-permute-done.100 = bf16[4,1,384,768]{3,2,1,0:T(8,128)(2,1)S(1)} collective-permute-done((bf16[4,1,384,768]{3,2,1,0:T(8,128)(2,1)S(1)}, bf16[4,1,384,768]{3,2,1,0:T(8,128)(2,1)S(1)}, u32[]{:S(2)}, u32[]{:S(2)}) %collective-permute-start.100) | collective-permute-done | bytes 2359328 | tf_op jit(solution)/shard_map/ppermute | solution.py:174
  2116.7 29.4 %collective-permute-done.87 = bf16[1,96,3072]{2,1,0:T(8,128)(2,1)S(1)} collective-permute-done((bf16[1,96,3072]{2,1,0:T(8,128)(2,1)S(1)}, bf16[1,96,3072]{2,1,0:T(8,128)(2,1)S(1)}, u32[]{:S(2)}, u32[]{:S(2)}) %collective-permute-start.87) | collective-permute-done | bytes 589856 | tf_op jit(solution)/shard_map/ppermute | solution.py:183
  (748 shorter events, 967.3 us)
Async XLA Ops:
  7.2 1553.0 %all-reduce.4.cloned.1.call-start = ((), (), s32[]{:S(2)}) async-start(), calls=%async_computation | async-start | bytes 163840
  259.3 140.4 %collective-permute-start.35 = (bf16[3,2,384,768]{3,2,1,0:T(8,128)(2,1)S(1)}, bf16[3,2,384,768]{3,2,1,0:T(8,128)(2,1)}, u32[]{:S(2)}, u32[]{:S(2)}) collective-permute-start(bf16[3,2,384,768]{3,2,1,0:T(8,128)(2,1)S(1)} %pad_maximum_fusion.1.refs_1_), channel_id=1, source_target_pairs={{0,2},{1,3},{2,0},{3,1},{4,6},{5,7},{6,4},{7,5},{8,10},{9,11},{10,... | collective-permute-start | bytes 10616840 | tf_op jit(solution)/shard_map/ppermute | solution.py:174
  273.3 126.7 %collective-permute-start.9 = (bf16[3,2,96,2304]{3,2,1,0:T(8,128)(2,1)}, bf16[3,2,96,2304]{3,2,1,0:T(8,128)(2,1)}, u32[]{:S(2)}, u32[]{:S(2)}) collective-permute-start(bf16[3,2,96,2304]{3,2,1,0:T(8,128)(2,1)} %collective-permute-done.5.refs_3_), channel_id=1, source_target_pairs={{0,1},{1,0},{2,3},{3,2},{4,5},{5,4},{6,7},{7,6},{8,9},{9,8},{10,11... | collective-permute-start | bytes 7962632 | tf_op jit(solution)/shard_map/ppermute | solution.py:178
  360.3 120.3 %collective-permute-start.26 = (bf16[3,2,96,3072]{3,2,1,0:T(8,128)(2,1)}, bf16[3,2,96,3072]{3,2,1,0:T(8,128)(2,1)}, u32[]{:S(2)}, u32[]{:S(2)}) collective-permute-start(bf16[3,2,96,3072]{3,2,1,0:T(8,128)(2,1)} %pad_maximum_fusion.refs_1_), channel_id=1, source_target_pairs={{0,2},{1,3},{2,0},{3,1},{4,6},{5,7},{6,4},{7,5},{8,10},{9,11},{10,... | collective-permute-start | bytes 10616840 | tf_op jit(solution)/shard_map/ppermute | solution.py:174
  400.0 139.3 %collective-permute-start.36 = (bf16[3,2,384,768]{3,2,1,0:T(8,128)(2,1)S(1)}, bf16[3,2,384,768]{3,2,1,0:T(8,128)(2,1)}, u32[]{:S(2)}, u32[]{:S(2)}) collective-permute-start(bf16[3,2,384,768]{3,2,1,0:T(8,128)(2,1)S(1)} %pad_maximum_fusion.1.refs_1_), channel_id=1, source_target_pairs={{0,16},{16,0},{1,17},{17,1},{2,18},{18,2},{3,19},{19,3},{4,20},{20... | collective-permute-start | bytes 10616840 | tf_op jit(solution)/shard_map/ppermute | solution.py:170
  412.4 237.1 %collective-permute-start.38 = (bf16[3,2,384,768]{3,2,1,0:T(8,128)(2,1)S(1)}, bf16[3,2,384,768]{3,2,1,0:T(8,128)(2,1)}, u32[]{:S(2)}, u32[]{:S(2)}) collective-permute-start(bf16[3,2,384,768]{3,2,1,0:T(8,128)(2,1)S(1)} %pad_maximum_fusion.1.refs_1_), channel_id=1, source_target_pairs={{0,1},{1,0},{2,3},{3,2},{4,5},{5,4},{6,7},{7,6},{8,9},{9,8},{10,11... | collective-permute-start | bytes 10616840 | tf_op jit(solution)/shard_map/ppermute | solution.py:178
  427.5 211.2 %collective-permute-start.37 = (bf16[3,2,384,768]{3,2,1,0:T(8,128)(2,1)}, bf16[3,2,384,768]{3,2,1,0:T(8,128)(2,1)}, u32[]{:S(2)}, u32[]{:S(2)}) collective-permute-start(bf16[3,2,384,768]{3,2,1,0:T(8,128)(2,1)} %collective-permute-done.35.refs_2_), channel_id=1, source_target_pairs={{0,16},{16,0},{1,17},{17,1},{2,18},{18,2},{3,19},{19,3},{4,20},{20... | collective-permute-start | bytes 10616840 | tf_op jit(solution)/shard_map/ppermute | solution.py:170
  480.6 170.0 %collective-permute-start.39 = (bf16[3,2,384,768]{3,2,1,0:T(8,128)(2,1)}, bf16[3,2,384,768]{3,2,1,0:T(8,128)(2,1)}, u32[]{:S(2)}, u32[]{:S(2)}) collective-permute-start(bf16[3,2,384,768]{3,2,1,0:T(8,128)(2,1)} %collective-permute-done.35.refs_2_), channel_id=1, source_target_pairs={{0,1},{1,0},{2,3},{3,2},{4,5},{5,4},{6,7},{7,6},{8,9},{9,8},{10,11... | collective-permute-start | bytes 10616840 | tf_op jit(solution)/shard_map/ppermute | solution.py:178
  482.9 167.1 %collective-permute-start.27 = (bf16[3,2,96,3072]{3,2,1,0:T(8,128)(2,1)}, bf16[3,2,96,3072]{3,2,1,0:T(8,128)(2,1)}, u32[]{:S(2)}, u32[]{:S(2)}) collective-permute-start(bf16[3,2,96,3072]{3,2,1,0:T(8,128)(2,1)} %collective-permute-done.25.refs_2_), channel_id=1, source_target_pairs={{0,2},{1,3},{2,0},{3,1},{4,6},{5,7},{6,4},{7,5},{8,10},{9,11},{10,... | collective-permute-start | bytes 10616840 | tf_op jit(solution)/shard_map/ppermute | solution.py:174
  655.2 445.1 %collective-permute-start.57 = (bf16[160,1536]{1,0:T(8,128)(2,1)}, bf16[160,1536]{1,0:T(8,128)(2,1)}, u32[]{:S(2)}, u32[]{:S(2)}) collective-permute-start(bf16[160,1536]{1,0:T(8,128)(2,1)} %get-tuple-element.203.a0), channel_id=1, source_target_pairs={{0,1},{1,0},{2,3},{3,2},{4,5},{5,4},{6,7},{7,6},{8,9},{9,8},{10,11... | collective-permute-start | bytes 1474568 | tf_op jit(solution)/shard_map/ppermute | solution.py:178
  696.6 448.2 %collective-permute-start.49 = (bf16[1024,1536]{1,0:T(8,128)(2,1)}, bf16[1024,1536]{1,0:T(8,128)(2,1)}, u32[]{:S(2)}, u32[]{:S(2)}) collective-permute-start(bf16[1024,1536]{1,0:T(8,128)(2,1)} %fusion.14.a0), channel_id=1, source_target_pairs={{0,1},{1,0},{2,3},{3,2},{4,5},{5,4},{6,7},{7,6},{8,9},{9,8},{10,11... | collective-permute-start | bytes 9437192 | tf_op jit(solution)/shard_map/ppermute | solution.py:178
  697.8 387.6 %collective-permute-start.73 = (bf16[160,1536]{1,0:T(8,128)(2,1)}, bf16[160,1536]{1,0:T(8,128)(2,1)}, u32[]{:S(2)}, u32[]{:S(2)}) collective-permute-start(bf16[160,1536]{1,0:T(8,128)(2,1)} %get-tuple-element.32.ot.a0), channel_id=1, source_target_pairs={{0,1},{1,0},{2,3},{3,2},{4,5},{5,4},{6,7},{7,6},{8,9},{9,8},{10,11... | collective-permute-start | bytes 1474568 | tf_op jit(solution)/shard_map/ppermute | solution.py:178
  697.9 420.1 %collective-permute-start.65 = (bf16[1024,1536]{1,0:T(8,128)(2,1)}, bf16[1024,1536]{1,0:T(8,128)(2,1)}, u32[]{:S(2)}, u32[]{:S(2)}) collective-permute-start(bf16[1024,1536]{1,0:T(8,128)(2,1)} %get-tuple-element.28.oi.a0), channel_id=1, source_target_pairs={{0,1},{1,0},{2,3},{3,2},{4,5},{5,4},{6,7},{7,6},{8,9},{9,8},{10,11... | collective-permute-start | bytes 9437192 | tf_op jit(solution)/shard_map/ppermute | solution.py:178
  763.0 322.4 %collective-permute-start.74 = (bf16[160,1536]{1,0:T(8,128)(2,1)}, bf16[160,1536]{1,0:T(8,128)(2,1)}, u32[]{:S(2)}, u32[]{:S(2)}) collective-permute-start(bf16[160,1536]{1,0:T(8,128)(2,1)} %get-tuple-element.119.b0), channel_id=1, source_target_pairs={{0,1},{1,0},{2,3},{3,2},{4,5},{5,4},{6,7},{7,6},{8,9},{9,8},{10,11... | collective-permute-start | bytes 1474568 | tf_op jit(solution)/shard_map/ppermute | solution.py:178
  1117.6 196.7 %collective-permute-start.59 = (bf16[768,2304]{1,0:T(8,128)(2,1)}, bf16[768,2304]{1,0:T(8,128)(2,1)}, u32[]{:S(2)}, u32[]{:S(2)}) collective-permute-start(bf16[768,2304]{1,0:T(8,128)(2,1)} %wgrad.19), channel_id=1, source_target_pairs={{0,16},{16,0},{1,17},{17,1},{2,18},{18,2},{3,19},{19,3},{4,20},{20... | collective-permute-start | bytes 10616840 | tf_op jit(solution)/shard_map/ppermute | solution.py:170
  1162.5 155.9 %collective-permute-start.46 = (bf16[512,1536]{1,0:T(8,128)(2,1)}, bf16[512,1536]{1,0:T(8,128)(2,1)}, u32[]{:S(2)}, u32[]{:S(2)}) collective-permute-start(bf16[512,1536]{1,0:T(8,128)(2,1)} %slice.245), channel_id=1, source_target_pairs={{0,16},{16,0},{1,17},{17,1},{2,18},{18,2},{3,19},{19,3},{4,20},{20... | collective-permute-start | bytes 4718600 | tf_op jit(solution)/shard_map/ppermute | solution.py:170
  1162.8 158.0 %collective-permute-start.42 = (bf16[512,1536]{1,0:T(8,128)(2,1)}, bf16[512,1536]{1,0:T(8,128)(2,1)}, u32[]{:S(2)}, u32[]{:S(2)}) collective-permute-start(bf16[512,1536]{1,0:T(8,128)(2,1)} %get-tuple-element.157), channel_id=1, source_target_pairs={{0,16},{16,0},{1,17},{17,1},{2,18},{18,2},{3,19},{19,3},{4,20},{20... | collective-permute-start | bytes 4718600 | tf_op jit(solution)/shard_map/ppermute | solution.py:170
  1318.4 372.7 %collective-permute-start.50 = (bf16[1024,4608]{1,0:T(8,128)(2,1)}, bf16[1024,4608]{1,0:T(8,128)(2,1)}, u32[]{:S(2)}, u32[]{:S(2)}) collective-permute-start(bf16[1024,4608]{1,0:T(8,128)(2,1)} %get-tuple-element.37.b0), channel_id=1, source_target_pairs={{0,1},{1,0},{2,3},{3,2},{4,5},{5,4},{6,7},{7,6},{8,9},{9,8},{10,11... | collective-permute-start | bytes 28311560 | tf_op jit(solution)/shard_map/ppermute | solution.py:178
  1320.7 251.7 %collective-permute-start.91 = (bf16[768,3072]{1,0:T(8,128)(2,1)}, bf16[768,3072]{1,0:T(8,128)(2,1)}, u32[]{:S(2)}, u32[]{:S(2)}) collective-permute-start(bf16[768,3072]{1,0:T(8,128)(2,1)} %wgrad.27), channel_id=1, source_target_pairs={{0,16},{16,0},{1,17},{17,1},{2,18},{18,2},{3,19},{19,3},{4,20},{20... | collective-permute-start | bytes 14155784 | tf_op jit(solution)/shard_map/ppermute | solution.py:170
  1321.7 251.1 %collective-permute-start.107 = (bf16[3072,768]{1,0:T(8,128)(2,1)}, bf16[3072,768]{1,0:T(8,128)(2,1)}, u32[]{:S(2)}, u32[]{:S(2)}) collective-permute-start(bf16[3072,768]{1,0:T(8,128)(2,1)} %wgrad.31), channel_id=1, source_target_pairs={{0,16},{16,0},{1,17},{17,1},{2,18},{18,2},{3,19},{19,3},{4,20},{20... | collective-permute-start | bytes 14155784 | tf_op jit(solution)/shard_map/ppermute | solution.py:170
  1345.6 452.0 %collective-permute-start.82 = (bf16[1024,6144]{1,0:T(8,128)(2,1)}, bf16[1024,6144]{1,0:T(8,128)(2,1)}, u32[]{:S(2)}, u32[]{:S(2)}) collective-permute-start(bf16[1024,6144]{1,0:T(8,128)(2,1)} %get-tuple-element.122.b0), channel_id=1, source_target_pairs={{0,1},{1,0},{2,3},{3,2},{4,5},{5,4},{6,7},{7,6},{8,9},{9,8},{10,11... | collective-permute-start | bytes 37748744 | tf_op jit(solution)/shard_map/ppermute | solution.py:178
  1365.5 447.5 %collective-permute-start.97 = (bf16[1024,6144]{1,0:T(8,128)(2,1)}, bf16[1024,6144]{1,0:T(8,128)(2,1)}, u32[]{:S(2)}, u32[]{:S(2)}) collective-permute-start(bf16[1024,6144]{1,0:T(8,128)(2,1)} %get-tuple-element.133.a0), channel_id=1, source_target_pairs={{0,1},{1,0},{2,3},{3,2},{4,5},{5,4},{6,7},{7,6},{8,9},{9,8},{10,11... | collective-permute-start | bytes 37748744 | tf_op jit(solution)/shard_map/ppermute | solution.py:178
  1812.3 139.9 %collective-permute-start.83 = (bf16[768,3072]{1,0:T(8,128)(2,1)}, bf16[768,3072]{1,0:T(8,128)(2,1)}, u32[]{:S(2)}, u32[]{:S(2)}) collective-permute-start(bf16[768,3072]{1,0:T(8,128)(2,1)} %wgrad.25), channel_id=1, source_target_pairs={{0,16},{16,0},{1,17},{17,1},{2,18},{18,2},{3,19},{19,3},{4,20},{20... | collective-permute-start | bytes 14155784 | tf_op jit(solution)/shard_map/ppermute | solution.py:170
  1829.4 223.9 %collective-permute-start.99 = (bf16[3072,768]{1,0:T(8,128)(2,1)}, bf16[3072,768]{1,0:T(8,128)(2,1)}, u32[]{:S(2)}, u32[]{:S(2)}) collective-permute-start(bf16[3072,768]{1,0:T(8,128)(2,1)} %wgrad.29), channel_id=1, source_target_pairs={{0,16},{16,0},{1,17},{17,1},{2,18},{18,2},{3,19},{19,3},{4,20},{20... | collective-permute-start | bytes 14155784 | tf_op jit(solution)/shard_map/ppermute | solution.py:170
  (253 other events, 11362.7 us)
Sparse Core Ops, SparseCore 0:
  1350.2 139.5 all-reduce.3

commit v2 on v1

v2 whole, which is shorter than its diff:
```python
import functools

import jax
import jax.numpy as jnp
from jax import lax
from jax.experimental import pallas as pl
from jax.experimental.pallas import tpu as pltpu
from jax.sharding import Mesh, PartitionSpec as P

EPSILON = 1e-06
HEAD_DIM=64
MASKED=-1000000000.0
def dot(a,b,ca,cb):
    return lax.dot_general(a,b,(((ca,),(cb,)),((),())),preferred_element_type=jnp.float32)

def attn_fwd_kernel(ti,tt,tq,len_ref,qi,ki,vi,qt,kt,vt,oi,ot,lse,ktp,vtp):
    tp=ktp.shape[0]
    ktp[...]=jnp.zeros_like(ktp); vtp[...]=jnp.zeros_like(vtp)
    ktp[:tt,:]=kt[...]; vtp[:tt,:]=vt[...]
    n_len=len_ref[0]; half=len_ref[1]; mine=len_ref[2]
    r=lax.broadcasted_iota(jnp.int32,(1,tp),1)
    pos=jnp.where(r<half,mine*half+r,(1-mine)*half+r-half)
    valid=(r<2*half)&(pos<n_len)
    lane=lax.broadcasted_iota(jnp.int32,(1,2*HEAD_DIM),1)
    k_img=ki[...]; v_img=vi[...]; k_txt=ktp[...]; v_txt=vtp[...]
    def one(q,rows):
        outs=[];lses=[]
        for h in range(2):
            qh=jnp.where((lane<HEAD_DIM)==(h==0),q.astype(jnp.float32)*(HEAD_DIM**-0.5),0.0).astype(jnp.bfloat16)
            s1=dot(qh,k_img,1,1); s2=dot(qh,k_txt,1,1)
            s2=jnp.where(valid,s2,MASKED)
            m=jnp.maximum(jnp.max(s1,axis=1,keepdims=True),jnp.max(s2,axis=1,keepdims=True))
            e1=jnp.exp(s1-m); e2=jnp.exp(s2-m)
            l=jnp.sum(e1,axis=1,keepdims=True)+jnp.sum(e2,axis=1,keepdims=True)
            inv=1.0/l
            o=dot((e1*inv).astype(jnp.bfloat16),v_img,1,0)+dot((e2*inv).astype(jnp.bfloat16),v_txt,1,0)
            outs.append(o); lses.append(m+jnp.log(l))
        o=jnp.where(lane<HEAD_DIM,outs[0],outs[1]).astype(jnp.bfloat16)
        both=jnp.where(lane<HEAD_DIM,jnp.broadcast_to(lses[0],(rows,128)),jnp.broadcast_to(lses[1],(rows,128)))
        return o,both.T
    def step(i,_):
        start=pl.multiple_of(i*tq,tq)
        o,b=one(qi[pl.ds(start,tq),:],tq)
        oi[pl.ds(start,tq),:]=o
        lse[0,0:1,pl.ds(start,tq)]=b[0:1]; lse[0,1:2,pl.ds(start,tq)]=b[64:65]
        return 0
    lax.fori_loop(0,ti//tq,step,0)
    qpad=jnp.concatenate([qt[...],jnp.zeros((tp-tt,128),jnp.bfloat16)],axis=0)
    o,b=one(qpad,tp)
    ot[...]=o[:tt]
    lse[0,0:1,ti:ti+tp]=b[0:1]; lse[0,1:2,ti:ti+tp]=b[64:65]

def attn_fwd(qkv_i,qkv_t,info,tq=256):
    ti,w3=qkv_i.shape; tt=qkv_t.shape[0]; w=w3//3; n=w//128; tp=256
    bi=lambda off: pl.BlockSpec((ti,128),lambda p,s,off=off:(0,p+off*n))
    bt=lambda off: pl.BlockSpec((tt,128),lambda p,s,off=off:(0,p+off*n))
    return pl.pallas_call(functools.partial(attn_fwd_kernel,ti,tt,tq),
        grid_spec=pltpu.PrefetchScalarGridSpec(num_scalar_prefetch=1,grid=(n,),
            in_specs=[bi(0),bi(1),bi(2),bt(0),bt(1),bt(2)],
            out_specs=[bi(0),bt(0),pl.BlockSpec((1,8,ti+tp),lambda p,s:(p,0,0))],
            scratch_shapes=[pltpu.VMEM((tp,128),jnp.bfloat16)]*2),
        out_shape=[jax.ShapeDtypeStruct((ti,w),jnp.bfloat16),jax.ShapeDtypeStruct((tt,w),jnp.bfloat16),
                   jax.ShapeDtypeStruct((n,8,ti+tp),jnp.float32)],
        compiler_params=pltpu.CompilerParams(vmem_limit_bytes=48<<20),
        cost_estimate=pl.CostEstimate(flops=8*(ti+tt)*(ti+tt)*w,bytes_accessed=8*(ti+tt)*w,transcendentals=2*n*(ti+tt)*(ti+tt)),
        name="attn_fwd")(info,qkv_i,qkv_i,qkv_i,qkv_t,qkv_t,qkv_t)

def attn_bwd_kernel(ti,tt,tq,len_ref,qi,ki,vi,qt,kt,vt,oi,ot,di,dt,lse,outi,outt,ktp,vtp,dk1,dk2,dv1,dv2,dqi,dqt):
    j=pl.program_id(1)
    tp=ktp.shape[0]
    @pl.when(j==0)
    def _():
        ktp[...]=jnp.zeros_like(ktp); vtp[...]=jnp.zeros_like(vtp)
        ktp[:tt,:]=kt[...]; vtp[:tt,:]=vt[...]
        n_len=len_ref[0]; half=len_ref[1]; mine=len_ref[2]
        r=lax.broadcasted_iota(jnp.int32,(tp,1),0)
        pos=jnp.where(r<half,mine*half+r,(1-mine)*half+r-half)
        valid=(r<2*half)&(pos<n_len)
        lane=lax.broadcasted_iota(jnp.int32,(1,128),1)
        sub=lax.broadcasted_iota(jnp.int32,(8,128),0); lane8=lax.broadcasted_iota(jnp.int32,(8,128),1)
        sel=jnp.where((lane8//HEAD_DIM)==sub,1.0,0.0).astype(jnp.bfloat16)
        k_img=ki[...]; v_img=vi[...]; k_txt=ktp[...]; v_txt=vtp[...]
        for ref in (dk1,dk2,dv1,dv2): ref[...]=jnp.zeros_like(ref)
        def one(q,do,o,ls):
            prod=do.astype(jnp.float32)*o.astype(jnp.float32)
            hi=prod.astype(jnp.bfloat16); lo=(prod-hi.astype(jnp.float32)).astype(jnp.bfloat16)
            dsum=dot(sel,hi,1,1)+dot(sel,lo,1,1)
            qs=(q.astype(jnp.float32)*(HEAD_DIM**-0.5))
            dof=do.astype(jnp.float32)
            dqs=[]
            for h in range(2):
                mk=(lane<HEAD_DIM)==(h==0)
                qh=jnp.where(mk,qs,0.0).astype(jnp.bfloat16)
                dh=jnp.where(mk,dof,0.0).astype(jnp.bfloat16)
                L=ls[h:h+1]; D=dsum[h:h+1]
                s1=dot(k_img,qh,1,1); s2=dot(k_txt,qh,1,1)
                p1=jnp.exp(s1-L); p2=jnp.where(valid,jnp.exp(s2-L),0.0)
                dp1=dot(v_img,dh,1,1); dp2=dot(v_txt,dh,1,1)
                ds1=(p1*(dp1-D)).astype(jnp.bfloat16); ds2=(p2*(dp2-D)).astype(jnp.bfloat16)
                dv1[...]+=dot(p1.astype(jnp.bfloat16),dh,1,0)
                dv2[...]+=dot(p2.astype(jnp.bfloat16),dh,1,0)
                dk1[...]+=dot(ds1,qh,1,0)
                dk2[...]+=dot(ds2,qh,1,0)
                dqs.append(dot(ds1,k_img,0,0)+dot(ds2,k_txt,0,0))
            return (jnp.where(lane<HEAD_DIM,dqs[0],dqs[1])*(HEAD_DIM**-0.5)).astype(jnp.bfloat16)
        def step(i,_):
            start=pl.multiple_of(i*tq,tq)
            sl=pl.ds(start,tq)
            dqi[sl,:]=one(qi[sl,:],di[sl,:],oi[sl,:],lse[0,:,sl])
            return 0
        lax.fori_loop(0,ti//tq,step,0)
        pad=lambda a: jnp.concatenate([a,jnp.zeros((tp-tt,128),jnp.bfloat16)],axis=0)
        dqt[...]=one(pad(qt[...]),pad(dt[...]),pad(ot[...]),lse[0,:,ti:ti+tp])[:tt]
        outi[...]=dqi[...]; outt[...]=dqt[...]
    @pl.when(j==1)
    def _():
        outi[...]=dk1[...].astype(jnp.bfloat16); outt[...]=dk2[:tt,:].astype(jnp.bfloat16)
    @pl.when(j==2)
    def _():
        outi[...]=dv1[...].astype(jnp.bfloat16); outt[...]=dv2[:tt,:].astype(jnp.bfloat16)

def attn_bwd(qkv_i,qkv_t,o_i,o_t,d_i,d_t,lse,info,tq=256):
    ti,w3=qkv_i.shape; tt=qkv_t.shape[0]; w=w3//3; n=w//128; tp=256
    bi=lambda off: pl.BlockSpec((ti,128),lambda p,j,s,off=off:(0,p+off*n))
    bt=lambda off: pl.BlockSpec((tt,128),lambda p,j,s,off=off:(0,p+off*n))
    return pl.pallas_call(functools.partial(attn_bwd_kernel,ti,tt,tq),
        grid_spec=pltpu.PrefetchScalarGridSpec(num_scalar_prefetch=1,grid=(n,3),
            in_specs=[bi(0),bi(1),bi(2),bt(0),bt(1),bt(2),bi(0),bt(0),bi(0),bt(0),pl.BlockSpec((1,8,ti+tp),lambda p,j,s:(p,0,0))],
            out_specs=[pl.BlockSpec((ti,128),lambda p,j,s:(0,p+j*n)),pl.BlockSpec((tt,128),lambda p,j,s:(0,p+j*n))],
            scratch_shapes=[pltpu.VMEM((tp,128),jnp.bfloat16)]*2+[pltpu.VMEM((ti,128),jnp.float32),pltpu.VMEM((tp,128),jnp.float32)]*2
              +[pltpu.VMEM((ti,128),jnp.bfloat16),pltpu.VMEM((tt,128),jnp.bfloat16)]),
        out_shape=[jax.ShapeDtypeStruct((ti,w3),jnp.bfloat16),jax.ShapeDtypeStruct((tt,w3),jnp.bfloat16)],
        compiler_params=pltpu.CompilerParams(vmem_limit_bytes=56<<20),
        cost_estimate=pl.CostEstimate(flops=20*(ti+tt)*(ti+tt)*w,bytes_accessed=16*(ti+tt)*w,transcendentals=2*n*(ti+tt)*(ti+tt)),
        name="attn_bwd")(info,qkv_i,qkv_i,qkv_i,qkv_t,qkv_t,qkv_t,o_i,o_t,d_i,d_t,lse)


def normalize(values):
    row_mean = jnp.mean(values, axis=-1, keepdims=True)
    centred = values - row_mean
    variance = jnp.mean(centred * centred, axis=-1, keepdims=True)
    inverse = lax.rsqrt(variance + EPSILON)
    return (centred * inverse, inverse)


def normalize_back(normed, inverse, upstream):
    mean_one = jnp.mean(upstream, axis=-1, keepdims=True)
    mean_two = jnp.mean(upstream * normed, axis=-1, keepdims=True)
    return inverse * (upstream - mean_one - normed * mean_two)


def linear(values, weight, offset):
    return jnp.dot(values, weight, preferred_element_type=jnp.float32) + offset.astype(jnp.float32)


def linear_back(upstream, weight):
    return dot(upstream, weight, 1, 1)


def gelu_tanh(values):
    return jax.nn.gelu(values, approximate=True)


DP = ("y", "core")


def coords():
    dp = lax.axis_index(DP)
    return lax.axis_index("seq"), lax.axis_index("fsdp"), dp // 4, (dp // 2) % 2, dp % 2


def flip_x(a):
    return lax.ppermute(a, "seq", [(0, 1), (1, 0)])


def flip_y(a):
    return lax.ppermute(a, DP, [(i, i ^ 2) for i in range(lax.axis_size(DP))])


def flip_core(a):
    return lax.ppermute(a, DP, [(i, i ^ 1) for i in range(lax.axis_size(DP))])


def shift_z(a, k):
    n = lax.axis_size("fsdp")
    return lax.ppermute(a, "fsdp", [(i, (i + k) % n) for i in range(n)])


def shift_group(a, k):
    n = lax.axis_size(DP)
    return lax.ppermute(a, DP, [(i, (i + 4 * k) % n) for i in range(n)])


def after(value, *earlier):
    return lax.optimization_barrier((value, *earlier))[0]


def enter(z_too=True, y_too=True, core_too=True):
    fs = lax.axis_size("fsdp")
    x, z, _, y, c = coords()
    targets = [{"seq": 1 - x}]
    if y_too:
        targets.append({"y": lax.axis_index("y") + 1 - 2 * y})
    if core_too:
        targets.append({"core": 1 - c})
    if z_too:
        targets += [{"fsdp": lax.rem(z + k, fs)} for k in range(1, fs)]
    barrier = pltpu.get_barrier_semaphore()
    for target in targets:
        pl.semaphore_signal(barrier, inc=1, device_id=target, device_id_type=pl.DeviceIdType.MESH)
    pl.semaphore_wait(barrier, len(targets))


def swap_copies(srcs, dsts, sems):
    x = lax.axis_index("seq")
    return [
        pltpu.make_async_remote_copy(
            src_ref=src,
            dst_ref=dst,
            send_sem=sems.at[i, 0],
            recv_sem=sems.at[i, 1],
            device_id={"seq": 1 - x},
            device_id_type=pl.DeviceIdType.MESH,
        )
        for i, (src, dst) in enumerate(zip(srcs, dsts))
    ]


def gather_weights(units, swaps, collective_id):
    fs = lax.axis_size("fsdp")
    count = len(units)
    kinds = ("first", "second", "core0", "forward", "core1", "core2", "core3")

    def kernel(*refs):
        n = count + len(swaps)
        shards, near, outs, far = refs[:count], refs[count:n], refs[n : n + count], refs[n + count : 2 * n]
        bufs = refs[2 * n : 2 * n + count]
        local_sem, send_sem, recv_sem, swap_sem = refs[2 * n + count :]
        x, z, _, y, c = coords()
        y_full = lax.axis_index("y")
        to_x, to_y, to_core = {"seq": 1 - x}, {"y": y_full + 1 - 2 * y}, {"core": 1 - c}
        enter()
        swapped = swap_copies(near, far, swap_sem)
        for cp in swapped:
            cp.start()

        def remote(src, dst, u, slot, target):
            return pltpu.make_async_remote_copy(
                src_ref=src,
                dst_ref=dst,
                send_sem=send_sem.at[u, slot],
                recv_sem=recv_sem.at[u, slot],
                device_id=target,
                device_id_type=pl.DeviceIdType.MESH,
            )

        def spot(u, from_z, dx, dy, cc):
            _, r, cols = units[u][0].shape
            q, h = r // 4, cols // 2
            xx = 1 - x if dx else x
            yy = 1 - y if dy else y
            row = pl.multiple_of(from_z * r + (xx * 2 + yy) * q, 16)
            return outs[u].at[pl.ds(row, q), pl.ds(pl.multiple_of(cc * h, 128), h)]

        def copy(u, kind, k):
            _, r, cols = units[u][0].shape
            q, h = r // 4, cols // 2
            if kind == "z":
                row = pl.multiple_of((x * 2 + y) * q, 16)
                src = shards[u].at[units[u][1], pl.ds(row, q), pl.ds(pl.multiple_of(c * h, 128), h)]
                return remote(src, spot(u, z, 0, 0, c), u, k - 1, {"fsdp": lax.rem(z + k, fs)})
            x_first = units[u][2]
            slot = (1 + kinds.index(kind)) * (fs - 1) + k - 1
            via = (1, 0) if x_first else (0, 1)
            other = (0, 1) if x_first else (1, 0)
            where, target = {
                "first": ((0, 0), to_x if x_first else to_y),
                "second": ((0, 0), to_y if x_first else to_x),
                "core0": ((0, 0), to_core),
                "forward": (via, to_y if x_first else to_x),
                "core1": (via, to_core),
                "core2": (other, to_core),
                "core3": ((1, 1), to_core),
            }[kind]
            place = spot(u, lax.rem(z - k + fs, fs), *where, c)
            return remote(place, place, u, slot, target)

        for u in range(count):
            pltpu.make_async_copy(shards[u].at[units[u][1]], bufs[u], local_sem.at[u, 0]).start()
            for k in range(1, fs):
                copy(u, "z", k).start()

        def own(u):
            r = units[u][0].shape[1]
            return pltpu.make_async_copy(
                bufs[u], outs[u].at[pl.ds(pl.multiple_of(z * r, 16), r), :], local_sem.at[u, 1]
            )

        for u in range(count):
            pltpu.make_async_copy(shards[u].at[units[u][1]], bufs[u], local_sem.at[u, 0]).wait()
            own(u).start()
        for t in range(count + 2):
            for u, arrived, send in (
                (t, "z", ("first", "second", "core0")),
                (t - 1, "first", ("forward", "core1")),
                (t - 2, "second", ("core2",)),
                (t - 2, "forward", ("core3",)),
            ):
                if not 0 <= u < count:
                    continue
                for k in range(1, fs):
                    copy(u, arrived, k).wait_recv()
                    for kind in send:
                        copy(u, kind, k).start()
        for u in range(count):
            for k in range(1, fs):
                for kind in ("core0", "core1", "core2", "core3"):
                    copy(u, kind, k).wait_recv()
                for kind in ("z",) + kinds:
                    copy(u, kind, k).wait_send()
            own(u).wait()
        for cp in swapped:
            cp.wait()

    total = sum(2 * u[0].shape[1] * fs * u[0].shape[2] for u in units)
    results = pl.pallas_call(
        kernel,
        out_shape=[jax.ShapeDtypeStruct((u[0].shape[1] * fs, u[0].shape[2]), u[0].dtype) for u in units]
        + [jax.ShapeDtypeStruct(a.shape, a.dtype) for a in swaps],
        in_specs=[pl.BlockSpec(memory_space=pl.ANY)] * (count + len(swaps)),
        out_specs=[pl.BlockSpec(memory_space=pl.ANY)] * (count + len(swaps)),
        scratch_shapes=[pltpu.VMEM(u[0].shape[1:], u[0].dtype) for u in units]
        + [
            pltpu.SemaphoreType.DMA((count, 2)),
            pltpu.SemaphoreType.DMA((count, 8 * (fs - 1))),
            pltpu.SemaphoreType.DMA((count, 8 * (fs - 1))),
            pltpu.SemaphoreType.DMA((max(len(swaps), 1), 2)),
        ],
        compiler_params=pltpu.CompilerParams(
            collective_id=collective_id, has_side_effects=True, vmem_limit_bytes=48 << 20
        ),
        cost_estimate=pl.CostEstimate(flops=0, bytes_accessed=8 * total, transcendentals=0),
        name="gather_weights",
    )(*[u[0] for u in units], *swaps)
    return results[:count], results[count:]


def reduce_weights(partials, units, swaps, collective_id):
    fs, groups = lax.axis_size("fsdp"), lax.axis_size(DP) // 4
    arrays = [p.reshape(2, fs, groups, 2, -1, p.shape[1]) for p in partials]
    count, held = len(units), len(arrays)

    def kernel(*refs):
        n = held + len(swaps)
        ins, near, outs, far = refs[:held], refs[held:n], refs[n : n + held], refs[n + held : 2 * n]
        scratch = refs[2 * n : 2 * n + 6 * count]
        load_sem, send_sem, recv_sem, swap_sem = refs[2 * n + 6 * count :]
        x, z, _, y, _ = coords()
        to_x, to_y = {"seq": 1 - x}, {"y": lax.axis_index("y") + 1 - 2 * y}
        enter(core_too=False)
        f32 = lambda a: a.astype(jnp.float32)

        def remote(u, slot, src, dst, target):
            return pltpu.make_async_remote_copy(
                src_ref=src,
                dst_ref=dst,
                send_sem=send_sem.at[u, slot],
                recv_sem=recv_sem.at[u, slot],
                device_id=target,
                device_id_type=pl.DeviceIdType.MESH,
            )

        def rows(u, k, mine):
            index, x_first, start, width = units[u]
            zz = lax.rem(z + k, fs)
            cols = pl.ds(start, width)
            if x_first:
                return ins[index].at[x if mine else 1 - x, zz, :, :, :, cols]
            return ins[index].at[:, zz, :, y if mine else 1 - y, :, cols]

        def load(u, k):
            return pltpu.make_async_copy(rows(u, k, True), scratch[6 * u].at[k - 1], load_sem.at[u, k - 1])

        def hop(u, stage, k):
            part, recv_one, send_two, recv_two, send_three, recv_three = scratch[6 * u : 6 * u + 6]
            x_first = units[u][1]
            if stage == 1:
                return remote(u, k - 1, rows(u, k, False), recv_one.at[k - 1], to_x if x_first else to_y)
            if stage == 2:
                return remote(u, fs + k - 1, send_two.at[k - 1], recv_two.at[k - 1], to_y if x_first else to_x)
            return remote(
                u, 2 * fs + k - 1, send_three.at[k - 1], recv_three.at[k - 1], {"fsdp": lax.rem(z + k, fs)}
            )

        def side(u, ref, k, mine):
            x_first = units[u][1]
            index = (y if mine else 1 - y) if x_first else (x if mine else 1 - x)
            return f32(ref[k - 1, :, index]) if x_first else f32(ref[k - 1, index])

        def second(u, k):
            part, recv_one, send_two = scratch[6 * u : 6 * u + 3]
            load(u, k).wait()
            hop(u, 1, k).wait_recv()
            send_two[k - 1] = (side(u, part, k, False) + side(u, recv_one, k, False)).astype(jnp.bfloat16)
            hop(u, 2, k).start()

        def third(u, k):
            part, recv_one, _, recv_two, send_three, _ = scratch[6 * u : 6 * u + 6]
            hop(u, 2, k).wait_recv()
            total = side(u, part, k, True) + side(u, recv_one, k, True) + f32(recv_two[k - 1])
            if k < fs:
                send_three[k - 1] = total.astype(jnp.bfloat16)
                hop(u, 3, k).start()
            else:
                index, _, start, width = units[u]
                outs[index][:, :, start : start + width] = total

        swapped = swap_copies(near, far, swap_sem)
        for k in range(1, fs + 1):
            for u in range(count):
                hop(u, 1, k).start()
                load(u, k).start()
        for cp in swapped:
            cp.start()
        for k in range(1, fs + 2):
            for u in range(count):
                if k <= fs:
                    second(u, k)
            for u in range(count):
                if k > 1:
                    third(u, k - 1)
        for u in range(count):
            index, _, start, width = units[u]
            total = outs[index][:, :, start : start + width]
            for k in range(1, fs):
                hop(u, 3, k).wait_recv()
                total = total + f32(scratch[6 * u + 5][k - 1])
            outs[index][:, :, start : start + width] = total
        for u in range(count):
            for k in range(1, fs + 1):
                for stage in (1, 2, 3) if k < fs else (1, 2):
                    hop(u, stage, k).wait_send()
        for cp in swapped:
            cp.wait()

    scratch = []
    for index, x_first, _, width in units:
        q = arrays[index].shape[4]
        both = (groups, 2, q, width) if x_first else (2, groups, q, width)
        for shape in ((fs, *both), (fs, *both)) + ((fs, groups, q, width),) * 2 + ((fs - 1, groups, q, width),) * 2:
            scratch.append(pltpu.VMEM(shape, jnp.bfloat16))
    results = pl.pallas_call(
        kernel,
        out_shape=[jax.ShapeDtypeStruct((groups, a.shape[4], a.shape[5]), jnp.float32) for a in arrays]
        + [jax.ShapeDtypeStruct(a.shape, a.dtype) for a in swaps],
        in_specs=[pl.BlockSpec(memory_space=pl.ANY)] * (held + len(swaps)),
        out_specs=[pl.BlockSpec(memory_space=pltpu.VMEM)] * held + [pl.BlockSpec(memory_space=pl.ANY)] * len(swaps),
        scratch_shapes=scratch
        + [
            pltpu.SemaphoreType.DMA((count, fs)),
            pltpu.SemaphoreType.DMA((count, 3 * fs)),
            pltpu.SemaphoreType.DMA((count, 3 * fs)),
            pltpu.SemaphoreType.DMA((max(len(swaps), 1), 2)),
        ],
        compiler_params=pltpu.CompilerParams(
            collective_id=collective_id, has_side_effects=True, vmem_limit_bytes=56 << 20
        ),
        cost_estimate=pl.CostEstimate(
            flops=0, bytes_accessed=8 * sum(p.size for p in partials), transcendentals=0
        ),
        name="reduce_weights",
    )(*arrays, *swaps)
    finals = []
    for total in results[:held]:
        g = lax.axis_index(DP) // 4
        at = lambda i: lax.dynamic_index_in_dim(total, i, 0, keepdims=False)
        mine = at(g)
        for k in range(1, groups):
            mine = mine + shift_group(at((g + k) % groups), k)
        finals.append(swap_halves(mine))
    return finals, results[held:]


def gather_offloaded(shard, stream, earlier=()):
    x, _, _, _, _ = coords()
    share = shard.shape[1] // (2 * lax.axis_size(DP))
    start = (x * lax.axis_size(DP) + lax.axis_index(DP)) * share
    piece = lax.dynamic_slice(shard, (stream, start, 0), (1, share, shard.shape[2]))[0]
    return lax.all_gather(after(piece, *earlier), ("fsdp", "seq", "y", "core"), axis=0, tiled=True)


def gather_plane(left, right):
    both = lax.all_gather(jnp.concatenate([left, right], axis=1), ("seq", "y", "core"), axis=0, tiled=True)
    return both[:, : left.shape[1]], both[:, left.shape[1] :]


def own_blocks(values, axis):
    fs, n = lax.axis_size("fsdp"), lax.axis_size(DP)
    lead, tail = values.shape[:axis], values.shape[axis + 1 :]
    split = values.reshape(*lead, 2, fs, n, -1, *tail)
    split = lax.dynamic_index_in_dim(split, lax.axis_index("seq"), axis, keepdims=False)
    split = lax.dynamic_index_in_dim(split, lax.axis_index(DP), axis + 1, keepdims=False)
    return split.reshape(*lead, -1, *tail)


def sum_fsdp(total):
    fs, z = lax.axis_size("fsdp"), lax.axis_index("fsdp")
    block = lambda i: lax.dynamic_index_in_dim(total, i, 0, keepdims=False)
    mine = block(z)
    for k in range(1, fs):
        mine = mine + shift_z(block((z + k) % fs).astype(jnp.bfloat16), k).astype(jnp.float32)
    return mine


def plane_grad(left, right):
    total = dot(own_blocks(left, 1), right, 0, 0)
    return sum_fsdp(total.reshape(lax.axis_size("fsdp"), -1, total.shape[1]))


def plane_mlp_grads(modded, d_mlp, weight_up, bias_up, weight_down):
    fs, n = lax.axis_size("fsdp"), lax.axis_size(DP)
    x = lax.axis_index("seq")
    hidden = linear(modded, own_blocks(weight_up, 1), own_blocks(bias_up, 0))
    active = gelu_tanh(hidden).astype(jnp.bfloat16)
    d_active = linear_back(d_mlp, own_blocks(weight_down, 0))
    d_hidden = jax.vjp(gelu_tanh, hidden)[1](d_active)[0].astype(jnp.bfloat16)
    down = dot(active, d_mlp, 0, 0)
    grad_down = sum_fsdp(down.reshape(fs, -1, down.shape[1]))
    up = dot(modded, d_hidden, 0, 0)
    rows, units = up.shape
    up = up.reshape(2, fs, rows // (2 * fs), units).transpose(1, 0, 2, 3)
    mine = sum_fsdp(up).reshape(rows // fs, units).astype(jnp.bfloat16)
    spread = lax.all_gather(mine, ("seq", "y", "core"), axis=0)
    spread = spread.reshape(2 * n, 2, n, rows // (2 * fs * n), units)
    spread = lax.dynamic_index_in_dim(spread, x, 1, keepdims=False)
    spread = lax.dynamic_index_in_dim(spread, lax.axis_index(DP), 1, keepdims=False)
    spread = spread.reshape(2, n, spread.shape[1], fs, -1).transpose(2, 0, 3, 1, 4)
    return grad_down, spread.reshape(spread.shape[0], -1).astype(jnp.float32)


def swap_halves(mine_rows):
    _, _, _, _, c = coords()
    rows = mine_rows.shape[0] // 2
    near = lax.dynamic_slice_in_dim(mine_rows, c * rows, rows, 0)
    far = flip_core(lax.dynamic_slice_in_dim(mine_rows, (1 - c) * rows, rows, 0))
    return jnp.concatenate([jnp.where(c == 0, near, far), jnp.where(c == 0, far, near)], axis=1)


def gather_small(value):
    fs = lax.axis_size("fsdp")
    z = lax.axis_index("fsdp")
    stack = jnp.stack([value] + [shift_z(value, k) for k in range(1, fs)])
    ordered = [lax.dynamic_index_in_dim(stack, (z - j) % fs, 0, keepdims=False) for j in range(fs)]
    return jnp.stack(ordered, axis=1)


def reduce_small(value):
    fs, groups = lax.axis_size("fsdp"), lax.axis_size(DP) // 4
    value = value + flip_core(value)
    value = value + flip_x(value)
    value = value + flip_y(value)
    value = value + sum(shift_z(value, k) for k in range(1, fs))
    if groups > 1:
        value = value + sum(shift_group(value, k) for k in range(1, groups))
    return value


def wgrad_kernel(sel_ref, a0, b0, a1, b1, out, a0t, a1t):
    @pl.when(pl.program_id(1) == 0)
    def _():
        a0t[...] = a0[...].T
        a1t[...] = a1[...].T

    out[...] = (dot(a0t[...], b0[...], 1, 0) + dot(a1t[...], b1[...], 1, 0)).astype(out.dtype)


def wgrad(a0, b0, a1, b1, row_half, col_half):
    tokens, rows = a0.shape
    cols = b0.shape[1]
    tr = tc = 768
    halves = 1 if row_half is None else 2
    nr, nc = rows // halves // tr, cols // 2 // tc
    row_start = jnp.int32(0) if row_half is None else row_half * nr
    a_spec = pl.BlockSpec((tokens, tr), lambda i, j, s: (0, s[0] + i))
    b_spec = pl.BlockSpec((tokens, tc), lambda i, j, s: (0, s[1] + j))
    return pl.pallas_call(
        wgrad_kernel,
        grid_spec=pltpu.PrefetchScalarGridSpec(
            num_scalar_prefetch=1,
            grid=(nr, nc),
            in_specs=[a_spec, b_spec, a_spec, b_spec],
            out_specs=pl.BlockSpec((tr, tc), lambda i, j, s: (i, j)),
            scratch_shapes=[pltpu.VMEM((tr, tokens), a0.dtype)] * 2,
        ),
        out_shape=jax.ShapeDtypeStruct((rows // halves, cols // 2), jnp.bfloat16),
        compiler_params=pltpu.CompilerParams(vmem_limit_bytes=48 << 20),
        cost_estimate=pl.CostEstimate(
            flops=2 * tokens * (rows // halves) * cols,
            bytes_accessed=2 * tokens * (rows + cols) + rows * cols,
            transcendentals=0,
        ),
        name="wgrad",
    )(jnp.stack([row_start, col_half * nc]).astype(jnp.int32), a0, b0, a1, b1)


def partial_grad(left, right, far_left, far_right):
    return wgrad(left, right, far_left, far_right, None, lax.axis_index("core"))


def local(
    image_in,
    text_in,
    modulation,
    text_len,
    w_qkv,
    b_qkv,
    w_out,
    b_out,
    w_up,
    b_up,
    w_down,
    b_down,
    d_image,
    d_text,
):
    x, z, g, y, c = coords()
    image_half, text_half = image_in.shape[1], text_in.shape[1]
    width = image_in.shape[2]
    text_rows = -(-2 * text_half // 16) * 16

    def take(arr, index=x):
        return lax.dynamic_index_in_dim(arr, index, 0, keepdims=False)

    def join(near, far, rows):
        pad = jnp.zeros((rows - 2 * near.shape[0], width), near.dtype)
        return jnp.concatenate([near, far, pad], axis=0)

    def in_order(near, far):
        return jnp.where(x == 0, jnp.stack([near, far]), jnp.stack([far, near]))

    gathered, far = gather_weights(
        [(w_qkv, 0, True), (w_qkv, 1, False)], [take(image_in, 1 - x), take(text_in, 1 - x)], 0
    )
    weight_qkv = gathered
    streams = (join(take(image_in), far[0], 2 * image_half), join(take(text_in), far[1], text_rows))
    text_weights = [gather_offloaded(w, 1, (weight_qkv[0],)) for w in (w_out, w_up, w_down)]
    image_weights, far = gather_weights(
        [(w_out, 0, True), (w_up, 0, False), (after(w_down, weight_qkv[0]), 0, True)],
        [take(d_image, 1 - x), take(d_text, 1 - x)],
        1,
    )
    cotangents = (join(take(d_image), far[0], 2 * image_half), join(take(d_text), far[1], text_rows))
    weight_out, weight_up, weight_down = zip(image_weights, text_weights)
    gains = take(modulation)
    info = jnp.stack([take(text_len), jnp.int32(text_half), x.astype(jnp.int32)])
    small = gather_small(jnp.concatenate([b_qkv, b_out, b_up, b_down], axis=1))
    biases, start = [], 0
    for b in (b_qkv, b_out, b_up, b_down):
        biases.append(small[:, :, start : start + b.shape[1]].reshape(2, -1).astype(jnp.float32))
        start += b.shape[1]
    bias_qkv, bias_out, bias_up, bias_down = biases

    fronts = []
    for s in range(2):
        mod = gains[s]
        normed, inverse = normalize(streams[s].astype(jnp.float32))
        modded = (normed * (1.0 + mod[1]) + mod[0]).astype(jnp.bfloat16)
        projected = linear(modded, weight_qkv[s], bias_qkv[s]).astype(jnp.bfloat16)
        fronts.append((normed, inverse, modded, projected))
    att_i, att_t, lse = attn_fwd(fronts[0][3], fronts[1][3], info, tq=2 * image_half)

    outs, backs, column_sums, parts = [], [], [], {}
    token = att_i
    for s in range(2):
        mod = gains[s]
        attended = after((att_i, att_t)[s], token)
        upstream = cotangents[s].astype(jnp.float32)
        d_mlp = (mod[5] * upstream).astype(jnp.bfloat16)
        branch = linear(attended, weight_out[s], bias_out[s])
        middle = streams[s].astype(jnp.float32) + mod[2] * branch
        normed_two, inverse_two = normalize(middle)
        modded_two = (normed_two * (1.0 + mod[4]) + mod[3]).astype(jnp.bfloat16)
        if s == 1:
            text_mlp = gather_plane(modded_two, d_mlp)
        hidden = linear(modded_two, weight_up[s], bias_up[s])
        active = gelu_tanh(hidden).astype(jnp.bfloat16)
        if s == 0:
            far_active, far_d_mlp = flip_core(active), flip_core(d_mlp)
        mlp_out = linear(active, weight_down[s], bias_down[s])
        outs.append((middle + mod[5] * mlp_out).astype(jnp.bfloat16))
        d_gate_two = jnp.sum(upstream * mlp_out, axis=0)
        if s == 0:
            parts["down"] = partial_grad(after(active, outs[s]), d_mlp, far_active, far_d_mlp)
            d_mlp = after(d_mlp, parts["down"])
        d_active = linear_back(d_mlp, weight_down[s])
        d_hidden = jax.vjp(gelu_tanh, hidden)[1](d_active)[0].astype(jnp.bfloat16)
        if s == 0:
            far_d_hidden, far_modded_two = flip_core(d_hidden), flip_core(modded_two)
        d_modded_two = linear_back(d_hidden, weight_up[s])
        d_shift_two = jnp.sum(d_modded_two, axis=0)
        d_scale_two = jnp.sum(d_modded_two * normed_two, axis=0)
        d_middle = upstream + normalize_back(normed_two, inverse_two, d_modded_two * (1.0 + mod[4]))
        d_gate_one = jnp.sum(d_middle * branch, axis=0)
        d_branch = (mod[2] * d_middle).astype(jnp.bfloat16)
        if s == 0:
            parts["up"] = partial_grad(after(modded_two, d_branch), d_hidden, far_modded_two, far_d_hidden)
            far_attended, far_d_branch = flip_core(attended), flip_core(d_branch)
            d_branch = after(d_branch, parts["up"])
        else:
            text_out = gather_plane(attended, d_branch)
        d_attended = linear_back(d_branch, weight_out[s]).astype(jnp.bfloat16)
        if s == 0:
            parts["out"] = partial_grad(after(attended, d_attended), d_branch, far_attended, far_d_branch)
            token = parts["out"]
        column_sums.append([jnp.sum(a.astype(jnp.float32), axis=0) for a in (d_branch, d_hidden, d_mlp)])
        backs.append((d_attended, d_middle, d_gate_one, d_shift_two, d_scale_two, d_gate_two))
    d_front = attn_bwd(
        fronts[0][3], fronts[1][3], att_i, att_t, backs[0][0], backs[1][0], lse, info, tq=image_half
    )
    text_qkv = gather_plane(fronts[1][2], d_front[1])
    far_front, far_modded = flip_core(d_front[0]), flip_core(fronts[0][2])
    sent = [outs[0][image_half:], outs[1][text_half : 2 * text_half]]
    reduced, far_outs = reduce_weights(
        [after(parts["down"], d_front[0]), parts["up"], parts["out"]],
        [(0, True, 0, parts["down"].shape[1]), (1, False, 0, parts["up"].shape[1]), (2, True, 0, parts["out"].shape[1])],
        sent,
        2,
    )
    grads = {("down", 0): reduced[0], ("up", 0): reduced[1], ("out", 0): reduced[2]}
    grads["down", 1], grads["up", 1] = plane_mlp_grads(*text_mlp, weight_up[1], bias_up[1], weight_down[1])
    grads["out", 1] = plane_grad(*text_out)
    input_grads, gain_grads = [], []
    for s in range(2):
        mod = gains[s]
        normed, inverse, modded, _ = fronts[s]
        d_attended, d_middle, d_gate_one, d_shift_two, d_scale_two, d_gate_two = backs[s]
        d_modded = linear_back(after(d_front[s], far_outs[0]), weight_qkv[s])
        d_shift_one = jnp.sum(d_modded, axis=0)
        d_scale_one = jnp.sum(d_modded * normed, axis=0)
        input_grads.append(d_middle + normalize_back(normed, inverse, d_modded * (1.0 + mod[1])))
        gain_grads.append(
            jnp.stack([d_shift_one, d_scale_one, d_gate_one, d_shift_two, d_scale_two, d_gate_two])
        )
    mine = jnp.stack(gain_grads)
    part = partial_grad(after(fronts[0][2], *input_grads), d_front[0], far_modded, far_front)
    cols = part.shape[1]
    sent = [input_grads[0][image_half:].astype(jnp.bfloat16), input_grads[1][text_half : 2 * text_half].astype(jnp.bfloat16)]
    reduced, far_grads = reduce_weights(
        [part], [(0, True, 0, cols // 2), (0, False, cols // 2, cols // 2)], sent + [mine.reshape(-1, width)], 3
    )
    grads["qkv", 0] = reduced[0]
    grads["qkv", 1] = plane_grad(*text_qkv)
    grad_modulation = in_order(mine, far_grads[2].reshape(mine.shape))

    count = lax.axis_size(("seq", "fsdp") + DP)
    index = lax.axis_index(("seq", "fsdp") + DP)

    def cut_bias(total):
        return lax.dynamic_index_in_dim(total.reshape(2, count, -1), index, 1, keepdims=False)

    sizes = [a.shape[0] for a in column_sums[0]]
    summed = reduce_small(jnp.stack([jnp.concatenate(column_sums[s]) for s in range(2)]))
    gb_out, gb_up, gb_down = [
        cut_bias(a) for a in jnp.split(summed, [sizes[0], sizes[0] + sizes[1]], axis=1)
    ]
    gb_qkv = cut_bias(reduce_small(jnp.stack([jnp.sum(d_front[s].astype(jnp.float32), axis=0) for s in range(2)])))
    grads_qkv, grads_out, grads_up, grads_down = [
        jnp.stack([grads[name, s] for s in range(2)]) for name in ("qkv", "out", "up", "down")
    ]
    halves = (image_half, text_half)
    return (
        *[in_order(outs[s][: halves[s]], far_outs[s]) for s in range(2)],
        *[in_order(input_grads[s][: halves[s]], far_grads[s].astype(jnp.float32)) for s in range(2)],
        grad_modulation,
        grads_qkv,
        gb_qkv,
        grads_out,
        gb_out,
        grads_up,
        gb_up,
        grads_down,
        gb_down,
    )


def solution(mesh):
    seq, fsdp, dp = (mesh.shape[name] for name in ("seq", "fsdp", "dp"))
    split = Mesh(mesh.devices.reshape(seq, fsdp, dp // 2, 2), ("seq", "fsdp", "y", "core"))
    batch = ("fsdp",) + DP
    tokens = P(batch, "seq", None)
    weight, bias = P(None, "fsdp", None), P(None, "fsdp")
    in_specs = (tokens, tokens, P(batch, None, None, None), P(batch))
    in_specs += (weight, bias) * 4 + (tokens, tokens)
    everywhere = ("seq",) + batch
    grad_w, grad_b = P(None, everywhere, None), P(None, everywhere)
    out_specs = (tokens,) * 4 + (P(batch, None, None, None),) + (grad_w, grad_b) * 4
    return jax.shard_map(local, mesh=split, in_specs=in_specs, out_specs=out_specs, check_vma=False)
```

time: 2190 us -> 1880 us (0.86)
  Pallas kernels: 438 us -> 1090 us
  waiting for transfers between devices: 785 us -> 194 us
  starting transfers between devices: 253 us -> 38.4 us
  blocking collectives: 202 us -> 0 us
  local copies, waits for them, and re-layouts: 80.4 us -> 132 us
  other arithmetic: 135 us -> 86.6 us
  matrix products: 274 us -> 316 us
    pallas_call x4, Pallas kernels: 86 us -> 792 us  [the longest x2 408 us: reduce_weights(): pl.pallas_call(kernel, out_shape=[jax.ShapeDtypeStruct((groups, a.shape[4...]
    ppermute x23 -> x2, waiting for transfers between devices: 374 us -> 3.51 us  [flip_x(): return lax.ppermute(a, 'seq', [(0, 1), (1, 0)])]
    unnamed x1 -> x0, blocking collectives: 189 us -> none
    ppermute x54 -> x16, waiting for transfers between devices: 171 us -> 6.58 us  [the longest x14 5.43 us: flip_core(): return lax.ppermute(a, DP, [(i, i ^ 1) for i in range(lax.axis_size(DP))])]
    ppermute x54 -> x16, starting transfers between devices: 165 us -> 13.6 us  [the longest x14 11.7 us: flip_core(): return lax.ppermute(a, DP, [(i, i ^ 1) for i in range(lax.axis_size(DP))])]
    ppermute x36 -> x21, waiting for transfers between devices: 241 us -> 138 us  [shift_z(): return lax.ppermute(a, 'fsdp', [(i, (i + k) % n) for i in range(n)])]
    pallas_call x16 -> x4, Pallas kernels: 141 us -> 84.6 us  [wgrad(): pl.pallas_call(wgrad_kernel, grid_spec=pltpu.PrefetchScalarGridSpec(num_s...]
    all_gather x0 -> x7, waiting for transfers between devices: none -> 46.1 us  [the longest x3 46.1 us: gather_plane(): lax.all_gather(jnp.concatenate([left, right], axis=1), ('seq', 'y', 'core...]
  transfers between devices with their start and end apart: 114 -> 46, of which waited for: 38 -> 15; matrix products, arithmetic and copies ran while one was open for 22% -> 25% of each run, Pallas kernels for 20% -> 51%
where the time goes in v2:
time: 1880 us; the launch traced here: 1870 us
  Pallas kernels  1090 us (58%)
  matrix products  316 us (17%)
  waiting for transfers between devices  194 us (10%)
  local copies, waits for them, and re-layouts  132 us (7%)
  other arithmetic  86.6 us (5%)
  starting transfers between devices  38.4 us (2%)
    pallas_call x2, Pallas kernels, reduce_weights(): pl.pallas_call(kernel, out_shape=[jax.ShapeDtypeStruct((groups, a.shape[4...  408 us
    pallas_call x2, Pallas kernels, gather_weights(): pl.pallas_call(kernel, out_shape=[jax.ShapeDtypeStruct((u[0].shape[1] * f...  384 us
    dot_general x12, matrix products, dot(): lax.dot_general(a, b, (((ca,), (cb,)), ((), ())), preferred_element_type=...  181 us
    pallas_call x1, Pallas kernels, attn_bwd(): pl.pallas_call(functools.partial(attn_bwd_kernel, ti, tt, tq), grid_spec=...  146 us
    ppermute x21, waiting for transfers between devices, shift_z(): return lax.ppermute(a, 'fsdp', [(i, (i + k) % n) for i in range(n)])  138 us
    dot_general x9, matrix products, linear(): jnp.dot(values, weight, preferred_element_type=jnp.float32)  135 us
    pallas_call x4, Pallas kernels, wgrad(): pl.pallas_call(wgrad_kernel, grid_spec=pltpu.PrefetchScalarGridSpec(num_s...  84.6 us
    pallas_call x1, Pallas kernels, attn_fwd(): pl.pallas_call(functools.partial(attn_fwd_kernel, ti, tt, tq), grid_spec=...  65.5 us
  transfers between devices with their start and end apart: 46, of which 15 were waited for; matrix products, arithmetic and copies ran while one was open for 25% of the time, Pallas kernels for 51%

profile of v2, /device:TPU:9, one launch (start us, length us, event | category | flops | bytes accessed | tf_op | source)
XLA Modules:
  0.0 1872.1 jit_solution(17041053646515098789)
XLA Ops:
  21.4 136.3 %gather_weights.2 = (bf16[1536,4608]{1,0:T(8,128)(2,1)}, bf16[1536,4608]{1,0:T(8,128)(2,1)}, bf16[512,1536]{1,0:T(8,128)(2,1)S(1)}, bf16[77,1536]{1,0:T(8,128)(2,1)S(1)}) custom-call(bf16[2,384,4608]{2,1,0:T(8,128)(2,1)} %refs_1_.2, bf16[2,384,4608]{2,1,0:T(8,128)(2,1)} %refs_1_.2, bf16[512,1536]{1,0:T(8,128)(2,1)S(1)} %copy-done.2, ...), custom_call_target="tpu_custom_call" | custom-call | bytes 226492416 | tf_op jit(solution)/shard_map/gather_weights/pallas_call | solution.py:326
  172.3 248.2 %gather_weights.3 = (bf16[1536,1536]{1,0:T(8,128)(2,1)}, bf16[1536,6144]{1,0:T(8,128)(2,1)}, bf16[6144,1536]{1,0:T(8,128)(2,1)}, bf16[512,1536]{1,0:T(8,128)(2,1)S(1)}, bf16[77,1536]{1,0:T(8,128)(2,1)S(1)}) custom-call(bf16[2,384,1536]{2,1,0:T(8,128)(2,1)S(1)} %copy-done.10, bf16[2,384,6144]{2,1,0:T(8,128)(2,1)} %refs_1_.3, bf16[2,1536,1536]{2,1,0:T(8,128)(2,1)} %refs_2_, ...), custom_call_target="tpu_custom_call" | custom-call | bytes 339738624 | tf_op jit(solution)/shard_map/gather_weights/pallas_call | solution.py:326
  439.1 20.8 %add_convert_fusion.qi.ki.vi = bf16[1024,4608]{1,0:T(8,128)(2,1)} fusion(bf16[1024,1536]{1,0:T(8,128)(2,1)} %fusion.15.a0, bf16[1536,4608]{1,0:T(8,128)(2,1)} %get-tuple-element.52, f32[4608]{0:T(1024)S(1)} %add.588), kind=kOutput, calls=%fused_computation.12 | convolution fusion | flops 14504951808 | bytes 26757120 | tf_op jit(solution)/shard_map/dot_general | solution.py:153
  459.9 65.5 %attn_fwd.1 = (bf16[1024,1536]{1,0:T(8,128)(2,1)S(1)}, bf16[160,1536]{1,0:T(8,128)(2,1)S(1)}, f32[12,8,1280]{2,1,0:T(8,128)S(1)}) custom-call(s32[3]{0:T(128)S(1)} %pad_add_fusion.3.len_ref, bf16[1024,4608]{1,0:T(8,128)(2,1)} %add_convert_fusion.qi.ki.vi, bf16[1024,4608]{1,0:T(8,128)(2,1)} %add_convert_fusion.qi.ki.vi, ...), custom_call_target="tpu_custom_call" | custom-call | flops 17226006528 | bytes 14548992 | tf_op jit(solution)/shard_map/attn_fwd/pallas_call | solution.py:57
  543.8 32.8 %multiply_convert_fusion = (bf16[1024,6144]{1,0:T(8,128)(2,1)}, f32[1024,6144]{1,0:T(8,128)}) fusion(f32[6144]{0:T(1024)S(1)} %bitcast.282, bf16[1024,1536]{1,0:T(8,128)(2,1)S(1)} %add_convert_fusion.2.a0, bf16[1536,6144]{1,0:T(8,128)(2,1)} %get-tuple-element.59), kind=kOutput, calls=%fused_computation.10 | convolution fusion | flops 19390267392 | bytes 59793408 | tf_op jit(solution)/shard_map/dot_general | solution.py:153
  579.0 29.8 %fusion.23 = (f32[1536]{0:T(1024)}, bf16[1024,1536]{1,0:T(8,128)(2,1)}, bf16[1024,1536]{1,0:T(8,128)(2,1)S(1)}) fusion(f32[1536]{0:T(1024)S(1)} %add.615, bf16[512,1536]{1,0:T(8,128)(2,1)} %copy-done.14, bf16[512,1536]{1,0:T(8,128)(2,1)} %get-tuple-element.205, f32[1024,1536]{1,0:T(8,128)} %copy-done.27, f32[1536]{0:T(1024)S(1)} %get-tuple-element.162, ...), kind=kOutput, calls=%fused_computation.37 | convolution fusion | flops 19346225152 | bytes 47204352 | tf_op jit(solution)/shard_map/dot_general | solution.py:153
  616.1 25.4 %wgrad.4 = bf16[6144,768]{1,0:T(8,128)(2,1)} custom-call(s32[2]{0:T(128)S(1)} %pad_add_fusion.2.sel_ref, bf16[1024,6144]{1,0:T(8,128)(2,1)} %get-tuple-element.61.a0, bf16[1024,1536]{1,0:T(8,128)(2,1)S(1)} %get-tuple-element.64.b0, bf16[1024,6144]{1,0:T(8,128)(2,1)} %collective-permute-done.3.a1, bf16[1024,1536]{1,0:T(8,128)(2,1)} %copy-done.109), custom_call_target="tpu_custom_call" | custom-call | flops 19327352832 | bytes 25165824 | tf_op jit(solution)/shard_map/wgrad/pallas_call | solution.py:586
  641.5 41.7 %convert_reduce_fusion = (f32[6144]{0:T(1024)}, bf16[1024,6144]{1,0:T(8,128)(2,1)}) fusion(f32[1024,6144]{1,0:T(8,128)} %get-tuple-element.245, f32[6144]{0:T(1024)S(1)} %bitcast.283, bf16[1024,1536]{1,0:T(8,128)(2,1)S(1)} %get-tuple-element.64.b0, bf16[6144,1536]{1,0:T(8,128)(2,1)} %get-tuple-element.60), kind=kOutput, calls=%fused_computation.9 | convolution fusion | flops 19472050176 | bytes 59817984 | tf_op jit(solution)/shard_map/dot_general | solution.py:14
  683.9 30.9 %multiply_reduce_fusion = (f32[1536]{0:T(1024)}, f32[1024]{0:T(1024)S(1)}, f32[1024]{0:T(1024)S(1)}, f32[1536]{0:T(1024)}, f32[1024,1536]{1,0:T(8,128)}) fusion(f32[1024,1536]{1,0:T(8,128)} %copy-done.27, f32[1024]{0:T(1024)S(1)} %copy-done.75, f32[1024]{0:T(1024)S(1)} %copy-done.71, f32[1536]{0:T(1024)S(1)} %copy-done.67, ...), kind=kOutput, calls=%fused_computation.41 | convolution fusion | flops 19341502464 | bytes 44075008 | tf_op jit(solution)/shard_map/dot_general | solution.py:14
  729.5 27.9 %wgrad.5 = bf16[1536,3072]{1,0:T(8,128)(2,1)} custom-call(s32[2]{0:T(128)S(1)} %pad_add_fusion.1.sel_ref, bf16[1024,1536]{1,0:T(8,128)(2,1)S(1)} %copy-done.9, bf16[1024,6144]{1,0:T(8,128)(2,1)} %get-tuple-element.177.b0, bf16[1024,1536]{1,0:T(8,128)(2,1)} %collective-permute-done.5.a1, bf16[1024,6144]{1,0:T(8,128)(2,1)} %collective-permute-done.6.b1), custom_call_target="tpu_custom_call" | custom-call | flops 19327352832 | bytes 25165824 | tf_op jit(solution)/shard_map/wgrad/pallas_call | solution.py:586
  783.2 24.7 %copy.65 = bf16[1536,6144]{0,1:T(8,128)(2,1)} copy(bf16[1536,6144]{1,0:T(8,128)(2,1)} %all-gather.12.cloned.1.call-done) | data formatting | bytes 37748736 | tf_op jit(solution)/shard_map/all_gather | solution.py:489
  814.3 46.1 %all-gather.18.cloned.1.call-done = bf16[1280,3072]{1,0:T(8,128)(2,1)} async-done(((bf16[160,3072]{1,0:T(8,128)(2,1)}), bf16[1280,3072]{1,0:T(8,128)(2,1)}) %all-gather.18.cloned.1.call-update) | async-done | bytes 7864336 | tf_op jit(solution)/shard_map/all_gather | solution.py:493
  868.4 16.1 fusion.46
  891.3 11.4 collective-permute-done.32
  902.7 36.9 %collective-permute-done.33 = bf16[2,192,768]{2,1,0:T(8,128)(2,1)} collective-permute-done((bf16[2,192,768]{2,1,0:T(8,128)(2,1)}, bf16[2,192,768]{2,1,0:T(8,128)(2,1)}, u32[]{:S(2)}, u32[]{:S(2)}) %collective-permute-start.33) | collective-permute-done | bytes 589856 | tf_op jit(solution)/shard_map/ppermute | solution.py:186
  945.1 14.6 fusion.149
  981.1 12.6 multiply_reduce_fusion.6
  1012.9 145.8 %attn_bwd.1 = (bf16[1024,4608]{1,0:T(8,128)(2,1)}, bf16[160,4608]{1,0:T(8,128)(2,1)}) custom-call(s32[3]{0:T(128)} %copy-done.20, bf16[1024,4608]{1,0:T(8,128)(2,1)} %add_convert_fusion.qi.ki.vi, bf16[1024,4608]{1,0:T(8,128)(2,1)} %add_convert_fusion.qi.ki.vi, bf16[1024,4608]{1,0:T(8,128)(2,1)} %add_convert_fusion.qi.ki.vi, bf16[160,4608]{1,0:T(8,128)(2,1)} %copy-done.25, ...), custom_call_target="tpu_custom_call" | custom-call | flops 43065016320 | bytes 29097984 | tf_op jit(solution)/shard_map/attn_bwd/pallas_call | solution.py:126
  1165.5 287.0 %reduce_weights.2 = (f32[1,384,768]{2,1,0:T(8,128)}, f32[1,96,3072]{2,1,0:T(8,128)}, f32[1,96,768]{2,1,0:T(8,128)}, bf16[512,1536]{1,0:T(8,128)(2,1)}, bf16[77,1536]{1,0:T(8,128)(2,1)}) custom-call(bf16[2,4,1,2,384,768]{5,4,3,2,1,0:T(8,128)(2,1)} %bitcast.247, bf16[2,4,1,2,96,3072]{5,4,3,2,1,0:T(8,128)(2,1)} %bitcast.248, ...), custom_call_target="tpu_custom_call" | custom-call | bytes 84934656 | tf_op jit(solution)/shard_map/reduce_weights/pallas_call | solution.py:452
  1455.6 24.0 %fusion.20 = (f32[1536]{0:T(1024)S(1)}, f32[1024]{0:T(1024)}, f32[1024]{0:T(1024)}, f32[1536]{0:T(1024)S(1)}, f32[1024,1536]{1,0:T(8,128)}) fusion(f32[1024]{0:T(1024)} %copy-done.72, f32[1024]{0:T(1024)} %copy-done.68, bf16[512,1536]{1,0:T(8,128)(2,1)S(1)} %copy-done.1, bf16[512,1536]{1,0:T(8,128)(2,1)S(1)} %copy-done.31, f32[1536]{0:T(1024)S(1)} %copy-done.61, ...), kind=kOutput, calls=%fused_computation.34 | convolution fusion | flops 14515955712 | bytes 33064960 | tf_op jit(solution)/shard_map/dot_general | solution.py:14
  1578.3 37.3 %collective-permute-done.37 = bf16[192,1536]{1,0:T(8,128)(2,1)S(1)} collective-permute-done((bf16[192,1536]{1,0:T(8,128)(2,1)S(1)}, bf16[192,1536]{1,0:T(8,128)(2,1)S(1)}, u32[]{:S(2)}, u32[]{:S(2)}) %collective-permute-start.37) | collective-permute-done | bytes 589856 | tf_op jit(solution)/shard_map/ppermute | solution.py:186
  1620.0 22.8 %wgrad.7 = bf16[1536,2304]{1,0:T(8,128)(2,1)} custom-call(s32[2]{0:T(128)S(1)} %pad_add_fusion.sel_ref, bf16[1024,1536]{1,0:T(8,128)(2,1)} %fusion.15.a0, bf16[1024,4608]{1,0:T(8,128)(2,1)} %get-tuple-element.78.b0, bf16[1024,1536]{1,0:T(8,128)(2,1)} %collective-permute-done.9.a1, bf16[1024,4608]{1,0:T(8,128)(2,1)} %collective-permute-done.10.b1), custom_call_target="tpu_custom_call" | custom-call | flops 14495514624 | bytes 19660800 | tf_op jit(solution)/shard_map/wgrad/pallas_call | solution.py:586
  1642.9 120.7 %reduce_weights.3 = (f32[1,96,2304]{2,1,0:T(8,128)}, bf16[512,1536]{1,0:T(8,128)(2,1)}, bf16[77,1536]{1,0:T(8,128)(2,1)}, f32[12,1536]{1,0:T(8,128)}) custom-call(bf16[2,4,1,2,96,2304]{5,4,3,2,1,0:T(8,128)(2,1)} %bitcast.255, bf16[512,1536]{1,0:T(8,128)(2,1)} %slice.258.refs_1_, bf16[77,1536]{1,0:T(8,128)(2,1)} %slice.259.refs_2_, f32[12,1536]{1,0:T(8,128)} %reshape.334.refs_3_), custom_call_target="tpu_custom_call" | custom-call | bytes 28311552 | tf_op jit(solution)/shard_map/reduce_weights/pallas_call | solution.py:452
  1832.6 26.6 %collective-permute-done.13 = bf16[48,4608]{1,0:T(8,128)(2,1)S(1)} collective-permute-done((bf16[48,4608]{1,0:T(8,128)(2,1)S(1)}, bf16[48,4608]{1,0:T(8,128)(2,1)S(1)}, u32[]{:S(2)}, u32[]{:S(2)}) %collective-permute-start.13) | collective-permute-done | bytes 442400 | tf_op jit(solution)/shard_map/ppermute | solution.py:186
  (503 shorter events, 370.1 us)
Async XLA Ops:
  7.2 769.6 %all-gather.8.cloned.1.call-start = ((), (), s32[]{:S(2)}) async-start(), calls=%async_computation | async-start | bytes 4866048 | tf_op jit(solution)/shard_map/all_gather | solution.py:489
  157.7 625.5 %all-gather.12.cloned.1.call-start = ((), (), s32[]{:S(2)}) async-start(), calls=%async_computation.2 | async-start | bytes 19464192 | tf_op jit(solution)/shard_map/all_gather | solution.py:489
  160.2 651.0 %all-gather.10.cloned.1.call-start = ((), (), s32[]{:S(2)}) async-start(), calls=%async_computation.1 | async-start | bytes 19464192 | tf_op jit(solution)/shard_map/all_gather | solution.py:489
  160.3 270.8 %collective-permute-start = (bf16[2,3456]{1,0:T(2,128)(2,1)S(1)}, bf16[2,3456]{1,0:T(2,128)(2,1)S(1)}, u32[]{:S(2)}, u32[]{:S(2)}) collective-permute-start(bf16[2,3456]{1,0:T(2,128)(2,1)S(1)} %constant_dynamic-update-slice_fusion), channel_id=1, source_target_pairs={{0,4},{4,8},{8,12},{12,0},{1,5},{5,9},{9,13},{13,1},{2,6},{6,10},{... | collective-permute-start | bytes 41480 | tf_op jit(solution)/shard_map/ppermute | solution.py:186
  161.2 270.0 %collective-permute-start.1 = (bf16[2,3456]{1,0:T(2,128)(2,1)S(1)}, bf16[2,3456]{1,0:T(2,128)(2,1)S(1)}, u32[]{:S(2)}, u32[]{:S(2)}) collective-permute-start(bf16[2,3456]{1,0:T(2,128)(2,1)S(1)} %constant_dynamic-update-slice_fusion), channel_id=1, source_target_pairs={{0,8},{4,12},{8,0},{12,4},{1,9},{5,13},{9,1},{13,5},{2,10},{6,14},... | collective-permute-start | bytes 41480 | tf_op jit(solution)/shard_map/ppermute | solution.py:186
  162.2 269.0 %collective-permute-start.2 = (bf16[2,3456]{1,0:T(2,128)(2,1)S(1)}, bf16[2,3456]{1,0:T(2,128)(2,1)S(1)}, u32[]{:S(2)}, u32[]{:S(2)}) collective-permute-start(bf16[2,3456]{1,0:T(2,128)(2,1)S(1)} %constant_dynamic-update-slice_fusion), channel_id=1, source_target_pairs={{0,12},{4,0},{8,4},{12,8},{1,13},{5,1},{9,5},{13,9},{2,14},{6,2},{... | collective-permute-start | bytes 41480 | tf_op jit(solution)/shard_map/ppermute | solution.py:186
  576.7 37.8 %collective-permute-start.3 = (bf16[1024,6144]{1,0:T(8,128)(2,1)}, bf16[1024,6144]{1,0:T(8,128)(2,1)}, u32[]{:S(2)}, u32[]{:S(2)}) collective-permute-start(bf16[1024,6144]{1,0:T(8,128)(2,1)} %get-tuple-element.61.a0), channel_id=1, source_target_pairs={{0,1},{1,0},{2,3},{3,2},{4,5},{5,4},{6,7},{7,6},{8,9},{9,8},{10,11... | collective-permute-start | bytes 37748744 | tf_op jit(solution)/shard_map/ppermute | solution.py:181
  578.9 281.5 %all-gather.18.cloned.1.call-start = ((), (), s32[]{:S(2)}) async-start(), calls=%async_computation.5 | async-start | bytes 8847360 | tf_op jit(solution)/shard_map/all_gather | solution.py:493
  683.2 46.3 %collective-permute-start.6 = (bf16[1024,6144]{1,0:T(8,128)(2,1)}, bf16[1024,6144]{1,0:T(8,128)(2,1)}, u32[]{:S(2)}, u32[]{:S(2)}) collective-permute-start(bf16[1024,6144]{1,0:T(8,128)(2,1)} %get-tuple-element.177.b0), channel_id=1, source_target_pairs={{0,1},{1,0},{2,3},{3,2},{4,5},{5,4},{6,7},{7,6},{8,9},{9,8},{10,11... | collective-permute-start | bytes 37748744 | tf_op jit(solution)/shard_map/ppermute | solution.py:181
  683.4 46.1 %collective-permute-start.5 = (bf16[1024,1536]{1,0:T(8,128)(2,1)}, bf16[1024,1536]{1,0:T(8,128)(2,1)}, u32[]{:S(2)}, u32[]{:S(2)}) collective-permute-start(bf16[1024,1536]{1,0:T(8,128)(2,1)} %copy-done.8), channel_id=1, source_target_pairs={{0,1},{1,0},{2,3},{3,2},{4,5},{5,4},{6,7},{7,6},{8,9},{9,8},{10,11... | collective-permute-start | bytes 9437192 | tf_op jit(solution)/shard_map/ppermute | solution.py:181
  683.7 83.1 %collective-permute-start.7 = (bf16[1024,1536]{1,0:T(8,128)(2,1)}, bf16[1024,1536]{1,0:T(8,128)(2,1)}, u32[]{:S(2)}, u32[]{:S(2)}) collective-permute-start(bf16[1024,1536]{1,0:T(8,128)(2,1)} %copy-done.21), channel_id=1, source_target_pairs={{0,1},{1,0},{2,3},{3,2},{4,5},{5,4},{6,7},{7,6},{8,9},{9,8},{10,11... | collective-permute-start | bytes 9437192 | tf_op jit(solution)/shard_map/ppermute | solution.py:181
  729.1 37.8 %collective-permute-start.8 = (bf16[1024,1536]{1,0:T(8,128)(2,1)}, bf16[1024,1536]{1,0:T(8,128)(2,1)}, u32[]{:S(2)}, u32[]{:S(2)}) collective-permute-start(bf16[1024,1536]{1,0:T(8,128)(2,1)} %multiply_convert_fusion.1.b0), channel_id=1, source_target_pairs={{0,1},{1,0},{2,3},{3,2},{4,5},{5,4},{6,7},{7,6},{8,9},{9,8},{10,11... | collective-permute-start | bytes 9437192 | tf_op jit(solution)/shard_map/ppermute | solution.py:181
  782.9 996.3 %all-gather.20.cloned.1.call-start = ((), (), s32[]{:S(2)}) async-start(), calls=%async_computation.6 | async-start | bytes 5308416 | tf_op jit(solution)/shard_map/all_gather | solution.py:533
  888.9 50.7 %collective-permute-start.33 = (bf16[2,192,768]{2,1,0:T(8,128)(2,1)}, bf16[2,192,768]{2,1,0:T(8,128)(2,1)}, u32[]{:S(2)}, u32[]{:S(2)}) collective-permute-start(bf16[2,192,768]{2,1,0:T(8,128)(2,1)} %get-tuple-element.198), channel_id=1, source_target_pairs={{0,8},{4,12},{8,0},{12,4},{1,9},{5,13},{9,1},{13,5},{2,10},{6,14},... | collective-permute-start | bytes 1769480 | tf_op jit(solution)/shard_map/ppermute | solution.py:186
  890.0 52.1 %collective-permute-start.34 = (bf16[2,192,768]{2,1,0:T(8,128)(2,1)S(1)}, bf16[2,192,768]{2,1,0:T(8,128)(2,1)}, u32[]{:S(2)}, u32[]{:S(2)}) collective-permute-start(bf16[2,192,768]{2,1,0:T(8,128)(2,1)S(1)} %get-tuple-element.197), channel_id=1, source_target_pairs={{0,12},{4,0},{8,4},{12,8},{1,13},{5,1},{9,5},{13,9},{2,14},{6,2},{... | collective-permute-start | bytes 1769480 | tf_op jit(solution)/shard_map/ppermute | solution.py:186
  945.0 841.7 %all-gather.16.cloned.1.call-start = ((), (), s32[]{:S(2)}) async-start(), calls=%async_computation.4 | async-start | bytes 8847360 | tf_op jit(solution)/shard_map/all_gather | solution.py:493
  997.8 806.1 %all-gather.14.cloned.1.call-start = ((), (), s32[]{:S(2)}) async-start(), calls=%async_computation.3 | async-start | bytes 17694720 | tf_op jit(solution)/shard_map/all_gather | solution.py:493
  997.9 622.1 %collective-permute-start.9 = (bf16[1024,1536]{1,0:T(8,128)(2,1)}, bf16[1024,1536]{1,0:T(8,128)(2,1)}, u32[]{:S(2)}, u32[]{:S(2)}) collective-permute-start(bf16[1024,1536]{1,0:T(8,128)(2,1)} %fusion.15.a0), channel_id=1, source_target_pairs={{0,1},{1,0},{2,3},{3,2},{4,5},{5,4},{6,7},{7,6},{8,9},{9,8},{10,11... | collective-permute-start | bytes 9437192 | tf_op jit(solution)/shard_map/ppermute | solution.py:181
  1159.4 373.1 %collective-permute-start.25 = (f32[2,9216]{1,0:T(2,128)}, f32[2,9216]{1,0:T(2,128)}, u32[]{:S(2)}, u32[]{:S(2)}) collective-permute-start(f32[2,9216]{1,0:T(2,128)} %pad_maximum_fusion.10), channel_id=1, source_target_pairs={{0,1},{1,0},{2,3},{3,2},{4,5},{5,4},{6,7},{7,6},{8,9},{9,8},{10,11... | collective-permute-start | bytes 221192 | tf_op jit(solution)/shard_map/ppermute | solution.py:181
  1453.5 65.4 %collective-permute-start.15 = (f32[2,4608]{1,0:T(2,128)}, f32[2,4608]{1,0:T(2,128)S(1)}, u32[]{:S(2)}, u32[]{:S(2)}) collective-permute-start(f32[2,4608]{1,0:T(2,128)} %pad_maximum_fusion.13), channel_id=1, source_target_pairs={{0,1},{1,0},{2,3},{3,2},{4,5},{5,4},{6,7},{7,6},{8,9},{9,8},{10,11... | collective-permute-start | bytes 110600 | tf_op jit(solution)/shard_map/ppermute | solution.py:181
  1524.7 95.4 %collective-permute-start.10 = (bf16[1024,4608]{1,0:T(8,128)(2,1)}, bf16[1024,4608]{1,0:T(8,128)(2,1)}, u32[]{:S(2)}, u32[]{:S(2)}) collective-permute-start(bf16[1024,4608]{1,0:T(8,128)(2,1)} %get-tuple-element.78.b0), channel_id=1, source_target_pairs={{0,1},{1,0},{2,3},{3,2},{4,5},{5,4},{6,7},{7,6},{8,9},{9,8},{10,11... | collective-permute-start | bytes 28311560 | tf_op jit(solution)/shard_map/ppermute | solution.py:181
  1565.3 50.2 %collective-permute-start.37 = (bf16[192,1536]{1,0:T(8,128)(2,1)S(1)}, bf16[192,1536]{1,0:T(8,128)(2,1)S(1)}, u32[]{:S(2)}, u32[]{:S(2)}) collective-permute-start(bf16[192,1536]{1,0:T(8,128)(2,1)S(1)} %get-tuple-element.195), channel_id=1, source_target_pairs={{0,8},{4,12},{8,0},{12,4},{1,9},{5,13},{9,1},{13,5},{2,10},{6,14},... | collective-permute-start | bytes 1769480 | tf_op jit(solution)/shard_map/ppermute | solution.py:186
  1568.0 50.1 %collective-permute-start.38 = (bf16[192,1536]{1,0:T(8,128)(2,1)S(1)}, bf16[192,1536]{1,0:T(8,128)(2,1)S(1)}, u32[]{:S(2)}, u32[]{:S(2)}) collective-permute-start(bf16[192,1536]{1,0:T(8,128)(2,1)S(1)} %get-tuple-element.194), channel_id=1, source_target_pairs={{0,12},{4,0},{8,4},{12,8},{1,13},{5,1},{9,5},{13,9},{2,14},{6,2},{... | collective-permute-start | bytes 1769480 | tf_op jit(solution)/shard_map/ppermute | solution.py:186
  1824.4 39.1 %collective-permute-start.14 = (bf16[48,4608]{1,0:T(8,128)(2,1)S(1)}, bf16[48,4608]{1,0:T(8,128)(2,1)S(1)}, u32[]{:S(2)}, u32[]{:S(2)}) collective-permute-start(bf16[48,4608]{1,0:T(8,128)(2,1)S(1)} %get-tuple-element.200), channel_id=1, source_target_pairs={{0,12},{4,0},{8,4},{12,8},{1,13},{5,1},{9,5},{13,9},{2,14},{6,2},{... | collective-permute-start | bytes 1327112 | tf_op jit(solution)/shard_map/ppermute | solution.py:186
  (135 other events, 4977.2 us)
Sparse Core Ops, SparseCore 0:
  157.8 122.7 all-gather.7
  284.1 178.9 all-gather.11
  579.1 145.9 all-gather.9
  783.0 77.3 all-gather.17
  945.1 38.2 all-gather.19
  998.0 51.2 all-gather.15
  1455.6 87.2 all-gather.13

commit v3 on v2

v3 whole, which is shorter than its diff:
```python
import functools

import jax
import jax.numpy as jnp
from jax import lax
from jax.experimental import pallas as pl
from jax.experimental.pallas import tpu as pltpu
from jax.sharding import Mesh, PartitionSpec as P

EPSILON = 1e-06
HEAD_DIM=64
MASKED=-1000000000.0
def dot(a,b,ca,cb):
    return lax.dot_general(a,b,(((ca,),(cb,)),((),())),preferred_element_type=jnp.float32)

def attn_fwd_kernel(ti,tt,tq,len_ref,qi,ki,vi,qt,kt,vt,oi,ot,lse,ktp,vtp):
    tp=ktp.shape[0]
    ktp[...]=jnp.zeros_like(ktp); vtp[...]=jnp.zeros_like(vtp)
    ktp[:tt,:]=kt[...]; vtp[:tt,:]=vt[...]
    n_len=len_ref[0]; half=len_ref[1]; mine=len_ref[2]
    r=lax.broadcasted_iota(jnp.int32,(1,tp),1)
    pos=jnp.where(r<half,mine*half+r,(1-mine)*half+r-half)
    valid=(r<2*half)&(pos<n_len)
    lane=lax.broadcasted_iota(jnp.int32,(1,2*HEAD_DIM),1)
    k_img=ki[...]; v_img=vi[...]; k_txt=ktp[...]; v_txt=vtp[...]
    def one(q,rows):
        outs=[];lses=[]
        for h in range(2):
            qh=jnp.where((lane<HEAD_DIM)==(h==0),q.astype(jnp.float32)*(HEAD_DIM**-0.5),0.0).astype(jnp.bfloat16)
            s1=dot(qh,k_img,1,1); s2=dot(qh,k_txt,1,1)
            s2=jnp.where(valid,s2,MASKED)
            m=jnp.maximum(jnp.max(s1,axis=1,keepdims=True),jnp.max(s2,axis=1,keepdims=True))
            e1=jnp.exp(s1-m); e2=jnp.exp(s2-m)
            l=jnp.sum(e1,axis=1,keepdims=True)+jnp.sum(e2,axis=1,keepdims=True)
            inv=1.0/l
            o=dot((e1*inv).astype(jnp.bfloat16),v_img,1,0)+dot((e2*inv).astype(jnp.bfloat16),v_txt,1,0)
            outs.append(o); lses.append(m+jnp.log(l))
        o=jnp.where(lane<HEAD_DIM,outs[0],outs[1]).astype(jnp.bfloat16)
        both=jnp.where(lane<HEAD_DIM,jnp.broadcast_to(lses[0],(rows,128)),jnp.broadcast_to(lses[1],(rows,128)))
        return o,both.T
    def step(i,_):
        start=pl.multiple_of(i*tq,tq)
        o,b=one(qi[pl.ds(start,tq),:],tq)
        oi[pl.ds(start,tq),:]=o
        lse[0,0:1,pl.ds(start,tq)]=b[0:1]; lse[0,1:2,pl.ds(start,tq)]=b[64:65]
        return 0
    lax.fori_loop(0,ti//tq,step,0)
    qpad=jnp.concatenate([qt[...],jnp.zeros((tp-tt,128),jnp.bfloat16)],axis=0)
    o,b=one(qpad,tp)
    ot[...]=o[:tt]
    lse[0,0:1,ti:ti+tp]=b[0:1]; lse[0,1:2,ti:ti+tp]=b[64:65]

def attn_bwd_kernel(ti,tt,tq,len_ref,qi,ki,vi,qt,kt,vt,oi,ot,di,dt,lse,outi,outt,ktp,vtp,dk1,dk2,dv1,dv2,dqi,dqt):
    j=pl.program_id(1)
    tp=ktp.shape[0]
    @pl.when(j==0)
    def _():
        ktp[...]=jnp.zeros_like(ktp); vtp[...]=jnp.zeros_like(vtp)
        ktp[:tt,:]=kt[...]; vtp[:tt,:]=vt[...]
        n_len=len_ref[0]; half=len_ref[1]; mine=len_ref[2]
        r=lax.broadcasted_iota(jnp.int32,(tp,1),0)
        pos=jnp.where(r<half,mine*half+r,(1-mine)*half+r-half)
        valid=(r<2*half)&(pos<n_len)
        lane=lax.broadcasted_iota(jnp.int32,(1,128),1)
        sub=lax.broadcasted_iota(jnp.int32,(8,128),0); lane8=lax.broadcasted_iota(jnp.int32,(8,128),1)
        sel=jnp.where((lane8//HEAD_DIM)==sub,1.0,0.0).astype(jnp.bfloat16)
        k_img=ki[...]; v_img=vi[...]; k_txt=ktp[...]; v_txt=vtp[...]
        for ref in (dk1,dk2,dv1,dv2): ref[...]=jnp.zeros_like(ref)
        def one(q,do,o,ls):
            prod=do.astype(jnp.float32)*o.astype(jnp.float32)
            hi=prod.astype(jnp.bfloat16); lo=(prod-hi.astype(jnp.float32)).astype(jnp.bfloat16)
            dsum=dot(sel,hi,1,1)+dot(sel,lo,1,1)
            qs=(q.astype(jnp.float32)*(HEAD_DIM**-0.5))
            dof=do.astype(jnp.float32)
            dqs=[]
            for h in range(2):
                mk=(lane<HEAD_DIM)==(h==0)
                qh=jnp.where(mk,qs,0.0).astype(jnp.bfloat16)
                dh=jnp.where(mk,dof,0.0).astype(jnp.bfloat16)
                L=ls[h:h+1]; D=dsum[h:h+1]
                s1=dot(k_img,qh,1,1); s2=dot(k_txt,qh,1,1)
                p1=jnp.exp(s1-L); p2=jnp.where(valid,jnp.exp(s2-L),0.0)
                dp1=dot(v_img,dh,1,1); dp2=dot(v_txt,dh,1,1)
                ds1=(p1*(dp1-D)).astype(jnp.bfloat16); ds2=(p2*(dp2-D)).astype(jnp.bfloat16)
                dv1[...]+=dot(p1.astype(jnp.bfloat16),dh,1,0)
                dv2[...]+=dot(p2.astype(jnp.bfloat16),dh,1,0)
                dk1[...]+=dot(ds1,qh,1,0)
                dk2[...]+=dot(ds2,qh,1,0)
                dqs.append(dot(ds1,k_img,0,0)+dot(ds2,k_txt,0,0))
            return (jnp.where(lane<HEAD_DIM,dqs[0],dqs[1])*(HEAD_DIM**-0.5)).astype(jnp.bfloat16)
        def step(i,_):
            start=pl.multiple_of(i*tq,tq)
            sl=pl.ds(start,tq)
            dqi[sl,:]=one(qi[sl,:],di[sl,:],oi[sl,:],lse[0,:,sl])
            return 0
        lax.fori_loop(0,ti//tq,step,0)
        pad=lambda a: jnp.concatenate([a,jnp.zeros((tp-tt,128),jnp.bfloat16)],axis=0)
        dqt[...]=one(pad(qt[...]),pad(dt[...]),pad(ot[...]),lse[0,:,ti:ti+tp])[:tt]
        outi[...]=dqi[...]; outt[...]=dqt[...]
    @pl.when(j==1)
    def _():
        outi[...]=dk1[...].astype(jnp.bfloat16); outt[...]=dk2[:tt,:].astype(jnp.bfloat16)
    @pl.when(j==2)
    def _():
        outi[...]=dv1[...].astype(jnp.bfloat16); outt[...]=dv2[:tt,:].astype(jnp.bfloat16)


def normalize(values):
    row_mean = jnp.mean(values, axis=-1, keepdims=True)
    centred = values - row_mean
    variance = jnp.mean(centred * centred, axis=-1, keepdims=True)
    inverse = lax.rsqrt(variance + EPSILON)
    return (centred * inverse, inverse)


def normalize_back(normed, inverse, upstream):
    mean_one = jnp.mean(upstream, axis=-1, keepdims=True)
    mean_two = jnp.mean(upstream * normed, axis=-1, keepdims=True)
    return inverse * (upstream - mean_one - normed * mean_two)


def linear(values, weight, offset):
    return jnp.dot(values, weight, preferred_element_type=jnp.float32) + offset.astype(jnp.float32)


def linear_back(upstream, weight):
    return dot(upstream, weight, 1, 1)


def gelu_both(values):
    inner = jnp.tanh(0.7978845608028654 * values * (1.0 + 0.044715 * values * values))
    half = 0.5 * (1.0 + inner)
    slope = half + 0.5 * values * (1.0 - inner * inner) * (0.7978845608028654 * (1.0 + 0.134145 * values * values))
    return (values * half).astype(jnp.bfloat16), slope.astype(jnp.bfloat16)


DP = ("y", "core")


def coords():
    dp = lax.axis_index(DP)
    return lax.axis_index("seq"), lax.axis_index("fsdp"), dp // 4, (dp // 2) % 2, dp % 2


def flip_x(a):
    return lax.ppermute(a, "seq", [(0, 1), (1, 0)])


def flip_y(a):
    return lax.ppermute(a, DP, [(i, i ^ 2) for i in range(lax.axis_size(DP))])


def flip_core(a):
    return lax.ppermute(a, DP, [(i, i ^ 1) for i in range(lax.axis_size(DP))])


def shift_z(a, k):
    n = lax.axis_size("fsdp")
    return lax.ppermute(a, "fsdp", [(i, (i + k) % n) for i in range(n)])


def shift_group(a, k):
    n = lax.axis_size(DP)
    return lax.ppermute(a, DP, [(i, (i + 4 * k) % n) for i in range(n)])


def after(value, *earlier):
    return lax.optimization_barrier((value, *earlier))[0]


def enter(z_too=True, y_too=True, core_too=True):
    fs = lax.axis_size("fsdp")
    x, z, _, y, c = coords()
    targets = [{"seq": 1 - x}]
    if y_too:
        targets.append({"y": lax.axis_index("y") + 1 - 2 * y})
    if core_too:
        targets.append({"core": 1 - c})
    if z_too:
        targets += [{"fsdp": lax.rem(z + k, fs)} for k in range(1, fs)]
    barrier = pltpu.get_barrier_semaphore()
    for target in targets:
        pl.semaphore_signal(barrier, inc=1, device_id=target, device_id_type=pl.DeviceIdType.MESH)
    pl.semaphore_wait(barrier, len(targets))


def swap_copies(srcs, dsts, sems):
    x = lax.axis_index("seq")
    return [
        pltpu.make_async_remote_copy(
            src_ref=src,
            dst_ref=dst,
            send_sem=sems.at[i, 0],
            recv_sem=sems.at[i, 1],
            device_id={"seq": 1 - x},
            device_id_type=pl.DeviceIdType.MESH,
        )
        for i, (src, dst) in enumerate(zip(srcs, dsts))
    ]


def gather_plan(units, shards, outs, bufs, local_sem, send_sem, recv_sem):
    fs = lax.axis_size("fsdp")
    count = len(units)
    kinds = ("first", "second", "core0", "forward", "core1", "core2", "core3")
    x, z, _, y, c = coords()
    to_x, to_y, to_core = {"seq": 1 - x}, {"y": lax.axis_index("y") + 1 - 2 * y}, {"core": 1 - c}

    def remote(src, dst, u, slot, target):
        return pltpu.make_async_remote_copy(
            src_ref=src,
            dst_ref=dst,
            send_sem=send_sem.at[u, slot],
            recv_sem=recv_sem.at[u, slot],
            device_id=target,
            device_id_type=pl.DeviceIdType.MESH,
        )

    def spot(u, from_z, dx, dy, cc):
        _, r, cols = units[u][0].shape
        q, h = r // 4, cols // 2
        xx = 1 - x if dx else x
        yy = 1 - y if dy else y
        row = pl.multiple_of(from_z * r + (xx * 2 + yy) * q, 16)
        return outs[u].at[pl.ds(row, q), pl.ds(pl.multiple_of(cc * h, 128), h)]

    def copy(u, kind, k):
        _, r, cols = units[u][0].shape
        q, h = r // 4, cols // 2
        if kind == "z":
            dst = spot(u, lax.rem(z - k + 1 + fs, fs), 0, 0, c)
            row = pl.multiple_of((x * 2 + y) * q, 16)
            own_piece = shards[u].at[units[u][1], pl.ds(row, q), pl.ds(pl.multiple_of(c * h, 128), h)]
            return remote(own_piece if k == 1 else dst, dst, u, k - 1, {"fsdp": lax.rem(z + 1, fs)})
        x_first = units[u][2]
        slot = (1 + kinds.index(kind)) * (fs - 1) + k - 1
        via = (1, 0) if x_first else (0, 1)
        other = (0, 1) if x_first else (1, 0)
        where, target = {
            "first": ((0, 0), to_x if x_first else to_y),
            "second": ((0, 0), to_y if x_first else to_x),
            "core0": ((0, 0), to_core),
            "forward": (via, to_y if x_first else to_x),
            "core1": (via, to_core),
            "core2": (other, to_core),
            "core3": ((1, 1), to_core),
        }[kind]
        place = spot(u, lax.rem(z - k + fs, fs), *where, c)
        return remote(place, place, u, slot, target)

    def fetch(u):
        return pltpu.make_async_copy(shards[u].at[units[u][1]], bufs[u], local_sem.at[u, 0])

    def own(u):
        r = units[u][0].shape[1]
        return pltpu.make_async_copy(
            bufs[u], outs[u].at[pl.ds(pl.multiple_of(z * r, 16), r), :], local_sem.at[u, 1]
        )

    ahead = min(2, count)
    order = [(u, k) for k in range(1, fs) for u in range(count)]

    def begin():
        for u, k in order[:ahead]:
            copy(u, "z", k).start()
        for u in range(count):
            fetch(u).start()
        for u in range(count):
            fetch(u).wait()
            own(u).start()

    def act(i):
        if i < len(order):
            u, k = order[i]
            copy(u, "z", k).wait_recv()
            if i + ahead < len(order):
                copy(order[i + ahead][0], "z", order[i + ahead][1]).start()
            for kind in ("first", "second", "core0"):
                copy(u, kind, k).start()
        if 0 <= i - lag < len(order):
            u, k = order[i - lag]
            copy(u, "first", k).wait_recv()
            copy(u, "forward", k).start()
            copy(u, "core1", k).start()
        if 0 <= i - 2 * lag < len(order):
            u, k = order[i - 2 * lag]
            copy(u, "second", k).wait_recv()
            copy(u, "core2", k).start()
            copy(u, "forward", k).wait_recv()
            copy(u, "core3", k).start()

    lag = 2
    actions = [functools.partial(act, i) for i in range(len(order) + 2 * lag)]

    def end():
        for u in range(count):
            for k in range(1, fs):
                for kind in ("core0", "core1", "core2", "core3"):
                    copy(u, kind, k).wait_recv()
                for kind in ("z",) + kinds:
                    copy(u, kind, k).wait_send()
            own(u).wait()

    return begin, actions, end


def gather_shapes(units):
    fs = lax.axis_size("fsdp")
    return [jax.ShapeDtypeStruct((u[0].shape[1] * fs, u[0].shape[2]), u[0].dtype) for u in units]


def gather_scratch(units, swaps):
    fs = lax.axis_size("fsdp")
    return [pltpu.VMEM(u[0].shape[1:], u[0].dtype) for u in units] + [
        pltpu.SemaphoreType.DMA((len(units), 2)),
        pltpu.SemaphoreType.DMA((len(units), 8 * (fs - 1))),
        pltpu.SemaphoreType.DMA((len(units), 8 * (fs - 1))),
        pltpu.SemaphoreType.DMA((max(len(swaps), 1), 2)),
    ]


def gather_weights(units, swaps, collective_id):
    count, n = len(units), len(units) + len(swaps)

    def kernel(*refs):
        shards, near, outs, far = refs[:count], refs[count:n], refs[n : n + count], refs[n + count : 2 * n]
        enter()
        swapped = swap_copies(near, far, refs[-1])
        for cp in swapped:
            cp.start()
        begin, actions, end = gather_plan(units, shards, outs, refs[2 * n : 2 * n + count], *refs[-4:-1])
        begin()
        for action in actions:
            action()
        end()
        for cp in swapped:
            cp.wait()

    results = pl.pallas_call(
        kernel,
        out_shape=gather_shapes(units) + [jax.ShapeDtypeStruct(a.shape, a.dtype) for a in swaps],
        in_specs=[pl.BlockSpec(memory_space=pl.ANY)] * n,
        out_specs=[pl.BlockSpec(memory_space=pl.ANY)] * n,
        scratch_shapes=gather_scratch(units, swaps),
        compiler_params=pltpu.CompilerParams(
            collective_id=collective_id, has_side_effects=True, vmem_limit_bytes=48 << 20
        ),
        name="gather_weights",
    )(*[u[0] for u in units], *swaps)
    return results[:count], results[count:]


def attend_and_gather(qkv_i, qkv_t, info, tq, units, swaps, collective_id):
    ti, w3 = qkv_i.shape
    tt, w, tp = qkv_t.shape[0], w3 // 3, 256
    steps = w // 128
    count, n = len(units), len(units) + len(swaps)
    bi = lambda off: pl.BlockSpec((ti, 128), lambda p, s, off=off: (0, p + off * steps))
    bt = lambda off: pl.BlockSpec((tt, 128), lambda p, s, off=off: (0, p + off * steps))

    def kernel(*refs):
        info_ref, attn_in = refs[0], refs[1:7]
        shards, near = refs[7 : 7 + count], refs[7 + count : 7 + n]
        attn_out, rest = refs[7 + n : 10 + n], refs[10 + n :]
        outs, far, pads = rest[:count], rest[count:n], rest[n : n + 2]
        step = pl.program_id(0)
        swapped = swap_copies(near, far, refs[-1])
        begin, actions, end = gather_plan(units, shards, outs, rest[n + 2 : n + 2 + count], *refs[-4:-1])

        @pl.when(step == 0)
        def _():
            enter()
            begin()
            for cp in swapped:
                cp.start()

        early = min(steps - 2, len(actions))
        for index in range(early):
            pl.when(step == index + 2)(actions[index])
        attn_fwd_kernel(ti, tt, tq, info_ref, *attn_in, *attn_out, *pads)

        @pl.when(step == steps - 1)
        def _():
            for action in actions[early:]:
                action()
            end()
            for cp in swapped:
                cp.wait()

    results = pl.pallas_call(
        kernel,
        grid_spec=pltpu.PrefetchScalarGridSpec(
            num_scalar_prefetch=1,
            grid=(steps,),
            in_specs=[bi(0), bi(1), bi(2), bt(0), bt(1), bt(2)] + [pl.BlockSpec(memory_space=pl.ANY)] * n,
            out_specs=[bi(0), bt(0), pl.BlockSpec((1, 8, ti + tp), lambda p, s: (p, 0, 0))]
            + [pl.BlockSpec(memory_space=pl.ANY)] * n,
            scratch_shapes=[pltpu.VMEM((tp, 128), jnp.bfloat16)] * 2 + gather_scratch(units, swaps),
        ),
        out_shape=[
            jax.ShapeDtypeStruct((ti, w), jnp.bfloat16),
            jax.ShapeDtypeStruct((tt, w), jnp.bfloat16),
            jax.ShapeDtypeStruct((steps, 8, ti + tp), jnp.float32),
        ]
        + gather_shapes(units)
        + [jax.ShapeDtypeStruct(a.shape, a.dtype) for a in swaps],
        compiler_params=pltpu.CompilerParams(
            collective_id=collective_id, has_side_effects=True, vmem_limit_bytes=56 << 20
        ),
        name="attend_and_gather",
    )(info, qkv_i, qkv_i, qkv_i, qkv_t, qkv_t, qkv_t, *[u[0] for u in units], *swaps)
    return results[:3], results[3 : 3 + count], results[3 + count :]


def reduce_plan(units, ins, outs, scratch, totals, load_sem, send_sem, recv_sem, out_sem):
    fs = lax.axis_size("fsdp")
    count = len(units)
    x, z, _, y, _ = coords()
    to_x, to_y = {"seq": 1 - x}, {"y": lax.axis_index("y") + 1 - 2 * y}
    f32 = lambda a: a.astype(jnp.float32)

    def remote(u, slot, src, dst, target):
        return pltpu.make_async_remote_copy(
            src_ref=src,
            dst_ref=dst,
            send_sem=send_sem.at[u, slot],
            recv_sem=recv_sem.at[u, slot],
            device_id=target,
            device_id_type=pl.DeviceIdType.MESH,
        )

    def rows(u, k, mine):
        index, x_first, start, width = units[u]
        zz = lax.rem(z + k, fs)
        cols = pl.ds(start, width)
        if x_first:
            return ins[index].at[x if mine else 1 - x, zz, :, :, :, cols]
        return ins[index].at[:, zz, :, y if mine else 1 - y, :, cols]

    def load(u, k):
        return pltpu.make_async_copy(rows(u, k, True), scratch[4 * u].at[k - 1], load_sem.at[u, k - 1])

    def side(u, ref, k, mine):
        x_first = units[u][1]
        index = (y if mine else 1 - y) if x_first else (x if mine else 1 - x)
        return ref.at[k - 1, :, index] if x_first else ref.at[k - 1, index]

    def hop(u, stage, k):
        part, recv_one, recv_two, recv_three = scratch[4 * u : 4 * u + 4]
        x_first = units[u][1]
        if stage == 1:
            return remote(u, k - 1, rows(u, k, False), recv_one.at[k - 1], to_x if x_first else to_y)
        if stage == 2:
            return remote(u, fs + k - 1, side(u, part, k, False), recv_two.at[k - 1], to_y if x_first else to_x)
        return remote(
            u, 2 * fs + k - 1, recv_two.at[k - 1], recv_three.at[k - 1], {"fsdp": lax.rem(z + k, fs)}
        )

    def second(u, k):
        part, recv_one = scratch[4 * u : 4 * u + 2]
        load(u, k).wait()
        if k + ahead > fs:
            hop(u, 1, k).wait_recv()
        spot = side(u, part, k, False)
        spot[...] = (f32(spot[...]) + f32(side(u, recv_one, k, False)[...])).astype(jnp.bfloat16)
        hop(u, 2, k).start()

    def third(u, k):
        part, recv_one, recv_two = scratch[4 * u : 4 * u + 3]
        hop(u, 2, k).wait_recv()
        total = f32(side(u, part, k, True)[...]) + f32(side(u, recv_one, k, True)[...]) + f32(recv_two[k - 1])
        if k < fs:
            recv_two[k - 1] = total.astype(jnp.bfloat16)
            hop(u, 3, k).start()
        else:
            index, _, start, width = units[u]
            totals[index][:, :, start : start + width] = total

    ahead = 2

    def begin():
        for k in range(1, fs + 1):
            for u in range(count):
                if k <= ahead:
                    hop(u, 1, k).start()
                load(u, k).start()

    def stage(k):
        if k + ahead <= fs:
            for u in range(count):
                hop(u, 1, k).wait_recv()
            for u in range(count):
                hop(u, 1, k + ahead).start()
        for u in range(count):
            if k <= fs:
                second(u, k)
        for u in range(count):
            if k > 1:
                third(u, k - 1)

    actions = [functools.partial(stage, k) for k in range(1, fs + 2)]

    def end():
        for u in range(count):
            index, _, start, width = units[u]
            total = totals[index][:, :, start : start + width]
            for k in range(1, fs):
                hop(u, 3, k).wait_recv()
                total = total + f32(scratch[4 * u + 3][k - 1])
            totals[index][:, :, start : start + width] = total
        stores = [pltpu.make_async_copy(totals[i], outs[i], out_sem.at[i]) for i in range(len(outs))]
        for cp in stores:
            cp.start()
        for u in range(count):
            for k in range(1, fs + 1):
                for number in (1, 2, 3) if k < fs else (1, 2):
                    hop(u, number, k).wait_send()
        for cp in stores:
            cp.wait()

    return begin, actions, end


def reduce_views(partials):
    fs, groups = lax.axis_size("fsdp"), lax.axis_size(DP) // 4
    return [p.reshape(2, fs, groups, 2, -1, p.shape[1]) for p in partials]


def reduce_scratch(arrays, units, swaps):
    fs, groups = lax.axis_size("fsdp"), lax.axis_size(DP) // 4
    scratch = []
    for index, x_first, _, width in units:
        q = arrays[index].shape[4]
        both = (groups, 2, q, width) if x_first else (2, groups, q, width)
        for shape in ((fs, *both), (fs, *both), (fs, groups, q, width), (fs - 1, groups, q, width)):
            scratch.append(pltpu.VMEM(shape, jnp.bfloat16))
    scratch += [pltpu.VMEM((groups, a.shape[4], a.shape[5]), jnp.float32) for a in arrays]
    return scratch + [
        pltpu.SemaphoreType.DMA((len(units), fs)),
        pltpu.SemaphoreType.DMA((len(units), 3 * fs)),
        pltpu.SemaphoreType.DMA((len(units), 3 * fs)),
        pltpu.SemaphoreType.DMA((len(arrays),)),
        pltpu.SemaphoreType.DMA((max(len(swaps), 1), 2)),
    ]


def reduce_shapes(arrays, swaps):
    groups = lax.axis_size(DP) // 4
    return [jax.ShapeDtypeStruct((groups, a.shape[4], a.shape[5]), jnp.float32) for a in arrays] + [
        jax.ShapeDtypeStruct(a.shape, a.dtype) for a in swaps
    ]


def finish_reduce(results):
    finals = []
    for total in results:
        groups, g = total.shape[0], lax.axis_index(DP) // 4
        at = lambda i: lax.dynamic_index_in_dim(total, i, 0, keepdims=False)
        mine = at(g)
        for k in range(1, groups):
            mine = mine + shift_group(at((g + k) % groups), k)
        finals.append(swap_halves(mine))
    return finals


def reduce_weights(partials, units, swaps, small, collective_id):
    fs, groups = lax.axis_size("fsdp"), lax.axis_size(DP) // 4
    arrays = reduce_views(partials)
    held = len(arrays)
    n, size = held + len(swaps), 4 * len(units)
    hops = 3 + fs - 1

    def kernel(*refs):
        ins, near, small_in = refs[:held], refs[held:n], refs[n]
        outs, far, small_out = refs[n + 1 : n + 1 + held], refs[n + 1 + held : 2 * n + 1], refs[2 * n + 1]
        rest = refs[2 * n + 2 :]
        scratch, totals = rest[:size], rest[size : size + held]
        staged, landed, small_sem = rest[size + held : size + held + 3]
        x, z, _, y, c = coords()
        enter()
        begin, actions, end = reduce_plan(units, ins, outs, scratch, totals, *refs[-5:-1])
        swapped = swap_copies(near, far, refs[-1])
        targets = [{"core": 1 - c}, {"seq": 1 - x}, {"y": lax.axis_index("y") + 1 - 2 * y}]
        targets += [{"fsdp": lax.rem(z + k, fs)} for k in range(1, fs)]

        def small_hop(i):
            return pltpu.make_async_remote_copy(
                src_ref=staged.at[min(i, 3)],
                dst_ref=landed.at[i],
                send_sem=small_sem.at[0, i],
                recv_sem=small_sem.at[1, i],
                device_id=targets[i],
                device_id_type=pl.DeviceIdType.MESH,
            )

        staged[0] = small_in[...]
        small_hop(0).start()
        begin()
        for cp in swapped:
            cp.start()
        for index, action in enumerate(actions):
            action()
            if index < 3:
                small_hop(index).wait_recv()
                staged[index + 1] = staged[index] + landed[index]
                for i in (index + 1,) if index < 2 else range(3, hops):
                    small_hop(i).start()
        end()
        total = staged[3]
        for i in range(3, hops):
            small_hop(i).wait_recv()
            total = total + landed[i]
        small_out[...] = total
        for i in range(hops):
            small_hop(i).wait_send()
        for cp in swapped:
            cp.wait()

    results = pl.pallas_call(
        kernel,
        out_shape=reduce_shapes(arrays, swaps) + [jax.ShapeDtypeStruct(small.shape, small.dtype)],
        in_specs=[pl.BlockSpec(memory_space=pl.ANY)] * n + [pl.BlockSpec(memory_space=pltpu.VMEM)],
        out_specs=[pl.BlockSpec(memory_space=pl.ANY)] * n + [pl.BlockSpec(memory_space=pltpu.VMEM)],
        scratch_shapes=(lambda base: base[: size + held]
        + [
            pltpu.VMEM((4, *small.shape), small.dtype),
            pltpu.VMEM((hops, *small.shape), small.dtype),
            pltpu.SemaphoreType.DMA((2, hops)),
        ]
        + base[size + held :])(reduce_scratch(arrays, units, swaps)),
        compiler_params=pltpu.CompilerParams(
            collective_id=collective_id, has_side_effects=True, vmem_limit_bytes=56 << 20
        ),
        name="reduce_weights",
    )(*arrays, *swaps, small)
    total = results[-1]
    if groups > 1:
        total = total + sum(shift_group(total, k) for k in range(1, groups))
    return finish_reduce(results[:held]), results[held:-1], total


def attend_back_and_reduce(qkv_i, qkv_t, o_i, o_t, d_i, d_t, lse, info, tq, partials, units, swaps, collective_id):
    ti, w3 = qkv_i.shape
    tt, w, tp = qkv_t.shape[0], w3 // 3, 256
    steps = w // 128
    arrays = reduce_views(partials)
    held = len(arrays)
    n, size = held + len(swaps), 4 * len(units)
    bi = lambda off: pl.BlockSpec((ti, 128), lambda p, j, s, off=off: (0, p + off * steps))
    bt = lambda off: pl.BlockSpec((tt, 128), lambda p, j, s, off=off: (0, p + off * steps))

    def kernel(*refs):
        info_ref, attn_in = refs[0], refs[1:12]
        ins, near = refs[12 : 12 + held], refs[12 + held : 12 + n]
        attn_out, rest = refs[12 + n : 14 + n], refs[14 + n :]
        outs, far, mine = rest[:held], rest[held:n], rest[n : n + 8]
        scratch, totals = rest[n + 8 : n + 8 + size], rest[n + 8 + size : n + 8 + size + held]
        pair, part = pl.program_id(0), pl.program_id(1)
        begin, actions, end = reduce_plan(units, ins, outs, scratch, totals, *refs[-5:-1])
        swapped = swap_copies(near, far, refs[-1])

        @pl.when((pair == 0) & (part == 0))
        def _():
            enter(core_too=False)
            begin()
            for cp in swapped:
                cp.start()

        times = (3, 6, 9, 11)
        early = min(len(times), len(actions) - 1)
        for index, at in zip(range(early), times):
            pl.when((pair == at) & (part == 0))(actions[index])
        attn_bwd_kernel(ti, tt, tq, info_ref, *attn_in, *attn_out, *mine)

        @pl.when((pair == steps - 1) & (part == 2))
        def _():
            for action in actions[early:]:
                action()
            end()
            for cp in swapped:
                cp.wait()

    results = pl.pallas_call(
        kernel,
        grid_spec=pltpu.PrefetchScalarGridSpec(
            num_scalar_prefetch=1,
            grid=(steps, 3),
            in_specs=[bi(0), bi(1), bi(2), bt(0), bt(1), bt(2), bi(0), bt(0), bi(0), bt(0)]
            + [pl.BlockSpec((1, 8, ti + tp), lambda p, j, s: (p, 0, 0))]
            + [pl.BlockSpec(memory_space=pl.ANY)] * n,
            out_specs=[
                pl.BlockSpec((ti, 128), lambda p, j, s: (0, p + j * steps)),
                pl.BlockSpec((tt, 128), lambda p, j, s: (0, p + j * steps)),
            ]
            + [pl.BlockSpec(memory_space=pl.ANY)] * n,
            scratch_shapes=[pltpu.VMEM((tp, 128), jnp.bfloat16)] * 2
            + [pltpu.VMEM((ti, 128), jnp.float32), pltpu.VMEM((tp, 128), jnp.float32)] * 2
            + [pltpu.VMEM((ti, 128), jnp.bfloat16), pltpu.VMEM((tt, 128), jnp.bfloat16)]
            + reduce_scratch(arrays, units, swaps),
        ),
        out_shape=[jax.ShapeDtypeStruct((ti, w3), jnp.bfloat16), jax.ShapeDtypeStruct((tt, w3), jnp.bfloat16)]
        + reduce_shapes(arrays, swaps),
        compiler_params=pltpu.CompilerParams(
            collective_id=collective_id, has_side_effects=True, vmem_limit_bytes=60 << 20
        ),
        name="attend_back_and_reduce",
    )(info, qkv_i, qkv_i, qkv_i, qkv_t, qkv_t, qkv_t, o_i, o_t, d_i, d_t, lse, *arrays, *swaps)
    return results[:2], finish_reduce(results[2 : 2 + held]), results[2 + held :]


def gather_offloaded(shard, stream, earlier=()):
    x, _, _, _, _ = coords()
    share = shard.shape[1] // (2 * lax.axis_size(DP))
    start = (x * lax.axis_size(DP) + lax.axis_index(DP)) * share
    piece = lax.dynamic_slice(shard, (stream, start, 0), (1, share, shard.shape[2]))[0]
    return lax.all_gather(after(piece, *earlier), ("fsdp", "seq", "y", "core"), axis=0, tiled=True)


def gather_plane(*values):
    both = jnp.concatenate(values, axis=1) if len(values) > 1 else values[0]
    both = lax.all_gather(both, ("seq", "y", "core"), axis=0, tiled=True)
    edges = [0]
    for v in values:
        edges.append(edges[-1] + v.shape[1])
    return [both[:, a:b] for a, b in zip(edges, edges[1:])]


def own_blocks(values, axis):
    fs, n = lax.axis_size("fsdp"), lax.axis_size(DP)
    size = values.shape[axis] // (2 * fs * n)
    start = (lax.axis_index("seq") * fs * n + lax.axis_index(DP)) * size
    return jnp.concatenate(
        [lax.dynamic_slice_in_dim(values, start + f * n * size, size, axis) for f in range(fs)], axis=axis
    )


def sum_fsdp(total):
    flat = total.astype(jnp.bfloat16).reshape(-1, total.shape[-1])
    mine = lax.psum_scatter(flat, "fsdp", scatter_dimension=0, tiled=True)
    return mine.reshape(total.shape[1:]).astype(jnp.float32)


def plane_total(left, right):
    total = dot(own_blocks(left, 1), right, 0, 0)
    return total.reshape(lax.axis_size("fsdp"), -1, total.shape[1]).astype(jnp.bfloat16)


def plane_mlp_grads(modded, d_mlp, weight_up, bias_up, weight_down):
    fs, n = lax.axis_size("fsdp"), lax.axis_size(DP)
    x = lax.axis_index("seq")
    hidden = linear(modded, own_blocks(weight_up, 1), own_blocks(bias_up, 0))
    active, slope = gelu_both(hidden)
    d_active = linear_back(d_mlp, own_blocks(weight_down, 0))
    d_hidden = (slope.astype(jnp.float32) * d_active).astype(jnp.bfloat16)
    down = dot(active, d_mlp, 0, 0)
    grad_down = sum_fsdp(down.reshape(fs, -1, down.shape[1]))
    up = dot(modded, d_hidden, 0, 0)
    rows, units = up.shape
    up = up.reshape(2, fs, rows // (2 * fs), units).transpose(1, 0, 2, 3)
    mine = sum_fsdp(up).reshape(rows // fs, units).astype(jnp.bfloat16)
    spread = lax.all_gather(mine, ("seq", "y", "core"), axis=0)
    spread = spread.reshape(2 * n, 2, n, rows // (2 * fs * n), units)
    spread = lax.dynamic_index_in_dim(spread, x, 1, keepdims=False)
    spread = lax.dynamic_index_in_dim(spread, lax.axis_index(DP), 1, keepdims=False)
    spread = spread.reshape(2, n, spread.shape[1], fs, -1).transpose(2, 0, 3, 1, 4)
    return grad_down, spread.reshape(spread.shape[0], -1).astype(jnp.float32)


def swap_halves(mine_rows):
    _, _, _, _, c = coords()
    rows = mine_rows.shape[0] // 2
    near = lax.dynamic_slice_in_dim(mine_rows, c * rows, rows, 0)
    far = flip_core(lax.dynamic_slice_in_dim(mine_rows, (1 - c) * rows, rows, 0))
    return jnp.concatenate([jnp.where(c == 0, near, far), jnp.where(c == 0, far, near)], axis=1)


def gather_small(value):
    fs = lax.axis_size("fsdp")
    z = lax.axis_index("fsdp")
    stack = jnp.stack([value] + [shift_z(value, k) for k in range(1, fs)])
    ordered = [lax.dynamic_index_in_dim(stack, (z - j) % fs, 0, keepdims=False) for j in range(fs)]
    return jnp.stack(ordered, axis=1)


def wgrad_kernel(sel_ref, a0, b0, a1, b1, out, a0t, a1t):
    @pl.when(pl.program_id(1) == 0)
    def _():
        a0t[...] = a0[...].T
        a1t[...] = a1[...].T

    out[...] = (dot(a0t[...], b0[...], 1, 0) + dot(a1t[...], b1[...], 1, 0)).astype(out.dtype)


def wgrad(a0, b0, a1, b1, row_half, col_half):
    tokens, rows = a0.shape
    cols = b0.shape[1]
    tr = tc = 768
    halves = 1 if row_half is None else 2
    nr, nc = rows // halves // tr, cols // 2 // tc
    row_start = jnp.int32(0) if row_half is None else row_half * nr
    a_spec = pl.BlockSpec((tokens, tr), lambda i, j, s: (0, s[0] + i))
    b_spec = pl.BlockSpec((tokens, tc), lambda i, j, s: (0, s[1] + j))
    return pl.pallas_call(
        wgrad_kernel,
        grid_spec=pltpu.PrefetchScalarGridSpec(
            num_scalar_prefetch=1,
            grid=(nr, nc),
            in_specs=[a_spec, b_spec, a_spec, b_spec],
            out_specs=pl.BlockSpec((tr, tc), lambda i, j, s: (i, j)),
            scratch_shapes=[pltpu.VMEM((tr, tokens), a0.dtype)] * 2,
        ),
        out_shape=jax.ShapeDtypeStruct((rows // halves, cols // 2), jnp.bfloat16),
        compiler_params=pltpu.CompilerParams(vmem_limit_bytes=48 << 20),
        cost_estimate=pl.CostEstimate(
            flops=2 * tokens * (rows // halves) * cols,
            bytes_accessed=2 * tokens * (rows + cols) + rows * cols,
            transcendentals=0,
        ),
        name="wgrad",
    )(jnp.stack([row_start, col_half * nc]).astype(jnp.int32), a0, b0, a1, b1)


def partial_grad(left, right, far_left, far_right):
    return wgrad(left, right, far_left, far_right, None, lax.axis_index("core"))


def local(
    image_in,
    text_in,
    modulation,
    text_len,
    w_qkv,
    b_qkv,
    w_out,
    b_out,
    w_up,
    b_up,
    w_down,
    b_down,
    d_image,
    d_text,
):
    x, z, g, y, c = coords()
    image_half, text_half = image_in.shape[1], text_in.shape[1]
    width = image_in.shape[2]
    text_rows = -(-2 * text_half // 16) * 16

    def take(arr, index=x):
        return lax.dynamic_index_in_dim(arr, index, 0, keepdims=False)

    def join(near, far, rows):
        pad = jnp.zeros((rows - 2 * near.shape[0], width), near.dtype)
        return jnp.concatenate([near, far, pad], axis=0)

    def in_order(near, far):
        return jnp.where(x == 0, jnp.stack([near, far]), jnp.stack([far, near]))

    gathered, far = gather_weights(
        [(w_qkv, 0, True), (w_qkv, 1, False)], [take(image_in, 1 - x), take(text_in, 1 - x)], 0
    )
    weight_qkv = gathered
    streams = (join(take(image_in), far[0], 2 * image_half), join(take(text_in), far[1], text_rows))
    text_weights = [gather_offloaded(w_out, 1, (weight_qkv[0],))]
    gains = take(modulation)
    info = jnp.stack([take(text_len), jnp.int32(text_half), x.astype(jnp.int32)])
    small = gather_small(jnp.concatenate([b_qkv, b_out, b_up, b_down], axis=1))
    biases, start = [], 0
    for b in (b_qkv, b_out, b_up, b_down):
        biases.append(small[:, :, start : start + b.shape[1]].reshape(2, -1).astype(jnp.float32))
        start += b.shape[1]
    bias_qkv, bias_out, bias_up, bias_down = biases

    fronts = []
    for s in range(2):
        mod = gains[s]
        normed, inverse = normalize(streams[s].astype(jnp.float32))
        modded = (normed * (1.0 + mod[1]) + mod[0]).astype(jnp.bfloat16)
        projected = linear(modded, weight_qkv[s], bias_qkv[s]).astype(jnp.bfloat16)
        fronts.append((normed, inverse, modded, projected))
    (att_i, att_t, lse), image_weights, far = attend_and_gather(
        fronts[0][3],
        fronts[1][3],
        info,
        2 * image_half,
        [(w_out, 0, True), (w_up, 0, False), (w_down, 0, True)],
        [take(d_image, 1 - x), take(d_text, 1 - x)],
        1,
    )
    cotangents = (join(take(d_image), far[0], 2 * image_half), join(take(d_text), far[1], text_rows))
    text_weights += [gather_offloaded(w, 1, (image_weights[0],)) for w in (w_up, w_down)]
    weight_out, weight_up, weight_down = zip(image_weights, text_weights)

    outs, backs, column_sums, parts = [], [], [], {}
    token = att_i
    for s in range(2):
        mod = gains[s]
        attended = after((att_i, att_t)[s], token)
        upstream = cotangents[s].astype(jnp.float32)
        d_mlp = (mod[5] * upstream).astype(jnp.bfloat16)
        branch = linear(attended, weight_out[s], bias_out[s])
        middle = streams[s].astype(jnp.float32) + mod[2] * branch
        normed_two, inverse_two = normalize(middle)
        modded_two = (normed_two * (1.0 + mod[4]) + mod[3]).astype(jnp.bfloat16)
        if s == 1:
            text_mlp = gather_plane(modded_two, d_mlp, fronts[1][2])
        hidden = linear(modded_two, weight_up[s], bias_up[s])
        active, slope = gelu_both(hidden)
        if s == 0:
            far_active, far_d_mlp = flip_core(active), flip_core(d_mlp)
        mlp_out = linear(active, weight_down[s], bias_down[s])
        outs.append((middle + mod[5] * mlp_out).astype(jnp.bfloat16))
        d_gate_two = jnp.sum(upstream * mlp_out, axis=0)
        if s == 0:
            parts["down"] = partial_grad(after(active, outs[s]), d_mlp, far_active, far_d_mlp)
            d_mlp = after(d_mlp, parts["down"])
        d_active = linear_back(d_mlp, weight_down[s])
        d_hidden = (slope.astype(jnp.float32) * d_active).astype(jnp.bfloat16)
        if s == 0:
            far_d_hidden, far_modded_two = flip_core(d_hidden), flip_core(modded_two)
        d_modded_two = linear_back(d_hidden, weight_up[s])
        d_shift_two = jnp.sum(d_modded_two, axis=0)
        d_scale_two = jnp.sum(d_modded_two * normed_two, axis=0)
        d_middle = upstream + normalize_back(normed_two, inverse_two, d_modded_two * (1.0 + mod[4]))
        d_gate_one = jnp.sum(d_middle * branch, axis=0)
        d_branch = (mod[2] * d_middle).astype(jnp.bfloat16)
        if s == 0:
            parts["up"] = partial_grad(after(modded_two, d_branch), d_hidden, far_modded_two, far_d_hidden)
            far_attended, far_d_branch = flip_core(attended), flip_core(d_branch)
            d_branch = after(d_branch, parts["up"])
        else:
            text_out = gather_plane(attended, d_branch)
        d_attended = linear_back(d_branch, weight_out[s]).astype(jnp.bfloat16)
        if s == 0:
            parts["out"] = partial_grad(after(attended, d_attended), d_branch, far_attended, far_d_branch)
            token = parts["out"]
        column_sums.append([jnp.sum(a.astype(jnp.float32), axis=0) for a in (d_branch, d_hidden, d_mlp)])
        backs.append((d_attended, d_middle, d_gate_one, d_shift_two, d_scale_two, d_gate_two))
    sent = [outs[0][image_half:], outs[1][text_half : 2 * text_half]]
    text_grads = plane_mlp_grads(text_mlp[0], after(text_mlp[1], backs[1][0]), weight_up[1], bias_up[1], weight_down[1])
    far_text_modded = text_mlp[2]
    d_front, reduced, far_outs = attend_back_and_reduce(
        fronts[0][3],
        fronts[1][3],
        att_i,
        att_t,
        backs[0][0],
        backs[1][0],
        lse,
        info,
        image_half // 2,
        [parts["down"], parts["up"], parts["out"]],
        [(0, True, 0, parts["down"].shape[1]), (1, False, 0, parts["up"].shape[1]), (2, True, 0, parts["out"].shape[1])],
        sent,
        2,
    )
    text_qkv = gather_plane(d_front[1])[0]
    text_out = [after(text_out[0], d_front[1]), text_out[1]]
    text_out_total = plane_total(*text_out)
    far_front, far_modded = flip_core(d_front[0]), flip_core(fronts[0][2])
    grads = {("down", 0): reduced[0], ("up", 0): reduced[1], ("out", 0): reduced[2]}
    input_grads, gain_grads = [], []
    for s in range(2):
        mod = gains[s]
        normed, inverse, modded, _ = fronts[s]
        d_attended, d_middle, d_gate_one, d_shift_two, d_scale_two, d_gate_two = backs[s]
        d_modded = linear_back(after(d_front[s], text_out_total), weight_qkv[s])
        d_shift_one = jnp.sum(d_modded, axis=0)
        d_scale_one = jnp.sum(d_modded * normed, axis=0)
        input_grads.append(d_middle + normalize_back(normed, inverse, d_modded * (1.0 + mod[1])))
        gain_grads.append(
            jnp.stack([d_shift_one, d_scale_one, d_gate_one, d_shift_two, d_scale_two, d_gate_two])
        )
    mine = jnp.stack(gain_grads)
    part = partial_grad(after(fronts[0][2], *input_grads), d_front[0], far_modded, far_front)
    text_qkv_total = plane_total(far_text_modded, after(text_qkv, part))
    part = after(part, text_qkv_total)
    cols = part.shape[1]
    sent = [input_grads[0][image_half:].astype(jnp.bfloat16), input_grads[1][text_half : 2 * text_half].astype(jnp.bfloat16)]
    front_sums = [jnp.sum(d_front[s].astype(jnp.float32), axis=0) for s in range(2)]
    small = jnp.concatenate([front_sums[s] for s in range(2)] + [v for s in range(2) for v in column_sums[s]])
    reduced, far_grads, small = reduce_weights(
        [part],
        [(0, True, 0, cols // 2), (0, False, cols // 2, cols // 2)],
        sent + [mine.reshape(-1, width)],
        small.reshape(-1, 128),
        3,
    )
    grads["qkv", 0] = reduced[0]
    grads["down", 1], grads["up", 1] = text_grads
    grads["out", 1] = sum_fsdp(text_out_total)
    grads["qkv", 1] = sum_fsdp(text_qkv_total)
    grad_modulation = in_order(mine, far_grads[2].reshape(mine.shape))

    count = lax.axis_size(("seq", "fsdp") + DP)
    index = lax.axis_index(("seq", "fsdp") + DP)

    def cut_bias(total):
        return lax.dynamic_index_in_dim(total.reshape(2, count, -1), index, 1, keepdims=False)

    small = small.reshape(-1)
    front = front_sums[0].shape[0]
    per_stream = small[2 * front :].reshape(2, -1)
    sizes = [a.shape[0] for a in column_sums[0]]
    gb_qkv = cut_bias(small[: 2 * front].reshape(2, front))
    gb_out, gb_up, gb_down = [
        cut_bias(a) for a in jnp.split(per_stream, [sizes[0], sizes[0] + sizes[1]], axis=1)
    ]
    grads_qkv, grads_out, grads_up, grads_down = [
        jnp.stack([grads[name, s] for s in range(2)]) for name in ("qkv", "out", "up", "down")
    ]
    halves = (image_half, text_half)
    return (
        *[in_order(outs[s][: halves[s]], far_outs[s]) for s in range(2)],
        *[in_order(input_grads[s][: halves[s]], far_grads[s].astype(jnp.float32)) for s in range(2)],
        grad_modulation,
        grads_qkv,
        gb_qkv,
        grads_out,
        gb_out,
        grads_up,
        gb_up,
        grads_down,
        gb_down,
    )


def solution(mesh):
    seq, fsdp, dp = (mesh.shape[name] for name in ("seq", "fsdp", "dp"))
    split = Mesh(mesh.devices.reshape(seq, fsdp, dp // 2, 2), ("seq", "fsdp", "y", "core"))
    batch = ("fsdp",) + DP
    tokens = P(batch, "seq", None)
    weight, bias = P(None, "fsdp", None), P(None, "fsdp")
    in_specs = (tokens, tokens, P(batch, None, None, None), P(batch))
    in_specs += (weight, bias) * 4 + (tokens, tokens)
    everywhere = ("seq",) + batch
    grad_w, grad_b = P(None, everywhere, None), P(None, everywhere)
    out_specs = (tokens,) * 4 + (P(batch, None, None, None),) + (grad_w, grad_b) * 4
    return jax.shard_map(local, mesh=split, in_specs=in_specs, out_specs=out_specs, check_vma=False)
```

time: 1880 us -> 1390 us (0.74)
  Pallas kernels: 1090 us -> 831 us
  waiting for transfers between devices: 194 us -> 33.7 us
  local copies, waits for them, and re-layouts: 132 us -> 95.3 us
  starting transfers between devices: 38.4 us -> 10.5 us
    pallas_call x6 -> x4, Pallas kernels: 1000 us -> 747 us  [the longest x1 290 us: attend_back_and_reduce(): pl.pallas_call(kernel, grid_spec=pltpu.PrefetchScalarGridSpec(num_scalar_...]
    ppermute x21 -> x3, waiting for transfers between devices: 138 us -> 0.01 us  [shift_z(): return lax.ppermute(a, 'fsdp', [(i, (i + k) % n) for i in range(n)])]
    all_gather x3, waiting for transfers between devices: 46.1 us -> 6.1 us  [gather_plane(): both = lax.all_gather(both, ('seq', 'y', 'core'), axis=0, tiled=True)]
    all_gather x1 -> x0, local copies, waits for them, and re-layouts: 24.7 us -> none  [gather_offloaded(): lax.all_gather(after(piece, *earlier), ('fsdp', 'seq', 'y', 'core'), axis...]
    reduce_scatter x0 -> x4, waiting for transfers between devices: none -> 22.1 us  [sum_fsdp(): mine = lax.psum_scatter(flat, 'fsdp', scatter_dimension=0, tiled=True)]
    ppermute x21 -> x3, starting transfers between devices: 23.3 us -> 3.74 us  [shift_z(): return lax.ppermute(a, 'fsdp', [(i, (i + k) % n) for i in range(n)])]
  transfers between devices with their start and end apart: 46 -> 26, of which waited for: 15 -> 3; matrix products, arithmetic and copies ran while one was open for 25% -> 33% of each run, Pallas kernels for 51% -> 51%
where the time goes in v3:
time: 1390 us; the launch traced here: 1380 us
  Pallas kernels  831 us (60%)
  matrix products  315 us (23%)
  local copies, waits for them, and re-layouts  95.3 us (7%)
  other arithmetic  75.2 us (5%)
  waiting for transfers between devices  33.7 us (2%)
  between operations  15.7 us (1%)
    pallas_call x1, Pallas kernels, attend_back_and_reduce(): pl.pallas_call(kernel, grid_spec=pltpu.PrefetchScalarGridSpec(num_scalar_...  290 us
    pallas_call x1, Pallas kernels, attend_and_gather(): pl.pallas_call(kernel, grid_spec=pltpu.PrefetchScalarGridSpec(num_scalar_...  179 us
    dot_general x12, matrix products, dot(): lax.dot_general(a, b, (((ca,), (cb,)), ((), ())), preferred_element_type=...  176 us
    pallas_call x1, Pallas kernels, reduce_weights(): pl.pallas_call(kernel, out_shape=reduce_shapes(arrays, swaps) + [jax.Shap...  145 us
    dot_general x9, matrix products, linear(): jnp.dot(values, weight, preferred_element_type=jnp.float32)  139 us
    pallas_call x1, Pallas kernels, gather_weights(): pl.pallas_call(kernel, out_shape=gather_shapes(units) + [jax.ShapeDtypeSt...  132 us
    pallas_call x4, Pallas kernels, wgrad(): pl.pallas_call(wgrad_kernel, grid_spec=pltpu.PrefetchScalarGridSpec(num_s...  84.7 us
    unnamed x231, local copies, waits for them, and re-layouts  28 us
  transfers between devices with their start and end apart: 26, of which 3 were waited for; matrix products, arithmetic and copies ran while one was open for 33% of the time, Pallas kernels for 51%

profile of v3, /device:TPU:9, one launch (start us, length us, event | category | flops | bytes accessed | tf_op | source)
XLA Modules:
  0.0 1376.3 jit_solution(12949421978993113172)
XLA Ops:
  20.0 132.1 %gather_weights.1 = (bf16[1536,4608]{1,0:T(8,128)(2,1)}, bf16[1536,4608]{1,0:T(8,128)(2,1)}, bf16[512,1536]{1,0:T(8,128)(2,1)S(1)}, bf16[77,1536]{1,0:T(8,128)(2,1)S(1)}) custom-call(bf16[2,384,4608]{2,1,0:T(8,128)(2,1)} %refs_1_.1, bf16[2,384,4608]{2,1,0:T(8,128)(2,1)} %refs_1_.1, bf16[512,1536]{1,0:T(8,128)(2,1)S(1)} %get-tuple-element.252.refs_2_, ...), custom_call_target="tpu_custom_call" | custom-call | tf_op jit(solution)/shard_map/gather_weights/pallas_call | solution.py:339
  179.0 8.9 fusion.25.refs_4_.refs_5_.refs_6_
  187.9 20.2 %add_convert_fusion.refs_1_.refs_2_.refs_3_ = bf16[1024,4608]{1,0:T(8,128)(2,1)} fusion(bf16[1024,1536]{1,0:T(8,128)(2,1)} %fusion.16.a0, bf16[1536,4608]{1,0:T(8,128)(2,1)} %get-tuple-element.54, f32[4608]{0:T(1024)S(1)} %add.507), kind=kOutput, calls=%fused_computation.15 | convolution fusion | flops 14504951808 | bytes 26757120 | tf_op jit(solution)/shard_map/dot_general | solution.py:123
  208.1 179.2 %attend_and_gather.1 = (bf16[1024,1536]{1,0:T(8,128)(2,1)}, bf16[160,1536]{1,0:T(8,128)(2,1)}, f32[12,8,1280]{2,1,0:T(8,128)}, bf16[1536,1536]{1,0:T(8,128)(2,1)...) custom-call(s32[3]{0:T(128)} %pad_add_fusion.3.refs_0_, ...), custom_call_target="tpu_custom_call" | custom-call | tf_op jit(solution)/shard_map/attend_and_gather/pallas_call | solution.py:390
  388.0 10.7 fusion.149
  402.1 33.1 %multiply_convert_fusion.1 = (bf16[1024,6144]{1,0:T(8,128)(2,1)}, f32[1024,6144]{1,0:T(8,128)}) fusion(f32[6144]{0:T(1024)S(1)} %bitcast.194, bf16[1024,1536]{1,0:T(8,128)(2,1)S(1)} %add_convert_fusion.2.a0, bf16[1536,6144]{1,0:T(8,128)(2,1)} %get-tuple-element.60), kind=kOutput, calls=%fused_computation.12 | convolution fusion | flops 19390267392 | bytes 59793408 | tf_op jit(solution)/shard_map/dot_general | solution.py:123
  437.5 29.9 %fusion.24 = (f32[1536]{0:T(1024)}, bf16[1024,1536]{1,0:T(8,128)(2,1)}, bf16[1024,1536]{1,0:T(8,128)(2,1)S(1)}) fusion(f32[1536]{0:T(1024)S(1)} %add.534, bf16[512,1536]{1,0:T(8,128)(2,1)S(1)} %copy-done.34, bf16[512,1536]{1,0:T(8,128)(2,1)S(1)} %copy-done.20, f32[1024,1536]{1,0:T(8,128)} %copy-done.14, f32[1536]{0:T(1024)S(1)} %copy-done.95, ...), kind=kOutput, calls=%fused_computation.40 | convolution fusion | flops 19346225152 | bytes 47204352 | tf_op jit(solution)/shard_map/dot_general | solution.py:123
  474.7 25.4 %wgrad.4 = bf16[6144,768]{1,0:T(8,128)(2,1)} custom-call(s32[2]{0:T(128)S(1)} %pad_add_fusion.2.sel_ref, bf16[1024,6144]{1,0:T(8,128)(2,1)} %get-tuple-element.64.a0, bf16[1024,1536]{1,0:T(8,128)(2,1)S(1)} %get-tuple-element.65.b0, bf16[1024,6144]{1,0:T(8,128)(2,1)} %collective-permute-done.3.a1, bf16[1024,1536]{1,0:T(8,128)(2,1)} %copy-done.102), custom_call_target="tpu_custom_call" | custom-call | flops 19327352832 | bytes 25165824 | tf_op jit(solution)/shard_map/wgrad/pallas_call | solution.py:803
  500.2 41.7 %convert_reduce_fusion = (f32[6144]{0:T(1024)}, bf16[1024,6144]{1,0:T(8,128)(2,1)}) fusion(bf16[1024,1536]{1,0:T(8,128)(2,1)} %copy-done.6, bf16[6144,1536]{1,0:T(8,128)(2,1)} %get-tuple-element.61, f32[1024,6144]{1,0:T(8,128)} %get-tuple-element.242, f32[6144]{0:T(1024)S(1)} %bitcast.195), kind=kOutput, calls=%fused_computation.10 | convolution fusion | flops 19478341632 | bytes 59817984 | tf_op jit(solution)/shard_map/dot_general | solution.py:14
  542.9 30.7 %multiply_reduce_fusion = (f32[1536]{0:T(1024)S(1)}, f32[1024]{0:T(1024)S(1)}, f32[1024]{0:T(1024)S(1)}, f32[1536]{0:T(1024)S(1)}, f32[1024,1536]{1,0:T(8,128)}) fusion(f32[1024,1536]{1,0:T(8,128)} %copy-done.14, f32[1024]{0:T(1024)S(1)} %copy-done.69, f32[1024]{0:T(1024)S(1)} %copy-done.65, f32[1536]{0:T(1024)S(1)} %copy-done.61, ...), kind=kOutput, calls=%fused_computation.44 | convolution fusion | flops 19341502464 | bytes 44075008 | tf_op jit(solution)/shard_map/dot_general | solution.py:14
  573.6 10.5 multiply_reduce_fusion.1
  591.6 28.1 %wgrad.5 = bf16[1536,3072]{1,0:T(8,128)(2,1)} custom-call(s32[2]{0:T(128)S(1)} %pad_add_fusion.1.sel_ref, bf16[1024,1536]{1,0:T(8,128)(2,1)S(1)} %copy-done.9, bf16[1024,6144]{1,0:T(8,128)(2,1)} %get-tuple-element.249.b0, bf16[1024,1536]{1,0:T(8,128)(2,1)} %collective-permute-done.5.a1, bf16[1024,6144]{1,0:T(8,128)(2,1)} %collective-permute-done.6.b1), custom_call_target="tpu_custom_call" | custom-call | flops 19327352832 | bytes 25165824 | tf_op jit(solution)/shard_map/wgrad/pallas_call | solution.py:803
  619.7 8.8 convolution_convert_fusion.1.refs_9_
  646.2 11.8 convolution_add_fusion
  658.0 11.3 convolution_add_fusion.4
  669.3 11.9 convert_reduce_fusion.5
  681.2 12.2 multiply_reduce_fusion.6
  727.1 15.0 %fusion.47 = bf16[1536,768]{1,0:T(8,128)(2,1)} fusion(bf16[1280,4608]{1,0:T(8,128)(2,1)} %all-gather.17.cloned.1.call-done, bf16[1280,1536]{1,0:T(8,128)(2,1)} %get-tuple-element.91, bf16[192,1536]{1,0:T(8,128)(2,1)} %get-tuple-element.183, bf16[192,1536]{1,0:T(8,128)(2,1)} %get-tuple-element.184, bf16[192,1536]{1,0:T(8,128)(2,1)} %get-tuple-element.185, ...), kind=kOutput, calls=%fused_computation.90 | convolution fusion | flops 6071058432 | bytes 16515072 | tf_op jit(solution)/shard_map/dot_general | solution.py:14
  749.3 289.8 %attend_back_and_reduce.1 = (bf16[1024,4608]{1,0:T(8,128)(2,1)}, bf16[160,4608]{1,0:T(8,128)(2,1)}, f32[1,384,768]{2,1,0:T(8,128)}, f32[1,96,3072]{2,1,0:T(8,128...) custom-call(s32[3]{0:T(128)} %pad_add_fusion.3.refs_0_, ...), custom_call_target="tpu_custom_call" | custom-call | tf_op jit(solution)/shard_map/attend_back_and_reduce/pallas_call | solution.py:683
  1092.4 21.9 %fusion.21 = (f32[1536]{0:T(1024)S(1)}, f32[1024]{0:T(1024)S(1)}, f32[1024]{0:T(1024)S(1)}, f32[1536]{0:T(1024)S(1)}, f32[1024,1536]{1,0:T(8,128)S(1)}) fusion(f32[1024]{0:T(1024)S(1)} %copy-done.67, f32[1024]{0:T(1024)S(1)} %copy-done.63, bf16[512,1536]{1,0:T(8,128)(2,1)S(1)} %copy-done.1, bf16[512,1536]{1,0:T(8,128)(2,1)S(1)} %copy-done.17, ...), kind=kOutput, calls=%fused_computation.37 | convolution fusion | flops 14515955712 | bytes 33064960 | tf_op jit(solution)/shard_map/dot_general | solution.py:14
  1124.4 11.2 fusion.90
  1137.0 22.9 %wgrad.7 = bf16[1536,2304]{1,0:T(8,128)(2,1)} custom-call(s32[2]{0:T(128)S(1)} %pad_add_fusion.sel_ref, bf16[1024,1536]{1,0:T(8,128)(2,1)} %fusion.16.a0, bf16[1024,4608]{1,0:T(8,128)(2,1)} %get-tuple-element.80.b0, bf16[1024,1536]{1,0:T(8,128)(2,1)} %collective-permute-done.9.a1, bf16[1024,4608]{1,0:T(8,128)(2,1)} %collective-permute-done.10.b1), custom_call_target="tpu_custom_call" | custom-call | flops 14495514624 | bytes 19660800 | tf_op jit(solution)/shard_map/wgrad/pallas_call | solution.py:803
  1160.9 145.5 %reduce_weights.1 = (f32[1,96,2304]{2,1,0:T(8,128)}, bf16[512,1536]{1,0:T(8,128)(2,1)}, bf16[77,1536]{1,0:T(8,128)(2,1)}, f32[12,1536]{1,0:T(8,128)}, f32[216,128]{1,0:T(8,128)}) custom-call(bf16[2,4,1,2,96,2304]{5,4,3,2,1,0:T(8,128)(2,1)} %bitcast.171, bf16[512,1536]{1,0:T(8,128)(2,1)} %slice.259.refs_1_, bf16[77,1536]{1,0:T(8,128)(2,1)} %slice.260.refs_2_, ...), custom_call_target="tpu_custom_call" | custom-call | tf_op jit(solution)/shard_map/reduce_weights/pallas_call | solution.py:619
  1345.0 22.1 %reduce-scatter.5.cloned.1.call-done = bf16[48,4608]{1,0:T(8,128)(2,1)} async-done(((bf16[192,4608]{1,0:T(8,128)(2,1)}), bf16[48,4608]{1,0:T(8,128)(2,1)}) %reduce-scatter.5.cloned.1.call-update) | async-done | bytes 442384 | tf_op jit(solution)/shard_map/reduce_scatter | solution.py:739
  (444 shorter events, 225.7 us)
Async XLA Ops:
  7.2 631.1 %all-gather.9.cloned.1.call-start = ((), (), s32[]{:S(2)}) async-start(), calls=%async_computation.4 | async-start | bytes 4866048 | tf_op jit(solution)/shard_map/all_gather | solution.py:716
  152.2 494.0 %all-gather.11.cloned.1.call-start = ((), (), s32[]{:S(2)}) async-start(), calls=%async_computation.5 | async-start | bytes 19464192 | tf_op jit(solution)/shard_map/all_gather | solution.py:716
  156.4 21.4 %collective-permute-start.2 = (bf16[2,3456]{1,0:T(2,128)(2,1)}, bf16[2,3456]{1,0:T(2,128)(2,1)}, u32[]{:S(2)}, u32[]{:S(2)}) collective-permute-start(bf16[2,3456]{1,0:T(2,128)(2,1)} %constant_dynamic-update-slice_fusion), channel_id=1, source_target_pairs={{0,12},{4,0},{8,4},{12,8},{1,13},{5,1},{9,5},{13,9},{2,14},{6,2},{... | collective-permute-start | bytes 41480 | tf_op jit(solution)/shard_map/ppermute | solution.py:159
  157.5 20.3 %collective-permute-start.1 = (bf16[2,3456]{1,0:T(2,128)(2,1)}, bf16[2,3456]{1,0:T(2,128)(2,1)}, u32[]{:S(2)}, u32[]{:S(2)}) collective-permute-start(bf16[2,3456]{1,0:T(2,128)(2,1)} %constant_dynamic-update-slice_fusion), channel_id=1, source_target_pairs={{0,8},{4,12},{8,0},{12,4},{1,9},{5,13},{9,1},{13,5},{2,10},{6,14},... | collective-permute-start | bytes 41480 | tf_op jit(solution)/shard_map/ppermute | solution.py:159
  387.3 270.7 %all-gather.13.cloned.1.call-start = ((), (), s32[]{:S(2)}) async-start(), calls=%async_computation.6 | async-start | bytes 19464192 | tf_op jit(solution)/shard_map/all_gather | solution.py:716
  435.3 37.8 %collective-permute-start.3 = (bf16[1024,6144]{1,0:T(8,128)(2,1)}, bf16[1024,6144]{1,0:T(8,128)(2,1)}, u32[]{:S(2)}, u32[]{:S(2)}) collective-permute-start(bf16[1024,6144]{1,0:T(8,128)(2,1)} %get-tuple-element.64.a0), channel_id=1, source_target_pairs={{0,1},{1,0},{2,3},{3,2},{4,5},{5,4},{6,7},{7,6},{8,9},{9,8},{10,11... | collective-permute-start | bytes 37748744 | tf_op jit(solution)/shard_map/ppermute | solution.py:154
  437.4 276.5 %all-gather.17.cloned.1.call-start = ((), (), s32[]{:S(2)}) async-start(), calls=%async_computation.8 | async-start | bytes 13271040 | tf_op jit(solution)/shard_map/all_gather | solution.py:721
  541.9 47.7 %collective-permute-start.6 = (bf16[1024,6144]{1,0:T(8,128)(2,1)}, bf16[1024,6144]{1,0:T(8,128)(2,1)}, u32[]{:S(2)}, u32[]{:S(2)}) collective-permute-start(bf16[1024,6144]{1,0:T(8,128)(2,1)} %get-tuple-element.249.b0), channel_id=1, source_target_pairs={{0,1},{1,0},{2,3},{3,2},{4,5},{5,4},{6,7},{7,6},{8,9},{9,8},{10,11... | collective-permute-start | bytes 37748744 | tf_op jit(solution)/shard_map/ppermute | solution.py:154
  542.3 47.3 %collective-permute-start.5 = (bf16[1024,1536]{1,0:T(8,128)(2,1)}, bf16[1024,1536]{1,0:T(8,128)(2,1)}, u32[]{:S(2)}, u32[]{:S(2)}) collective-permute-start(bf16[1024,1536]{1,0:T(8,128)(2,1)} %copy-done.8), channel_id=1, source_target_pairs={{0,1},{1,0},{2,3},{3,2},{4,5},{5,4},{6,7},{7,6},{8,9},{9,8},{10,11... | collective-permute-start | bytes 9437192 | tf_op jit(solution)/shard_map/ppermute | solution.py:154
  542.5 86.0 %collective-permute-start.7 = (bf16[1024,1536]{1,0:T(8,128)(2,1)S(1)}, bf16[1024,1536]{1,0:T(8,128)(2,1)}, u32[]{:S(2)}, u32[]{:S(2)}) collective-permute-start(bf16[1024,1536]{1,0:T(8,128)(2,1)S(1)} %copy-done.5), channel_id=1, source_target_pairs={{0,1},{1,0},{2,3},{3,2},{4,5},{5,4},{6,7},{7,6},{8,9},{9,8},{10,11... | collective-permute-start | bytes 9437192 | tf_op jit(solution)/shard_map/ppermute | solution.py:154
  587.8 40.7 %collective-permute-start.8 = (bf16[1024,1536]{1,0:T(8,128)(2,1)}, bf16[1024,1536]{1,0:T(8,128)(2,1)}, u32[]{:S(2)}, u32[]{:S(2)}) collective-permute-start(bf16[1024,1536]{1,0:T(8,128)(2,1)} %multiply_convert_fusion.2.b0), channel_id=1, source_target_pairs={{0,1},{1,0},{2,3},{3,2},{4,5},{5,4},{6,7},{7,6},{8,9},{9,8},{10,11... | collective-permute-start | bytes 9437192 | tf_op jit(solution)/shard_map/ppermute | solution.py:154
  645.6 439.7 %all-gather.15.cloned.1.call-start = ((), (), s32[]{:S(2)}) async-start(), calls=%async_computation.7 | async-start | bytes 8847360 | tf_op jit(solution)/shard_map/all_gather | solution.py:721
  696.7 427.3 %reduce-scatter.9.cloned.1.call-start = ((), (), s32[]{:S(2)}) async-start(), calls=%async_computation.12 | async-start | bytes 2949120 | tf_op jit(solution)/shard_map/reduce_scatter | solution.py:739
  746.2 577.0 %all-gather.19.cloned.1.call-start = ((), (), s32[]{:S(2)}) async-start(), calls=%async_computation.9 | async-start | bytes 13271040 | tf_op jit(solution)/shard_map/all_gather | solution.py:721
  1039.1 292.4 %reduce-scatter.11.cloned.1.call-start = ((), (), s32[]{:S(2)}) async-start(), calls=%async_computation.13 | async-start | bytes 2949120 | tf_op jit(solution)/shard_map/reduce_scatter | solution.py:739
  1039.4 97.7 %collective-permute-start.9 = (bf16[1024,1536]{1,0:T(8,128)(2,1)}, bf16[1024,1536]{1,0:T(8,128)(2,1)}, u32[]{:S(2)}, u32[]{:S(2)}) collective-permute-start(bf16[1024,1536]{1,0:T(8,128)(2,1)} %fusion.16.a0), channel_id=1, source_target_pairs={{0,1},{1,0},{2,3},{3,2},{4,5},{5,4},{6,7},{7,6},{8,9},{9,8},{10,11... | collective-permute-start | bytes 9437192 | tf_op jit(solution)/shard_map/ppermute | solution.py:154
  1050.9 86.1 %collective-permute-start.10 = (bf16[1024,4608]{1,0:T(8,128)(2,1)}, bf16[1024,4608]{1,0:T(8,128)(2,1)}, u32[]{:S(2)}, u32[]{:S(2)}) collective-permute-start(bf16[1024,4608]{1,0:T(8,128)(2,1)} %get-tuple-element.80.b0), channel_id=1, source_target_pairs={{0,1},{1,0},{2,3},{3,2},{4,5},{5,4},{6,7},{7,6},{8,9},{9,8},{10,11... | collective-permute-start | bytes 28311560 | tf_op jit(solution)/shard_map/ppermute | solution.py:154
  1053.7 21.8 %collective-permute-start.12 = (f32[48,768]{1,0:T(8,128)}, f32[48,768]{1,0:T(8,128)}, u32[]{:S(2)}, u32[]{:S(2)}) collective-permute-start(f32[48,768]{1,0:T(8,128)} %dynamic-slice_bitcast_fusion.9), channel_id=1, source_target_pairs={{0,1},{1,0},{2,3},{3,2},{4,5},{5,4},{6,7},{7,6},{8,9},{9,8},{10,11... | collective-permute-start | bytes 442376 | tf_op jit(solution)/shard_map/ppermute | solution.py:154
  1056.1 21.2 %collective-permute-start.13 = (f32[48,3072]{1,0:T(8,128)}, f32[48,3072]{1,0:T(8,128)}, u32[]{:S(2)}, u32[]{:S(2)}) collective-permute-start(f32[48,3072]{1,0:T(8,128)} %dynamic-slice_bitcast_fusion.5), channel_id=1, source_target_pairs={{0,1},{1,0},{2,3},{3,2},{4,5},{5,4},{6,7},{7,6},{8,9},{9,8},{10,11... | collective-permute-start | bytes 1769480 | tf_op jit(solution)/shard_map/ppermute | solution.py:154
  1058.0 20.4 %collective-permute-start.14 = (f32[192,768]{1,0:T(8,128)}, f32[192,768]{1,0:T(8,128)}, u32[]{:S(2)}, u32[]{:S(2)}) collective-permute-start(f32[192,768]{1,0:T(8,128)} %dynamic-slice_bitcast_fusion.4), channel_id=1, source_target_pairs={{0,1},{1,0},{2,3},{3,2},{4,5},{5,4},{6,7},{7,6},{8,9},{9,8},{10,11... | collective-permute-start | bytes 1769480 | tf_op jit(solution)/shard_map/ppermute | solution.py:154
  1069.0 266.5 %reduce-scatter.7.cloned.1.call-start = ((), (), s32[]{:S(2)}) async-start(), calls=%async_computation.11 | async-start | bytes 737280 | tf_op jit(solution)/shard_map/reduce_scatter | solution.py:739
  1092.3 245.1 %all-gather.21.cloned.1.call-start = ((), (), s32[]{:S(2)}) async-start(), calls=%async_computation.14 | async-start | bytes 5308416 | tf_op jit(solution)/shard_map/all_gather | solution.py:761
  1124.1 243.0 %reduce-scatter.5.cloned.1.call-start = ((), (), s32[]{:S(2)}) async-start(), calls=%async_computation.10 | async-start | bytes 2211840 | tf_op jit(solution)/shard_map/reduce_scatter | solution.py:739
  1311.8 22.7 %collective-permute-start.11 = (f32[48,2304]{1,0:T(8,128)S(1)}, f32[48,2304]{1,0:T(8,128)S(1)}, u32[]{:S(2)}, u32[]{:S(2)}) collective-permute-start(f32[48,2304]{1,0:T(8,128)S(1)} %dynamic-slice_bitcast_fusion.8), channel_id=1, source_target_pairs={{0,1},{1,0},{2,3},{3,2},{4,5},{5,4},{6,7},{7,6},{8,9},{9,8},{10,11... | collective-permute-start | bytes 1327112 | tf_op jit(solution)/shard_map/ppermute | solution.py:154
  (109 other events, 2890.0 us)
Sparse Core Ops, SparseCore 0:
  152.3 63.0 all-gather.8
  387.4 122.8 all-gather.10
  513.8 122.8 all-gather.12
  645.7 68.0 all-gather.16
  715.6 61.9 all-gather.14
  779.8 46.1 reduce-scatter.8
  1039.3 69.0 all-gather.18
  1111.2 45.2 reduce-scatter.10
  1159.4 20.2 reduce-scatter.6
  1181.4 60.2 all-gather.20
  1331.6 35.4 reduce-scatter.4

commit v4 on v3

--- a/solution.py
+++ b/solution.py
@@ -134,6 +134,10 @@
     return (values * half).astype(jnp.bfloat16), slope.astype(jnp.bfloat16)
 
 
+def column_sum(values):
+    return dot(jnp.ones((8, values.shape[0]), values.dtype), values, 1, 0)[0]
+
+
 DP = ("y", "core")
 
 
@@ -415,7 +419,7 @@
 def reduce_plan(units, ins, outs, scratch, totals, load_sem, send_sem, recv_sem, out_sem):
     fs = lax.axis_size("fsdp")
     count = len(units)
-    x, z, _, y, _ = coords()
+    x, z, _, y, c = coords()
     to_x, to_y = {"seq": 1 - x}, {"y": lax.axis_index("y") + 1 - 2 * y}
     f32 = lambda a: a.astype(jnp.float32)
 
@@ -434,8 +438,8 @@
         zz = lax.rem(z + k, fs)
         cols = pl.ds(start, width)
         if x_first:
-            return ins[index].at[x if mine else 1 - x, zz, :, :, :, cols]
-        return ins[index].at[:, zz, :, y if mine else 1 - y, :, cols]
+            return ins[index].at[x if mine else 1 - x, zz, :, :, :, :, cols]
+        return ins[index].at[:, zz, :, y if mine else 1 - y, :, :, cols]
 
     def load(u, k):
         return pltpu.make_async_copy(rows(u, k, True), scratch[4 * u].at[k - 1], load_sem.at[u, k - 1])
@@ -474,9 +478,9 @@
             hop(u, 3, k).start()
         else:
             index, _, start, width = units[u]
-            totals[index][:, :, start : start + width] = total
-
-    ahead = 2
+            totals[index][:, :, :, start : start + width] = total
+
+    ahead = 1
 
     def begin():
         for k in range(1, fs + 1):
@@ -503,19 +507,33 @@
     def end():
         for u in range(count):
             index, _, start, width = units[u]
-            total = totals[index][:, :, start : start + width]
+            total = totals[index][:, :, :, start : start + width]
             for k in range(1, fs):
                 hop(u, 3, k).wait_recv()
                 total = total + f32(scratch[4 * u + 3][k - 1])
-            totals[index][:, :, start : start + width] = total
-        stores = [pltpu.make_async_copy(totals[i], outs[i], out_sem.at[i]) for i in range(len(outs))]
-        for cp in stores:
+            totals[index][:, :, :, start : start + width] = total
+        stores, sends = [], []
+        for i, (total, out) in enumerate(zip(totals, outs)):
+            h = total.shape[-1]
+            place = out.at[:, :, pl.ds(pl.multiple_of(c * h, 128), h)]
+            stores.append(pltpu.make_async_copy(total.at[:, c], place, out_sem.at[i, 0]))
+            sends.append(
+                pltpu.make_async_remote_copy(
+                    src_ref=total.at[:, 1 - c],
+                    dst_ref=place,
+                    send_sem=out_sem.at[i, 1],
+                    recv_sem=out_sem.at[i, 2],
+                    device_id={"core": 1 - c},
+                    device_id_type=pl.DeviceIdType.MESH,
+                )
+            )
+        for cp in stores + sends:
             cp.start()
         for u in range(count):
             for k in range(1, fs + 1):
                 for number in (1, 2, 3) if k < fs else (1, 2):
                     hop(u, number, k).wait_send()
-        for cp in stores:
+        for cp in stores + sends:
             cp.wait()
 
     return begin, actions, end
@@ -523,30 +541,31 @@
 
 def reduce_views(partials):
     fs, groups = lax.axis_size("fsdp"), lax.axis_size(DP) // 4
-    return [p.reshape(2, fs, groups, 2, -1, p.shape[1]) for p in partials]
+    return [p.reshape(2, fs, groups, 2, 2, -1, p.shape[1]) for p in partials]
 
 
 def reduce_scratch(arrays, units, swaps):
     fs, groups = lax.axis_size("fsdp"), lax.axis_size(DP) // 4
     scratch = []
     for index, x_first, _, width in units:
-        q = arrays[index].shape[4]
-        both = (groups, 2, q, width) if x_first else (2, groups, q, width)
-        for shape in ((fs, *both), (fs, *both), (fs, groups, q, width), (fs - 1, groups, q, width)):
+        rows = arrays[index].shape[5]
+        both = (groups, 2, 2, rows, width) if x_first else (2, groups, 2, rows, width)
+        one = (groups, 2, rows, width)
+        for shape in ((fs, *both), (fs, *both), (fs, *one), (fs - 1, *one)):
             scratch.append(pltpu.VMEM(shape, jnp.bfloat16))
-    scratch += [pltpu.VMEM((groups, a.shape[4], a.shape[5]), jnp.float32) for a in arrays]
+    scratch += [pltpu.VMEM((groups, 2, *a.shape[5:]), jnp.float32) for a in arrays]
     return scratch + [
         pltpu.SemaphoreType.DMA((len(units), fs)),
         pltpu.SemaphoreType.DMA((len(units), 3 * fs)),
         pltpu.SemaphoreType.DMA((len(units), 3 * fs)),
-        pltpu.SemaphoreType.DMA((len(arrays),)),
+        pltpu.SemaphoreType.DMA((len(arrays), 3)),
         pltpu.SemaphoreType.DMA((max(len(swaps), 1), 2)),
     ]
 
 
 def reduce_shapes(arrays, swaps):
     groups = lax.axis_size(DP) // 4
-    return [jax.ShapeDtypeStruct((groups, a.shape[4], a.shape[5]), jnp.float32) for a in arrays] + [
+    return [jax.ShapeDtypeStruct((groups, a.shape[5], 2 * a.shape[6]), jnp.float32) for a in arrays] + [
         jax.ShapeDtypeStruct(a.shape, a.dtype) for a in swaps
     ]
 
@@ -559,11 +578,11 @@
         mine = at(g)
         for k in range(1, groups):
             mine = mine + shift_group(at((g + k) % groups), k)
-        finals.append(swap_halves(mine))
+        finals.append(mine)
     return finals
 
 
-def reduce_weights(partials, units, swaps, small, collective_id):
+def reduce_weights(partials, units, swaps, small, earlier, collective_id):
     fs, groups = lax.axis_size("fsdp"), lax.axis_size(DP) // 4
     arrays = reduce_views(partials)
     held = len(arrays)
@@ -572,6 +591,7 @@
 
     def kernel(*refs):
         ins, near, small_in = refs[:held], refs[held:n], refs[n]
+        refs = refs[: n + 1] + refs[n + 1 + len(earlier) :]
         outs, far, small_out = refs[n + 1 : n + 1 + held], refs[n + 1 + held : 2 * n + 1], refs[2 * n + 1]
         rest = refs[2 * n + 2 :]
         scratch, totals = rest[:size], rest[size : size + held]
@@ -619,7 +639,9 @@
     results = pl.pallas_call(
         kernel,
         out_shape=reduce_shapes(arrays, swaps) + [jax.ShapeDtypeStruct(small.shape, small.dtype)],
-        in_specs=[pl.BlockSpec(memory_space=pl.ANY)] * n + [pl.BlockSpec(memory_space=pltpu.VMEM)],
+        in_specs=[pl.BlockSpec(memory_space=pl.ANY)] * n
+        + [pl.BlockSpec(memory_space=pltpu.VMEM)]
+        + [pl.BlockSpec(memory_space=pl.ANY)] * len(earlier),
         out_specs=[pl.BlockSpec(memory_space=pl.ANY)] * n + [pl.BlockSpec(memory_space=pltpu.VMEM)],
         scratch_shapes=(lambda base: base[: size + held]
         + [
@@ -632,14 +654,14 @@
             collective_id=collective_id, has_side_effects=True, vmem_limit_bytes=56 << 20
         ),
         name="reduce_weights",
-    )(*arrays, *swaps, small)
+    )(*arrays, *swaps, small, *earlier)
     total = results[-1]
     if groups > 1:
         total = total + sum(shift_group(total, k) for k in range(1, groups))
     return finish_reduce(results[:held]), results[held:-1], total
 
 
-def attend_back_and_reduce(qkv_i, qkv_t, o_i, o_t, d_i, d_t, lse, info, tq, partials, units, swaps, collective_id):
+def attend_back_and_reduce(qkv_i, qkv_t, o_i, o_t, d_i, d_t, lse, info, tq, partials, units, swaps, earlier, collective_id):
     ti, w3 = qkv_i.shape
     tt, w, tp = qkv_t.shape[0], w3 // 3, 256
     steps = w // 128
@@ -652,6 +674,7 @@
     def kernel(*refs):
         info_ref, attn_in = refs[0], refs[1:12]
         ins, near = refs[12 : 12 + held], refs[12 + held : 12 + n]
+        refs = refs[: 12 + n] + refs[12 + n + len(earlier) :]
         attn_out, rest = refs[12 + n : 14 + n], refs[14 + n :]
         outs, far, mine = rest[:held], rest[held:n], rest[n : n + 8]
         scratch, totals = rest[n + 8 : n + 8 + size], rest[n + 8 + size : n + 8 + size + held]
@@ -661,12 +684,12 @@
 
         @pl.when((pair == 0) & (part == 0))
         def _():
-            enter(core_too=False)
+            enter()
             begin()
             for cp in swapped:
                 cp.start()
 
-        times = (3, 6, 9, 11)
+        times = (2, 4, 7, 10)
         early = min(len(times), len(actions) - 1)
         for index, at in zip(range(early), times):
             pl.when((pair == at) & (part == 0))(actions[index])
@@ -687,7 +710,7 @@
             grid=(steps, 3),
             in_specs=[bi(0), bi(1), bi(2), bt(0), bt(1), bt(2), bi(0), bt(0), bi(0), bt(0)]
             + [pl.BlockSpec((1, 8, ti + tp), lambda p, j, s: (p, 0, 0))]
-            + [pl.BlockSpec(memory_space=pl.ANY)] * n,
+            + [pl.BlockSpec(memory_space=pl.ANY)] * (n + len(earlier)),
             out_specs=[
                 pl.BlockSpec((ti, 128), lambda p, j, s: (0, p + j * steps)),
                 pl.BlockSpec((tt, 128), lambda p, j, s: (0, p + j * steps)),
@@ -704,7 +727,7 @@
             collective_id=collective_id, has_side_effects=True, vmem_limit_bytes=60 << 20
         ),
         name="attend_back_and_reduce",
-    )(info, qkv_i, qkv_i, qkv_i, qkv_t, qkv_t, qkv_t, o_i, o_t, d_i, d_t, lse, *arrays, *swaps)
+    )(info, qkv_i, qkv_i, qkv_i, qkv_t, qkv_t, qkv_t, o_i, o_t, d_i, d_t, lse, *arrays, *swaps, *earlier)
     return results[:2], finish_reduce(results[2 : 2 + held]), results[2 + held :]
 
 
@@ -734,10 +757,17 @@
     )
 
 
-def sum_fsdp(total):
-    flat = total.astype(jnp.bfloat16).reshape(-1, total.shape[-1])
-    mine = lax.psum_scatter(flat, "fsdp", scatter_dimension=0, tiled=True)
-    return mine.reshape(total.shape[1:]).astype(jnp.float32)
+def sum_fsdp(*totals):
+    fs = totals[0].shape[0]
+    width = totals[0].shape[-1]
+    flat = jnp.concatenate([t.astype(jnp.bfloat16).reshape(fs, -1, width) for t in totals], axis=1)
+    mine = lax.psum_scatter(flat.reshape(-1, width), "fsdp", scatter_dimension=0, tiled=True)
+    result, start = [], 0
+    for t in totals:
+        rows = t.size // (fs * width)
+        result.append(mine[start : start + rows].reshape(t.shape[1:]))
+        start += rows
+    return result
 
 
 def plane_total(left, right):
@@ -745,33 +775,28 @@
     return total.reshape(lax.axis_size("fsdp"), -1, total.shape[1]).astype(jnp.bfloat16)
 
 
-def plane_mlp_grads(modded, d_mlp, weight_up, bias_up, weight_down):
-    fs, n = lax.axis_size("fsdp"), lax.axis_size(DP)
-    x = lax.axis_index("seq")
+def plane_mlp_totals(modded, d_mlp, weight_up, bias_up, weight_down):
+    fs = lax.axis_size("fsdp")
     hidden = linear(modded, own_blocks(weight_up, 1), own_blocks(bias_up, 0))
     active, slope = gelu_both(hidden)
     d_active = linear_back(d_mlp, own_blocks(weight_down, 0))
     d_hidden = (slope.astype(jnp.float32) * d_active).astype(jnp.bfloat16)
-    down = dot(active, d_mlp, 0, 0)
-    grad_down = sum_fsdp(down.reshape(fs, -1, down.shape[1]))
-    up = dot(modded, d_hidden, 0, 0)
+    down = dot(active, d_mlp, 0, 0).astype(jnp.bfloat16)
+    up = dot(modded, d_hidden, 0, 0).astype(jnp.bfloat16)
     rows, units = up.shape
     up = up.reshape(2, fs, rows // (2 * fs), units).transpose(1, 0, 2, 3)
-    mine = sum_fsdp(up).reshape(rows // fs, units).astype(jnp.bfloat16)
-    spread = lax.all_gather(mine, ("seq", "y", "core"), axis=0)
-    spread = spread.reshape(2 * n, 2, n, rows // (2 * fs * n), units)
-    spread = lax.dynamic_index_in_dim(spread, x, 1, keepdims=False)
+    return down.reshape(fs, -1, down.shape[1]), up
+
+
+def spread_up(mine):
+    fs, n = lax.axis_size("fsdp"), lax.axis_size(DP)
+    _, rows, units = mine.shape
+    spread = lax.all_gather(mine.reshape(-1, units), ("seq", "y", "core"), axis=0, tiled=True)
+    spread = spread.reshape(2 * n, 2, n, rows // n, units)
+    spread = lax.dynamic_index_in_dim(spread, lax.axis_index("seq"), 1, keepdims=False)
     spread = lax.dynamic_index_in_dim(spread, lax.axis_index(DP), 1, keepdims=False)
     spread = spread.reshape(2, n, spread.shape[1], fs, -1).transpose(2, 0, 3, 1, 4)
-    return grad_down, spread.reshape(spread.shape[0], -1).astype(jnp.float32)
-
-
-def swap_halves(mine_rows):
-    _, _, _, _, c = coords()
-    rows = mine_rows.shape[0] // 2
-    near = lax.dynamic_slice_in_dim(mine_rows, c * rows, rows, 0)
-    far = flip_core(lax.dynamic_slice_in_dim(mine_rows, (1 - c) * rows, rows, 0))
-    return jnp.concatenate([jnp.where(c == 0, near, far), jnp.where(c == 0, far, near)], axis=1)
+    return spread.reshape(spread.shape[0], -1).astype(jnp.float32)
 
 
 def gather_small(value):
@@ -928,15 +953,15 @@
             far_attended, far_d_branch = flip_core(attended), flip_core(d_branch)
             d_branch = after(d_branch, parts["up"])
         else:
-            text_out = gather_plane(attended, d_branch)
+            text_out = (attended, d_branch)
         d_attended = linear_back(d_branch, weight_out[s]).astype(jnp.bfloat16)
         if s == 0:
             parts["out"] = partial_grad(after(attended, d_attended), d_branch, far_attended, far_d_branch)
             token = parts["out"]
-        column_sums.append([jnp.sum(a.astype(jnp.float32), axis=0) for a in (d_branch, d_hidden, d_mlp)])
+        column_sums.append([column_sum(a) for a in (d_branch, d_hidden, d_mlp)])
         backs.append((d_attended, d_middle, d_gate_one, d_shift_two, d_scale_two, d_gate_two))
     sent = [outs[0][image_half:], outs[1][text_half : 2 * text_half]]
-    text_grads = plane_mlp_grads(text_mlp[0], after(text_mlp[1], backs[1][0]), weight_up[1], bias_up[1], weight_down[1])
+    text_totals = plane_mlp_totals(text_mlp[0], after(text_mlp[1], backs[1][0]), weight_up[1], bias_up[1], weight_down[1])
     far_text_modded = text_mlp[2]
     d_front, reduced, far_outs = attend_back_and_reduce(
         fronts[0][3],
@@ -951,10 +976,12 @@
         [parts["down"], parts["up"], parts["out"]],
         [(0, True, 0, parts["down"].shape[1]), (1, False, 0, parts["up"].shape[1]), (2, True, 0, parts["out"].shape[1])],
         sent,
+        text_totals,
         2,
     )
-    text_qkv = gather_plane(d_front[1])[0]
-    text_out = [after(text_out[0], d_front[1]), text_out[1]]
+    text_qkv, *text_out = gather_plane(d_front[1], *text_out)
+    text_down, text_up = sum_fsdp(*text_totals)
+    text_up = spread_up(text_up)
     text_out_total = plane_total(*text_out)
     far_front, far_modded = flip_core(d_front[0]), flip_core(fronts[0][2])
     grads = {("down", 0): reduced[0], ("up", 0): reduced[1], ("out", 0): reduced[2]}
@@ -963,7 +990,7 @@
         mod = gains[s]
         normed, inverse, modded, _ = fronts[s]
         d_attended, d_middle, d_gate_one, d_shift_two, d_scale_two, d_gate_two = backs[s]
-        d_modded = linear_back(after(d_front[s], text_out_total), weight_qkv[s])
+        d_modded = linear_back(d_front[s], weight_qkv[s])
         d_shift_one = jnp.sum(d_modded, axis=0)
         d_scale_one = jnp.sum(d_modded * normed, axis=0)
         input_grads.append(d_middle + normalize_back(normed, inverse, d_modded * (1.0 + mod[1])))
@@ -973,22 +1000,22 @@
     mine = jnp.stack(gain_grads)
     part = partial_grad(after(fronts[0][2], *input_grads), d_front[0], far_modded, far_front)
     text_qkv_total = plane_total(far_text_modded, after(text_qkv, part))
-    part = after(part, text_qkv_total)
     cols = part.shape[1]
     sent = [input_grads[0][image_half:].astype(jnp.bfloat16), input_grads[1][text_half : 2 * text_half].astype(jnp.bfloat16)]
-    front_sums = [jnp.sum(d_front[s].astype(jnp.float32), axis=0) for s in range(2)]
+    front_sums = [column_sum(d_front[s]) for s in range(2)]
     small = jnp.concatenate([front_sums[s] for s in range(2)] + [v for s in range(2) for v in column_sums[s]])
     reduced, far_grads, small = reduce_weights(
         [part],
         [(0, True, 0, cols // 2), (0, False, cols // 2, cols // 2)],
         sent + [mine.reshape(-1, width)],
         small.reshape(-1, 128),
+        [text_qkv_total, text_out_total],
         3,
     )
     grads["qkv", 0] = reduced[0]
-    grads["down", 1], grads["up", 1] = text_grads
-    grads["out", 1] = sum_fsdp(text_out_total)
-    grads["qkv", 1] = sum_fsdp(text_qkv_total)
+    grads["down", 1], grads["up", 1] = text_down.astype(jnp.float32), text_up
+    for name, total in zip(("out", "qkv"), sum_fsdp(text_out_total, text_qkv_total)):
+        grads[name, 1] = total.astype(jnp.float32)
     grad_modulation = in_order(mine, far_grads[2].reshape(mine.shape))
 
     count = lax.axis_size(("seq", "fsdp") + DP)

time: 1390 us -> 1320 us (0.950)
  Pallas kernels: 831 us -> 771 us
    pallas_call x1, Pallas kernels: 290 us -> 251 us  [attend_back_and_reduce(): pl.pallas_call(kernel, grid_spec=pltpu.PrefetchScalarGridSpec(num_scalar_...]
    reduce_scatter x4 -> x2, waiting for transfers between devices: 22.1 us -> 0.01 us  [sum_fsdp(): lax.psum_scatter(flat.reshape(-1, width), 'fsdp', scatter_dimension=0, ti...]
    pallas_call x1, Pallas kernels: 145 us -> 125 us  [reduce_weights(): pl.pallas_call(kernel, out_shape=reduce_shapes(arrays, swaps) + [jax.Shap...]
    dot_general x12 -> x20, matrix products: 176 us -> 188 us  [dot(): lax.dot_general(a, b, (((ca,), (cb,)), ((), ())), preferred_element_type=...]
    unnamed x231 -> x267, local copies, waits for them, and re-layouts: 28 us -> 24.9 us
  transfers between devices with their start and end apart: 26 -> 19, of which waited for: 3 -> 3; matrix products, arithmetic and copies ran while one was open for 33% -> 32% of each run, Pallas kernels for 51% -> 48%
where the time goes in v4:
time: 1320 us
  Pallas kernels  771 us (58%)
  matrix products  326 us (25%)
  local copies, waits for them, and re-layouts  101 us (8%)
  other arithmetic  73.8 us (6%)
  waiting for transfers between devices  23 us (2%)
  between operations  16.1 us (1%)
    pallas_call x1, Pallas kernels, attend_back_and_reduce(): pl.pallas_call(kernel, grid_spec=pltpu.PrefetchScalarGridSpec(num_scalar_...  251 us
    dot_general x20, matrix products, dot(): lax.dot_general(a, b, (((ca,), (cb,)), ((), ())), preferred_element_type=...  188 us
    pallas_call x1, Pallas kernels, attend_and_gather(): pl.pallas_call(kernel, grid_spec=pltpu.PrefetchScalarGridSpec(num_scalar_...  179 us
    dot_general x9, matrix products, linear(): jnp.dot(values, weight, preferred_element_type=jnp.float32)  137 us
    pallas_call x1, Pallas kernels, gather_weights(): pl.pallas_call(kernel, out_shape=gather_shapes(units) + [jax.ShapeDtypeSt...  132 us
    pallas_call x1, Pallas kernels, reduce_weights(): pl.pallas_call(kernel, out_shape=reduce_shapes(arrays, swaps) + [jax.Shap...  125 us
    pallas_call x4, Pallas kernels, wgrad(): pl.pallas_call(wgrad_kernel, grid_spec=pltpu.PrefetchScalarGridSpec(num_s...  84.8 us
  transfers between devices with their start and end apart: 19, of which 3 were waited for; matrix products, arithmetic and copies ran while one was open for 32% of the time, Pallas kernels for 48%

profile of v4, /device:TPU:9, one launch (start us, length us, event | category | flops | bytes accessed | tf_op | source)
XLA Modules:
  0.0 1318.6 jit_solution(8055954877681728360)
XLA Ops:
  20.0 132.1 %gather_weights.1 = (bf16[1536,4608]{1,0:T(8,128)(2,1)}, bf16[1536,4608]{1,0:T(8,128)(2,1)}, bf16[512,1536]{1,0:T(8,128)(2,1)S(1)}, bf16[77,1536]{1,0:T(8,128)(2,1)S(1)}) custom-call(bf16[2,384,4608]{2,1,0:T(8,128)(2,1)} %refs_1_.1, bf16[2,384,4608]{2,1,0:T(8,128)(2,1)} %refs_1_.1, bf16[512,1536]{1,0:T(8,128)(2,1)S(1)} %get-tuple-element.230.refs_2_, ...), custom_call_target="tpu_custom_call" | custom-call | tf_op jit(solution)/shard_map/gather_weights/pallas_call | solution.py:343
  179.4 8.9 fusion.25.refs_4_.refs_5_.refs_6_
  188.3 20.2 %add_convert_fusion.refs_1_.refs_2_.refs_3_ = bf16[1024,4608]{1,0:T(8,128)(2,1)} fusion(bf16[1024,1536]{1,0:T(8,128)(2,1)} %fusion.16.a0, bf16[1536,4608]{1,0:T(8,128)(2,1)} %get-tuple-element.51, f32[4608]{0:T(1024)S(1)} %add.477), kind=kOutput, calls=%fused_computation.13 | convolution fusion | flops 14504951808 | bytes 26757120 | tf_op jit(solution)/shard_map/dot_general | solution.py:123
  208.5 178.9 %attend_and_gather.1 = (bf16[1024,1536]{1,0:T(8,128)(2,1)}, bf16[160,1536]{1,0:T(8,128)(2,1)}, f32[12,8,1280]{2,1,0:T(8,128)}, bf16[1536,1536]{1,0:T(8,128)(2,1)...) custom-call(s32[3]{0:T(128)} %pad_add_fusion.3.refs_0_, ...), custom_call_target="tpu_custom_call" | custom-call | tf_op jit(solution)/shard_map/attend_and_gather/pallas_call | solution.py:394
  388.2 10.7 fusion.164
  402.2 33.2 %multiply_convert_fusion.1 = (bf16[1024,6144]{1,0:T(8,128)(2,1)}, f32[1024,6144]{1,0:T(8,128)}) fusion(f32[6144]{0:T(1024)S(1)} %bitcast.189, bf16[1024,1536]{1,0:T(8,128)(2,1)S(1)} %add_convert_fusion.2.a0, bf16[1536,6144]{1,0:T(8,128)(2,1)} %get-tuple-element.57), kind=kOutput, calls=%fused_computation.11 | convolution fusion | flops 19390267392 | bytes 59793408 | tf_op jit(solution)/shard_map/dot_general | solution.py:123
  437.6 30.0 %fusion.24 = (f32[1536]{0:T(1024)}, bf16[1024,1536]{1,0:T(8,128)(2,1)}, bf16[1024,1536]{1,0:T(8,128)(2,1)S(1)}) fusion(f32[1536]{0:T(1024)S(1)} %add.504, bf16[512,1536]{1,0:T(8,128)(2,1)} %get-tuple-element.60, bf16[512,1536]{1,0:T(8,128)(2,1)} %get-tuple-element.192, f32[1024,1536]{1,0:T(8,128)} %copy-done.12, f32[1536]{0:T(1024)S(1)} %copy-done.108, ...), kind=kOutput, calls=%fused_computation.38 | convolution fusion | flops 19346225152 | bytes 47204352 | tf_op jit(solution)/shard_map/dot_general | solution.py:123
  474.9 25.4 %wgrad.4 = bf16[6144,768]{1,0:T(8,128)(2,1)} custom-call(s32[2]{0:T(128)S(1)} %pad_add_fusion.2.sel_ref, bf16[1024,6144]{1,0:T(8,128)(2,1)} %get-tuple-element.61.a0, bf16[1024,1536]{1,0:T(8,128)(2,1)S(1)} %get-tuple-element.62.b0, bf16[1024,6144]{1,0:T(8,128)(2,1)} %collective-permute-done.3.a1, bf16[1024,1536]{1,0:T(8,128)(2,1)} %copy-done.120), custom_call_target="tpu_custom_call" | custom-call | flops 19327352832 | bytes 25165824 | tf_op jit(solution)/shard_map/wgrad/pallas_call | solution.py:828
  500.3 39.5 %multiply_convert_fusion.b0 = bf16[1024,6144]{1,0:T(8,128)(2,1)} fusion(bf16[1024,1536]{1,0:T(8,128)(2,1)S(1)} %get-tuple-element.62.b0, bf16[6144,1536]{1,0:T(8,128)(2,1)} %get-tuple-element.58, f32[1024,6144]{1,0:T(8,128)} %get-tuple-element.224, f32[6144]{0:T(1024)S(1)} %bitcast.190), kind=kOutput, calls=%fused_computation.10 | convolution fusion | flops 19465764864 | bytes 59793408 | tf_op jit(solution)/shard_map/dot_general | solution.py:14
  540.9 31.3 %multiply_reduce_fusion = (f32[1536]{0:T(1024)}, f32[1024]{0:T(1024)S(1)}, f32[1024]{0:T(1024)S(1)}, f32[1536]{0:T(1024)}, f32[1024,1536]{1,0:T(8,128)}) fusion(f32[1024,1536]{1,0:T(8,128)} %copy-done.12, f32[1024]{0:T(1024)S(1)} %copy-done.77, f32[1024]{0:T(1024)S(1)} %copy-done.73, f32[1536]{0:T(1024)S(1)} %copy-done.69, ...), kind=kOutput, calls=%fused_computation.40 | convolution fusion | flops 19341502464 | bytes 44075008 | tf_op jit(solution)/shard_map/dot_general | solution.py:14
  572.2 9.6 multiply_reduce_fusion.1
  588.1 27.7 %wgrad.5 = bf16[1536,3072]{1,0:T(8,128)(2,1)} custom-call(s32[2]{0:T(128)S(1)} %pad_add_fusion.1.sel_ref, bf16[1024,1536]{1,0:T(8,128)(2,1)S(1)} %copy-done.7, bf16[1024,6144]{1,0:T(8,128)(2,1)} %multiply_convert_fusion.b0, bf16[1024,1536]{1,0:T(8,128)(2,1)} %collective-permute-done.5.a1, bf16[1024,6144]{1,0:T(8,128)(2,1)} %collective-permute-done.6.b1), custom_call_target="tpu_custom_call" | custom-call | flops 19327352832 | bytes 25165824 | tf_op jit(solution)/shard_map/wgrad/pallas_call | solution.py:828
  615.8 9.4 convolution_convert_fusion.1.refs_9_
  641.3 11.5 convolution_add_fusion
  652.9 12.3 convolution_add_fusion.4
  665.1 11.3 fusion.14
  676.4 13.0 multiply_reduce_fusion.6
  701.2 9.2 all-gather.13.cloned.1.call-done
  727.2 14.7 %fusion.47 = bf16[1536,768]{1,0:T(8,128)(2,1)} fusion(bf16[1280,4608]{1,0:T(8,128)(2,1)} %all-gather.13.cloned.1.call-done, bf16[1280,1536]{1,0:T(8,128)(2,1)} %copy-done.32, bf16[192,1536]{1,0:T(8,128)(2,1)S(1)} %copy-done.51, bf16[192,1536]{1,0:T(8,128)(2,1)S(1)} %copy-done.52, bf16[192,1536]{1,0:T(8,128)(2,1)S(1)} %copy-done.53, ...), kind=kOutput, calls=%fused_computation.86 | convolution fusion | flops 6071058432 | bytes 16515072 | tf_op jit(solution)/shard_map/dot_general | solution.py:14
  755.7 250.9 %attend_back_and_reduce.1 = (bf16[1024,4608]{1,0:T(8,128)(2,1)}, bf16[160,4608]{1,0:T(8,128)(2,1)}, f32[1,192,1536]{2,1,0:T(8,128)}, f32[1,48,6144]{2,1,0:T(8,12...) custom-call(s32[3]{0:T(128)} %pad_add_fusion.3.refs_0_, ...), custom_call_target="tpu_custom_call" | custom-call | tf_op jit(solution)/shard_map/attend_back_and_reduce/pallas_call | solution.py:706
  1030.2 11.9 fusion.90
  1042.7 23.6 %fusion.21 = (f32[1536]{0:T(1024)}, f32[1024]{0:T(1024)S(1)}, f32[1024]{0:T(1024)S(1)}, f32[1536]{0:T(1024)}, f32[1024,1536]{1,0:T(8,128)}) fusion(f32[1024]{0:T(1024)S(1)} %copy-done.75, f32[1024]{0:T(1024)S(1)} %copy-done.71, bf16[512,1536]{1,0:T(8,128)(2,1)S(1)} %copy-done.1, bf16[512,1536]{1,0:T(8,128)(2,1)S(1)} %copy-done.15, f32[1536]{0:T(1024)S(1)} %copy-done.64, ...), kind=kOutput, calls=%fused_computation.35 | convolution fusion | flops 14515955712 | bytes 33064960 | tf_op jit(solution)/shard_map/dot_general | solution.py:14
  1100.9 23.0 %wgrad.7 = bf16[1536,2304]{1,0:T(8,128)(2,1)} custom-call(s32[2]{0:T(128)S(1)} %pad_add_fusion.sel_ref, bf16[1024,1536]{1,0:T(8,128)(2,1)} %fusion.16.a0, bf16[1024,4608]{1,0:T(8,128)(2,1)} %get-tuple-element.75.b0, bf16[1024,1536]{1,0:T(8,128)(2,1)} %collective-permute-done.9.a1, bf16[1024,4608]{1,0:T(8,128)(2,1)} %collective-permute-done.10.b1), custom_call_target="tpu_custom_call" | custom-call | flops 14495514624 | bytes 19660800 | tf_op jit(solution)/shard_map/wgrad/pallas_call | solution.py:828
  1168.2 124.7 %reduce_weights.1 = (f32[1,48,4608]{2,1,0:T(8,128)}, bf16[512,1536]{1,0:T(8,128)(2,1)}, bf16[77,1536]{1,0:T(8,128)(2,1)}, f32[12,1536]{1,0:T(8,128)}, f32[216,128]{1,0:T(8,128)}) custom-call(bf16[2,4,1,2,2,48,2304]{6,5,4,3,2,1,0:T(8,128)(2,1)} %bitcast.162, bf16[512,1536]{1,0:T(8,128)(2,1)} %slice.339.refs_1_, bf16[77,1536]{1,0:T(8,128)(2,1)} %slice.340.refs_2_, ...), custom_call_target="tpu_custom_call" | custom-call | tf_op jit(solution)/shard_map/reduce_weights/pallas_call | solution.py:639
  (464 shorter events, 239.4 us)
Async XLA Ops:
  7.2 628.3 %all-gather.7.cloned.1.call-start = ((), (), s32[]{:S(2)}) async-start(), calls=%async_computation.2 | async-start | bytes 4866048 | tf_op jit(solution)/shard_map/all_gather | solution.py:739
  20.0 142.9 %copy-start.78 = (f32[2,2,6,1536]{3,1,2,0:T(2,128)S(1)}, f32[2,2,6,1536]{3,1,2,0:T(2,128)}, u32[]{:S(2)}) copy-start(f32[2,2,6,1536]{3,1,2,0:T(2,128)} %param.16) | copy-start | bytes 442372
  152.1 236.1 %copy-start = (bf16[512,1536]{1,0:T(8,128)(2,1)}, bf16[512,1536]{1,0:T(8,128)(2,1)S(1)}, u32[]{:S(2)}) copy-start(bf16[512,1536]{1,0:T(8,128)(2,1)S(1)} %get-tuple-element.50) | copy-start | bytes 4718596
  152.2 489.2 %all-gather.9.cloned.1.call-start = ((), (), s32[]{:S(2)}) async-start(), calls=%async_computation.3 | async-start | bytes 19464192 | tf_op jit(solution)/shard_map/all_gather | solution.py:739
  156.4 21.8 %collective-permute-start.2 = (bf16[2,3456]{1,0:T(2,128)(2,1)}, bf16[2,3456]{1,0:T(2,128)(2,1)}, u32[]{:S(2)}, u32[]{:S(2)}) collective-permute-start(bf16[2,3456]{1,0:T(2,128)(2,1)} %constant_dynamic-update-slice_fusion), channel_id=1, source_target_pairs={{0,12},{4,0},{8,4},{12,8},{1,13},{5,1},{9,5},{13,9},{2,14},{6,2},{... | collective-permute-start | bytes 41480 | tf_op jit(solution)/shard_map/ppermute | solution.py:163
  157.5 20.7 %collective-permute-start.1 = (bf16[2,3456]{1,0:T(2,128)(2,1)}, bf16[2,3456]{1,0:T(2,128)(2,1)}, u32[]{:S(2)}, u32[]{:S(2)}) collective-permute-start(bf16[2,3456]{1,0:T(2,128)(2,1)} %constant_dynamic-update-slice_fusion), channel_id=1, source_target_pairs={{0,8},{4,12},{8,0},{12,4},{1,9},{5,13},{9,1},{13,5},{2,10},{6,14},... | collective-permute-start | bytes 41480 | tf_op jit(solution)/shard_map/ppermute | solution.py:163
  157.8 20.4 %collective-permute-start = (bf16[2,3456]{1,0:T(2,128)(2,1)}, bf16[2,3456]{1,0:T(2,128)(2,1)}, u32[]{:S(2)}, u32[]{:S(2)}) collective-permute-start(bf16[2,3456]{1,0:T(2,128)(2,1)} %constant_dynamic-update-slice_fusion), channel_id=1, source_target_pairs={{0,4},{4,8},{8,12},{12,0},{1,5},{5,9},{9,13},{13,1},{2,6},{6,10},{... | collective-permute-start | bytes 41480 | tf_op jit(solution)/shard_map/ppermute | solution.py:163
  163.7 224.5 %copy-start.88 = (f32[1536]{0:T(1024)}, f32[1536]{0:T(1024)S(1)}, u32[]{:S(2)}) copy-start(f32[1536]{0:T(1024)S(1)} %get-tuple-element.152) | copy-start | bytes 18436
  163.7 237.2 %copy-start.68 = (f32[1536]{0:T(1024)}, f32[1536]{0:T(1024)S(1)}, u32[]{:S(2)}) copy-start(f32[1536]{0:T(1024)S(1)} %get-tuple-element.146) | copy-start | bytes 18436
  387.4 265.4 %all-gather.11.cloned.1.call-start = ((), (), s32[]{:S(2)}) async-start(), calls=%async_computation.4 | async-start | bytes 19464192 | tf_op jit(solution)/shard_map/all_gather | solution.py:739
  435.4 37.8 %collective-permute-start.3 = (bf16[1024,6144]{1,0:T(8,128)(2,1)}, bf16[1024,6144]{1,0:T(8,128)(2,1)}, u32[]{:S(2)}, u32[]{:S(2)}) collective-permute-start(bf16[1024,6144]{1,0:T(8,128)(2,1)} %get-tuple-element.61.a0), channel_id=1, source_target_pairs={{0,1},{1,0},{2,3},{3,2},{4,5},{5,4},{6,7},{7,6},{8,9},{9,8},{10,11... | collective-permute-start | bytes 37748744 | tf_op jit(solution)/shard_map/ppermute | solution.py:158
  437.5 272.9 %all-gather.13.cloned.1.call-start = ((), (), s32[]{:S(2)}) async-start(), calls=%async_computation.5 | async-start | bytes 13271040 | tf_op jit(solution)/shard_map/all_gather | solution.py:744
  467.6 5.7 collective-permute-start.4
  539.9 48.2 %collective-permute-start.6 = (bf16[1024,6144]{1,0:T(8,128)(2,1)}, bf16[1024,6144]{1,0:T(8,128)(2,1)}, u32[]{:S(2)}, u32[]{:S(2)}) collective-permute-start(bf16[1024,6144]{1,0:T(8,128)(2,1)} %multiply_convert_fusion.b0), channel_id=1, source_target_pairs={{0,1},{1,0},{2,3},{3,2},{4,5},{5,4},{6,7},{7,6},{8,9},{9,8},{10,11... | collective-permute-start | bytes 37748744 | tf_op jit(solution)/shard_map/ppermute | solution.py:158
  540.3 47.7 %collective-permute-start.5 = (bf16[1024,1536]{1,0:T(8,128)(2,1)}, bf16[1024,1536]{1,0:T(8,128)(2,1)}, u32[]{:S(2)}, u32[]{:S(2)}) collective-permute-start(bf16[1024,1536]{1,0:T(8,128)(2,1)} %copy-done.6), channel_id=1, source_target_pairs={{0,1},{1,0},{2,3},{3,2},{4,5},{5,4},{6,7},{7,6},{8,9},{9,8},{10,11... | collective-permute-start | bytes 9437192 | tf_op jit(solution)/shard_map/ppermute | solution.py:158
  540.4 84.8 %collective-permute-start.7 = (bf16[1024,1536]{1,0:T(8,128)(2,1)}, bf16[1024,1536]{1,0:T(8,128)(2,1)}, u32[]{:S(2)}, u32[]{:S(2)}) collective-permute-start(bf16[1024,1536]{1,0:T(8,128)(2,1)} %get-tuple-element.66.a0.refs_7_), channel_id=1, source_target_pairs={{0,1},{1,0},{2,3},{3,2},{4,5},{5,4},{6,7},{7,6},{8,9},{9,8},{10,11... | collective-permute-start | bytes 9437192 | tf_op jit(solution)/shard_map/ppermute | solution.py:158
  586.0 39.3 %collective-permute-start.8 = (bf16[1024,1536]{1,0:T(8,128)(2,1)}, bf16[1024,1536]{1,0:T(8,128)(2,1)}, u32[]{:S(2)}, u32[]{:S(2)}) collective-permute-start(bf16[1024,1536]{1,0:T(8,128)(2,1)} %multiply_convert_fusion.2.b0), channel_id=1, source_target_pairs={{0,1},{1,0},{2,3},{3,2},{4,5},{5,4},{6,7},{7,6},{8,9},{9,8},{10,11... | collective-permute-start | bytes 9437192 | tf_op jit(solution)/shard_map/ppermute | solution.py:158
  641.1 426.4 %reduce-scatter.5.cloned.1.call-start = ((), (), s32[]{:S(2)}) async-start(), calls=%async_computation.8 | async-start | bytes 5898240 | tf_op jit(solution)/shard_map/reduce_scatter | solution.py:764
  751.1 372.7 %all-gather.15.cloned.1.call-start = ((), (), s32[]{:S(2)}) async-start(), calls=%async_computation.6 | async-start | bytes 22118400 | tf_op jit(solution)/shard_map/all_gather | solution.py:744
  755.7 251.0 %copy-start.21 = (bf16[160,1536]{1,0:T(8,128)(2,1)S(1)}, bf16[160,1536]{1,0:T(8,128)(2,1)}, u32[]{:S(2)}) copy-start(bf16[160,1536]{1,0:T(8,128)(2,1)} %copy-done.20) | copy-start | bytes 1474564
  1010.0 142.7 %all-gather.17.cloned.1.call-start = ((), (), s32[]{:S(2)}) async-start(), calls=%async_computation.9 | async-start | bytes 5308416 | tf_op jit(solution)/shard_map/all_gather | solution.py:794
  1010.5 90.4 %collective-permute-start.9 = (bf16[1024,1536]{1,0:T(8,128)(2,1)}, bf16[1024,1536]{1,0:T(8,128)(2,1)}, u32[]{:S(2)}, u32[]{:S(2)}) collective-permute-start(bf16[1024,1536]{1,0:T(8,128)(2,1)} %fusion.16.a0), channel_id=1, source_target_pairs={{0,1},{1,0},{2,3},{3,2},{4,5},{5,4},{6,7},{7,6},{8,9},{9,8},{10,11... | collective-permute-start | bytes 9437192 | tf_op jit(solution)/shard_map/ppermute | solution.py:158
  1029.7 71.2 %collective-permute-start.10 = (bf16[1024,4608]{1,0:T(8,128)(2,1)}, bf16[1024,4608]{1,0:T(8,128)(2,1)}, u32[]{:S(2)}, u32[]{:S(2)}) collective-permute-start(bf16[1024,4608]{1,0:T(8,128)(2,1)} %get-tuple-element.75.b0), channel_id=1, source_target_pairs={{0,1},{1,0},{2,3},{3,2},{4,5},{5,4},{6,7},{7,6},{8,9},{9,8},{10,11... | collective-permute-start | bytes 28311560 | tf_op jit(solution)/shard_map/ppermute | solution.py:158
  1072.1 233.6 %reduce-scatter.3.cloned.1.call-start = ((), (), s32[]{:S(2)}) async-start(), calls=%async_computation.7 | async-start | bytes 2949120 | tf_op jit(solution)/shard_map/reduce_scatter | solution.py:764
  (121 other events, 1453.3 us)
Sparse Core Ops, SparseCore 0:
  152.3 62.9 all-gather.6
  387.6 122.8 all-gather.8
  513.9 122.8 all-gather.10
  641.2 69.1 all-gather.12
  751.2 84.8 reduce-scatter.4
  1010.2 101.1 all-gather.14
  1113.8 38.9 all-gather.16
  1155.0 45.2 reduce-scatter.2

commit v5 on v4

--- a/solution.py
+++ b/solution.py
@@ -689,7 +689,7 @@
             for cp in swapped:
                 cp.start()
 
-        times = (2, 4, 7, 10)
+        times = (3, 6, 8, 11)
         early = min(len(times), len(actions) - 1)
         for index, at in zip(range(early), times):
             pl.when((pair == at) & (part == 0))(actions[index])

time: 1320 us -> 1320 us (level)
  no operation moved by 1% of the time
where the time goes in v5:
time: 1320 us; the launch traced here: 1310 us
  Pallas kernels  766 us (58%)
  matrix products  326 us (25%)
  local copies, waits for them, and re-layouts  101 us (8%)
  other arithmetic  73.8 us (6%)
  waiting for transfers between devices  23.1 us (2%)
  between operations  16.1 us (1%)
    pallas_call x1, Pallas kernels, attend_back_and_reduce(): pl.pallas_call(kernel, grid_spec=pltpu.PrefetchScalarGridSpec(num_scalar_...  246 us
    dot_general x20, matrix products, dot(): lax.dot_general(a, b, (((ca,), (cb,)), ((), ())), preferred_element_type=...  188 us
    pallas_call x1, Pallas kernels, attend_and_gather(): pl.pallas_call(kernel, grid_spec=pltpu.PrefetchScalarGridSpec(num_scalar_...  179 us
    dot_general x9, matrix products, linear(): jnp.dot(values, weight, preferred_element_type=jnp.float32)  137 us
    pallas_call x1, Pallas kernels, gather_weights(): pl.pallas_call(kernel, out_shape=gather_shapes(units) + [jax.ShapeDtypeSt...  132 us
    pallas_call x1, Pallas kernels, reduce_weights(): pl.pallas_call(kernel, out_shape=reduce_shapes(arrays, swaps) + [jax.Shap...  125 us
    pallas_call x4, Pallas kernels, wgrad(): pl.pallas_call(wgrad_kernel, grid_spec=pltpu.PrefetchScalarGridSpec(num_s...  84.8 us
  transfers between devices with their start and end apart: 19, of which 3 were waited for; matrix products, arithmetic and copies ran while one was open for 32% of the time, Pallas kernels for 48%

profile of v5, /device:TPU:9, one launch (start us, length us, event | category | flops | bytes accessed | tf_op | source)
XLA Modules:
  0.0 1313.3 jit_solution(16952148226554322420)
XLA Ops:
  20.0 132.1 %gather_weights.1 = (bf16[1536,4608]{1,0:T(8,128)(2,1)}, bf16[1536,4608]{1,0:T(8,128)(2,1)}, bf16[512,1536]{1,0:T(8,128)(2,1)S(1)}, bf16[77,1536]{1,0:T(8,128)(2,1)S(1)}) custom-call(bf16[2,384,4608]{2,1,0:T(8,128)(2,1)} %refs_1_.1, bf16[2,384,4608]{2,1,0:T(8,128)(2,1)} %refs_1_.1, bf16[512,1536]{1,0:T(8,128)(2,1)S(1)} %get-tuple-element.230.refs_2_, ...), custom_call_target="tpu_custom_call" | custom-call | tf_op jit(solution)/shard_map/gather_weights/pallas_call | solution.py:343
  179.4 8.9 fusion.25.refs_4_.refs_5_.refs_6_
  188.3 20.2 %add_convert_fusion.refs_1_.refs_2_.refs_3_ = bf16[1024,4608]{1,0:T(8,128)(2,1)} fusion(bf16[1024,1536]{1,0:T(8,128)(2,1)} %fusion.16.a0, bf16[1536,4608]{1,0:T(8,128)(2,1)} %get-tuple-element.51, f32[4608]{0:T(1024)S(1)} %add.477), kind=kOutput, calls=%fused_computation.13 | convolution fusion | flops 14504951808 | bytes 26757120 | tf_op jit(solution)/shard_map/dot_general | solution.py:123
  208.5 178.9 %attend_and_gather.1 = (bf16[1024,1536]{1,0:T(8,128)(2,1)}, bf16[160,1536]{1,0:T(8,128)(2,1)}, f32[12,8,1280]{2,1,0:T(8,128)}, bf16[1536,1536]{1,0:T(8,128)(2,1)...) custom-call(s32[3]{0:T(128)} %pad_add_fusion.3.refs_0_, ...), custom_call_target="tpu_custom_call" | custom-call | tf_op jit(solution)/shard_map/attend_and_gather/pallas_call | solution.py:394
  388.2 10.7 fusion.164
  402.2 33.2 %multiply_convert_fusion.1 = (bf16[1024,6144]{1,0:T(8,128)(2,1)}, f32[1024,6144]{1,0:T(8,128)}) fusion(f32[6144]{0:T(1024)S(1)} %bitcast.189, bf16[1024,1536]{1,0:T(8,128)(2,1)S(1)} %add_convert_fusion.2.a0, bf16[1536,6144]{1,0:T(8,128)(2,1)} %get-tuple-element.57), kind=kOutput, calls=%fused_computation.11 | convolution fusion | flops 19390267392 | bytes 59793408 | tf_op jit(solution)/shard_map/dot_general | solution.py:123
  437.6 30.0 %fusion.24 = (f32[1536]{0:T(1024)}, bf16[1024,1536]{1,0:T(8,128)(2,1)}, bf16[1024,1536]{1,0:T(8,128)(2,1)S(1)}) fusion(f32[1536]{0:T(1024)S(1)} %add.504, bf16[512,1536]{1,0:T(8,128)(2,1)} %get-tuple-element.60, bf16[512,1536]{1,0:T(8,128)(2,1)} %get-tuple-element.192, f32[1024,1536]{1,0:T(8,128)} %copy-done.12, f32[1536]{0:T(1024)S(1)} %copy-done.108, ...), kind=kOutput, calls=%fused_computation.38 | convolution fusion | flops 19346225152 | bytes 47204352 | tf_op jit(solution)/shard_map/dot_general | solution.py:123
  474.9 25.4 %wgrad.4 = bf16[6144,768]{1,0:T(8,128)(2,1)} custom-call(s32[2]{0:T(128)S(1)} %pad_add_fusion.2.sel_ref, bf16[1024,6144]{1,0:T(8,128)(2,1)} %get-tuple-element.61.a0, bf16[1024,1536]{1,0:T(8,128)(2,1)S(1)} %get-tuple-element.62.b0, bf16[1024,6144]{1,0:T(8,128)(2,1)} %collective-permute-done.3.a1, bf16[1024,1536]{1,0:T(8,128)(2,1)} %copy-done.120), custom_call_target="tpu_custom_call" | custom-call | flops 19327352832 | bytes 25165824 | tf_op jit(solution)/shard_map/wgrad/pallas_call | solution.py:828
  500.3 39.5 %multiply_convert_fusion.b0 = bf16[1024,6144]{1,0:T(8,128)(2,1)} fusion(bf16[1024,1536]{1,0:T(8,128)(2,1)S(1)} %get-tuple-element.62.b0, bf16[6144,1536]{1,0:T(8,128)(2,1)} %get-tuple-element.58, f32[1024,6144]{1,0:T(8,128)} %get-tuple-element.224, f32[6144]{0:T(1024)S(1)} %bitcast.190), kind=kOutput, calls=%fused_computation.10 | convolution fusion | flops 19465764864 | bytes 59793408 | tf_op jit(solution)/shard_map/dot_general | solution.py:14
  540.9 31.3 %multiply_reduce_fusion = (f32[1536]{0:T(1024)}, f32[1024]{0:T(1024)S(1)}, f32[1024]{0:T(1024)S(1)}, f32[1536]{0:T(1024)}, f32[1024,1536]{1,0:T(8,128)}) fusion(f32[1024,1536]{1,0:T(8,128)} %copy-done.12, f32[1024]{0:T(1024)S(1)} %copy-done.77, f32[1024]{0:T(1024)S(1)} %copy-done.73, f32[1536]{0:T(1024)S(1)} %copy-done.69, ...), kind=kOutput, calls=%fused_computation.40 | convolution fusion | flops 19341502464 | bytes 44075008 | tf_op jit(solution)/shard_map/dot_general | solution.py:14
  572.2 9.6 multiply_reduce_fusion.1
  588.1 27.7 %wgrad.5 = bf16[1536,3072]{1,0:T(8,128)(2,1)} custom-call(s32[2]{0:T(128)S(1)} %pad_add_fusion.1.sel_ref, bf16[1024,1536]{1,0:T(8,128)(2,1)S(1)} %copy-done.7, bf16[1024,6144]{1,0:T(8,128)(2,1)} %multiply_convert_fusion.b0, bf16[1024,1536]{1,0:T(8,128)(2,1)} %collective-permute-done.5.a1, bf16[1024,6144]{1,0:T(8,128)(2,1)} %collective-permute-done.6.b1), custom_call_target="tpu_custom_call" | custom-call | flops 19327352832 | bytes 25165824 | tf_op jit(solution)/shard_map/wgrad/pallas_call | solution.py:828
  615.8 9.4 convolution_convert_fusion.1.refs_9_
  641.3 11.5 convolution_add_fusion
  652.9 12.3 convolution_add_fusion.4
  665.1 11.3 fusion.14
  676.4 13.0 multiply_reduce_fusion.6
  701.2 9.2 all-gather.13.cloned.1.call-done
  727.2 14.7 %fusion.47 = bf16[1536,768]{1,0:T(8,128)(2,1)} fusion(bf16[1280,4608]{1,0:T(8,128)(2,1)} %all-gather.13.cloned.1.call-done, bf16[1280,1536]{1,0:T(8,128)(2,1)} %copy-done.32, bf16[192,1536]{1,0:T(8,128)(2,1)S(1)} %copy-done.51, bf16[192,1536]{1,0:T(8,128)(2,1)S(1)} %copy-done.52, bf16[192,1536]{1,0:T(8,128)(2,1)S(1)} %copy-done.53, ...), kind=kOutput, calls=%fused_computation.86 | convolution fusion | flops 6071058432 | bytes 16515072 | tf_op jit(solution)/shard_map/dot_general | solution.py:14
  755.7 245.7 %attend_back_and_reduce.1 = (bf16[1024,4608]{1,0:T(8,128)(2,1)}, bf16[160,4608]{1,0:T(8,128)(2,1)}, f32[1,192,1536]{2,1,0:T(8,128)}, f32[1,48,6144]{2,1,0:T(8,12...) custom-call(s32[3]{0:T(128)} %pad_add_fusion.3.refs_0_, ...), custom_call_target="tpu_custom_call" | custom-call | tf_op jit(solution)/shard_map/attend_back_and_reduce/pallas_call | solution.py:706
  1025.0 11.9 fusion.90
  1037.5 23.6 %fusion.21 = (f32[1536]{0:T(1024)}, f32[1024]{0:T(1024)S(1)}, f32[1024]{0:T(1024)S(1)}, f32[1536]{0:T(1024)}, f32[1024,1536]{1,0:T(8,128)}) fusion(f32[1024]{0:T(1024)S(1)} %copy-done.75, f32[1024]{0:T(1024)S(1)} %copy-done.71, bf16[512,1536]{1,0:T(8,128)(2,1)S(1)} %copy-done.1, bf16[512,1536]{1,0:T(8,128)(2,1)S(1)} %copy-done.15, f32[1536]{0:T(1024)S(1)} %copy-done.64, ...), kind=kOutput, calls=%fused_computation.35 | convolution fusion | flops 14515955712 | bytes 33064960 | tf_op jit(solution)/shard_map/dot_general | solution.py:14
  1095.7 23.0 %wgrad.7 = bf16[1536,2304]{1,0:T(8,128)(2,1)} custom-call(s32[2]{0:T(128)S(1)} %pad_add_fusion.sel_ref, bf16[1024,1536]{1,0:T(8,128)(2,1)} %fusion.16.a0, bf16[1024,4608]{1,0:T(8,128)(2,1)} %get-tuple-element.75.b0, bf16[1024,1536]{1,0:T(8,128)(2,1)} %collective-permute-done.9.a1, bf16[1024,4608]{1,0:T(8,128)(2,1)} %collective-permute-done.10.b1), custom_call_target="tpu_custom_call" | custom-call | flops 14495514624 | bytes 19660800 | tf_op jit(solution)/shard_map/wgrad/pallas_call | solution.py:828
  1163.0 124.7 %reduce_weights.1 = (f32[1,48,4608]{2,1,0:T(8,128)}, bf16[512,1536]{1,0:T(8,128)(2,1)}, bf16[77,1536]{1,0:T(8,128)(2,1)}, f32[12,1536]{1,0:T(8,128)}, f32[216,128]{1,0:T(8,128)}) custom-call(bf16[2,4,1,2,2,48,2304]{6,5,4,3,2,1,0:T(8,128)(2,1)} %bitcast.162, bf16[512,1536]{1,0:T(8,128)(2,1)} %slice.339.refs_1_, bf16[77,1536]{1,0:T(8,128)(2,1)} %slice.340.refs_2_, ...), custom_call_target="tpu_custom_call" | custom-call | tf_op jit(solution)/shard_map/reduce_weights/pallas_call | solution.py:639
  (464 shorter events, 239.4 us)
Async XLA Ops:
  7.2 628.3 %all-gather.7.cloned.1.call-start = ((), (), s32[]{:S(2)}) async-start(), calls=%async_computation.2 | async-start | bytes 4866048 | tf_op jit(solution)/shard_map/all_gather | solution.py:739
  20.0 142.9 %copy-start.78 = (f32[2,2,6,1536]{3,1,2,0:T(2,128)S(1)}, f32[2,2,6,1536]{3,1,2,0:T(2,128)}, u32[]{:S(2)}) copy-start(f32[2,2,6,1536]{3,1,2,0:T(2,128)} %param.16) | copy-start | bytes 442372
  152.1 236.1 %copy-start = (bf16[512,1536]{1,0:T(8,128)(2,1)}, bf16[512,1536]{1,0:T(8,128)(2,1)S(1)}, u32[]{:S(2)}) copy-start(bf16[512,1536]{1,0:T(8,128)(2,1)S(1)} %get-tuple-element.50) | copy-start | bytes 4718596
  152.2 489.2 %all-gather.9.cloned.1.call-start = ((), (), s32[]{:S(2)}) async-start(), calls=%async_computation.3 | async-start | bytes 19464192 | tf_op jit(solution)/shard_map/all_gather | solution.py:739
  156.4 21.8 %collective-permute-start.2 = (bf16[2,3456]{1,0:T(2,128)(2,1)}, bf16[2,3456]{1,0:T(2,128)(2,1)}, u32[]{:S(2)}, u32[]{:S(2)}) collective-permute-start(bf16[2,3456]{1,0:T(2,128)(2,1)} %constant_dynamic-update-slice_fusion), channel_id=1, source_target_pairs={{0,12},{4,0},{8,4},{12,8},{1,13},{5,1},{9,5},{13,9},{2,14},{6,2},{... | collective-permute-start | bytes 41480 | tf_op jit(solution)/shard_map/ppermute | solution.py:163
  157.5 20.7 %collective-permute-start.1 = (bf16[2,3456]{1,0:T(2,128)(2,1)}, bf16[2,3456]{1,0:T(2,128)(2,1)}, u32[]{:S(2)}, u32[]{:S(2)}) collective-permute-start(bf16[2,3456]{1,0:T(2,128)(2,1)} %constant_dynamic-update-slice_fusion), channel_id=1, source_target_pairs={{0,8},{4,12},{8,0},{12,4},{1,9},{5,13},{9,1},{13,5},{2,10},{6,14},... | collective-permute-start | bytes 41480 | tf_op jit(solution)/shard_map/ppermute | solution.py:163
  157.8 20.4 %collective-permute-start = (bf16[2,3456]{1,0:T(2,128)(2,1)}, bf16[2,3456]{1,0:T(2,128)(2,1)}, u32[]{:S(2)}, u32[]{:S(2)}) collective-permute-start(bf16[2,3456]{1,0:T(2,128)(2,1)} %constant_dynamic-update-slice_fusion), channel_id=1, source_target_pairs={{0,4},{4,8},{8,12},{12,0},{1,5},{5,9},{9,13},{13,1},{2,6},{6,10},{... | collective-permute-start | bytes 41480 | tf_op jit(solution)/shard_map/ppermute | solution.py:163
  163.7 224.5 %copy-start.88 = (f32[1536]{0:T(1024)}, f32[1536]{0:T(1024)S(1)}, u32[]{:S(2)}) copy-start(f32[1536]{0:T(1024)S(1)} %get-tuple-element.152) | copy-start | bytes 18436
  163.7 237.2 %copy-start.68 = (f32[1536]{0:T(1024)}, f32[1536]{0:T(1024)S(1)}, u32[]{:S(2)}) copy-start(f32[1536]{0:T(1024)S(1)} %get-tuple-element.146) | copy-start | bytes 18436
  387.4 265.4 %all-gather.11.cloned.1.call-start = ((), (), s32[]{:S(2)}) async-start(), calls=%async_computation.4 | async-start | bytes 19464192 | tf_op jit(solution)/shard_map/all_gather | solution.py:739
  435.4 37.8 %collective-permute-start.3 = (bf16[1024,6144]{1,0:T(8,128)(2,1)}, bf16[1024,6144]{1,0:T(8,128)(2,1)}, u32[]{:S(2)}, u32[]{:S(2)}) collective-permute-start(bf16[1024,6144]{1,0:T(8,128)(2,1)} %get-tuple-element.61.a0), channel_id=1, source_target_pairs={{0,1},{1,0},{2,3},{3,2},{4,5},{5,4},{6,7},{7,6},{8,9},{9,8},{10,11... | collective-permute-start | bytes 37748744 | tf_op jit(solution)/shard_map/ppermute | solution.py:158
  437.5 272.9 %all-gather.13.cloned.1.call-start = ((), (), s32[]{:S(2)}) async-start(), calls=%async_computation.5 | async-start | bytes 13271040 | tf_op jit(solution)/shard_map/all_gather | solution.py:744
  467.6 5.7 collective-permute-start.4
  539.9 48.2 %collective-permute-start.6 = (bf16[1024,6144]{1,0:T(8,128)(2,1)}, bf16[1024,6144]{1,0:T(8,128)(2,1)}, u32[]{:S(2)}, u32[]{:S(2)}) collective-permute-start(bf16[1024,6144]{1,0:T(8,128)(2,1)} %multiply_convert_fusion.b0), channel_id=1, source_target_pairs={{0,1},{1,0},{2,3},{3,2},{4,5},{5,4},{6,7},{7,6},{8,9},{9,8},{10,11... | collective-permute-start | bytes 37748744 | tf_op jit(solution)/shard_map/ppermute | solution.py:158
  540.3 47.7 %collective-permute-start.5 = (bf16[1024,1536]{1,0:T(8,128)(2,1)}, bf16[1024,1536]{1,0:T(8,128)(2,1)}, u32[]{:S(2)}, u32[]{:S(2)}) collective-permute-start(bf16[1024,1536]{1,0:T(8,128)(2,1)} %copy-done.6), channel_id=1, source_target_pairs={{0,1},{1,0},{2,3},{3,2},{4,5},{5,4},{6,7},{7,6},{8,9},{9,8},{10,11... | collective-permute-start | bytes 9437192 | tf_op jit(solution)/shard_map/ppermute | solution.py:158
  540.4 84.8 %collective-permute-start.7 = (bf16[1024,1536]{1,0:T(8,128)(2,1)}, bf16[1024,1536]{1,0:T(8,128)(2,1)}, u32[]{:S(2)}, u32[]{:S(2)}) collective-permute-start(bf16[1024,1536]{1,0:T(8,128)(2,1)} %get-tuple-element.66.a0.refs_7_), channel_id=1, source_target_pairs={{0,1},{1,0},{2,3},{3,2},{4,5},{5,4},{6,7},{7,6},{8,9},{9,8},{10,11... | collective-permute-start | bytes 9437192 | tf_op jit(solution)/shard_map/ppermute | solution.py:158
  586.0 39.3 %collective-permute-start.8 = (bf16[1024,1536]{1,0:T(8,128)(2,1)}, bf16[1024,1536]{1,0:T(8,128)(2,1)}, u32[]{:S(2)}, u32[]{:S(2)}) collective-permute-start(bf16[1024,1536]{1,0:T(8,128)(2,1)} %multiply_convert_fusion.2.b0), channel_id=1, source_target_pairs={{0,1},{1,0},{2,3},{3,2},{4,5},{5,4},{6,7},{7,6},{8,9},{9,8},{10,11... | collective-permute-start | bytes 9437192 | tf_op jit(solution)/shard_map/ppermute | solution.py:158
  641.1 421.2 %reduce-scatter.5.cloned.1.call-start = ((), (), s32[]{:S(2)}) async-start(), calls=%async_computation.8 | async-start | bytes 5898240 | tf_op jit(solution)/shard_map/reduce_scatter | solution.py:764
  751.1 367.5 %all-gather.15.cloned.1.call-start = ((), (), s32[]{:S(2)}) async-start(), calls=%async_computation.6 | async-start | bytes 22118400 | tf_op jit(solution)/shard_map/all_gather | solution.py:744
  755.7 245.8 %copy-start.21 = (bf16[160,1536]{1,0:T(8,128)(2,1)S(1)}, bf16[160,1536]{1,0:T(8,128)(2,1)}, u32[]{:S(2)}) copy-start(bf16[160,1536]{1,0:T(8,128)(2,1)} %copy-done.20) | copy-start | bytes 1474564
  1004.8 142.7 %all-gather.17.cloned.1.call-start = ((), (), s32[]{:S(2)}) async-start(), calls=%async_computation.9 | async-start | bytes 5308416 | tf_op jit(solution)/shard_map/all_gather | solution.py:794
  1005.3 90.4 %collective-permute-start.9 = (bf16[1024,1536]{1,0:T(8,128)(2,1)}, bf16[1024,1536]{1,0:T(8,128)(2,1)}, u32[]{:S(2)}, u32[]{:S(2)}) collective-permute-start(bf16[1024,1536]{1,0:T(8,128)(2,1)} %fusion.16.a0), channel_id=1, source_target_pairs={{0,1},{1,0},{2,3},{3,2},{4,5},{5,4},{6,7},{7,6},{8,9},{9,8},{10,11... | collective-permute-start | bytes 9437192 | tf_op jit(solution)/shard_map/ppermute | solution.py:158
  1024.5 71.2 %collective-permute-start.10 = (bf16[1024,4608]{1,0:T(8,128)(2,1)}, bf16[1024,4608]{1,0:T(8,128)(2,1)}, u32[]{:S(2)}, u32[]{:S(2)}) collective-permute-start(bf16[1024,4608]{1,0:T(8,128)(2,1)} %get-tuple-element.75.b0), channel_id=1, source_target_pairs={{0,1},{1,0},{2,3},{3,2},{4,5},{5,4},{6,7},{7,6},{8,9},{9,8},{10,11... | collective-permute-start | bytes 28311560 | tf_op jit(solution)/shard_map/ppermute | solution.py:158
  1066.9 233.6 %reduce-scatter.3.cloned.1.call-start = ((), (), s32[]{:S(2)}) async-start(), calls=%async_computation.7 | async-start | bytes 2949120 | tf_op jit(solution)/shard_map/reduce_scatter | solution.py:764
  (121 other events, 1453.3 us)
Sparse Core Ops, SparseCore 0:
  152.3 62.9 all-gather.6
  387.6 122.8 all-gather.8
  513.9 122.8 all-gather.10
  641.2 69.1 all-gather.12
  751.2 84.8 reduce-scatter.4
  1004.9 101.1 all-gather.14
  1108.6 38.9 all-gather.16
  1149.8 45.2 reduce-scatter.2
